TPU v7x, 256 devices: a whole 4x4x8 slice. The times are simulated.
256 devices in a mesh: bucket: 128 (over y, z, x), rep: 2 (over core).
Axes of the slice: x: 4, y: 4, z: 8, core: 2. Of those that a mesh axis runs over, the one named last changes fastest.
Arguments:
- entity_table: bfloat16 [131072, 512], P('bucket'), may hold values from -1.75 to 1.75
- relations: bfloat16 [16, 8, 64, 64], replicated, may hold values from -0.75 to 0.75
- send_rows: int32 [128, 2, 2, 256], P('bucket', 'rep'), may hold values from 0 to 1023, as said below
- send_count: int32 [128, 2, 2, 128], P('bucket', 'rep'), may hold values from 1 to 2, as said below
- heads: int32 [128, 2, 2, 1, 512], P('bucket', 'rep'), may hold values from 0 to 255, as said below
- tails: int32 [128, 2, 2, 1, 512], P('bucket', 'rep'), may hold values from 0 to 255, as said below
- negatives: int32 [128, 2, 2, 1, 1000], P('bucket', 'rep'), may hold values from 0 to 255, as said below
- span_rel: int32 [128, 2, 2, 1], P('bucket', 'rep'), may hold values from 0 to 15
Outputs:
- entity_grad: float32 [131072, 512], P('bucket')
- relation_grad: float32 [16, 8, 64, 64], replicated
Inputs may be any that keep to these rules, and one draw needn't show every extreme that they name: send_count[s, r, k, d] rows go from device (s, r) to bucket index d for edge bucket k; for every r and k one destination, drawn from the seed, receives exactly 2 rows from every source. The first entries of send_rows[s, r, k] list the rows for destination 0, then for destination 1 and so on, send_count[s, r, k, d] of them each; later entries are unused. `heads`: a slot s * 2 + j named on device (d, r) for bucket k always has j < send_count[s, r, k, d]. `tails`: a slot s * 2 + j named on device (d, r) for bucket k always has j < send_count[s, r, k, d]. `negatives`: a slot s * 2 + j named on device (d, r) for bucket k always has j < send_count[s, r, k, d].
All inputs are finite; a program needn't handle non-finite values.
Results may differ from a plain program's by a relative error of at most 0.009.
Values may be sent and summed in bfloat16 or wider, within the bound.
No kernel may reach another device: no remote copies, remote signals or barrier semaphores. Data moves between devices by JAX's collectives and lax.ppermute only.
A program may use at most 64 MiB of HBM per device.

v0:
```python
import jax
import jax.numpy as jnp
from jax import lax
from jax.sharding import PartitionSpec as P


def prepare(entity_table, send_rows, send_count, bucket, capacity):
    counts_k = send_count[0, 0, bucket]
    starts = jnp.cumsum(counts_k) - counts_k
    column = jnp.arange(capacity, dtype=jnp.int32)
    limit = send_rows.shape[3] - 1
    flat_pos = jnp.clip(starts[:, None] + column[None, :], 0, limit)
    row_ids = send_rows[0, 0, bucket][flat_pos]
    is_valid = column[None, :] < counts_k[:, None]
    out_rows = jnp.where(
        is_valid[:, :, None], entity_table[row_ids], jnp.zeros((), entity_table.dtype)
    )
    return (out_rows, row_ids, is_valid)


def span_grads(fetched, rel_mat, head_ids, tail_ids, neg_ids):
    edge_count = head_ids.shape[0]
    neg_count = neg_ids.shape[0]
    blocks = rel_mat.shape[0]
    block_size = rel_mat.shape[1]
    head_rows = fetched[head_ids]
    tail_rows = fetched[tail_ids]
    neg_rows = fetched[neg_ids]
    head_blocks = head_rows.reshape(edge_count, blocks, block_size)
    rotated = (
        jnp.einsum("ebi,bio->ebo", head_blocks, rel_mat, preferred_element_type=jnp.float32)
        .reshape(edge_count, -1)
        .astype(jnp.bfloat16)
    )
    positive = jnp.sum(rotated.astype(jnp.float32) * tail_rows.astype(jnp.float32), axis=1)
    negative = lax.dot_general(
        rotated, neg_rows, (((1,), (1,)), ((), ())), preferred_element_type=jnp.float32
    )
    pos_grad = -jax.nn.sigmoid(-positive)
    neg_weight = (jax.nn.sigmoid(negative) / neg_count).astype(jnp.bfloat16)
    grad_tail = pos_grad[:, None] * rotated.astype(jnp.float32)
    grad_negative = lax.dot_general(
        neg_weight, rotated, (((0,), (0,)), ((), ())), preferred_element_type=jnp.float32
    )
    grad_rotated = (
        pos_grad[:, None] * tail_rows.astype(jnp.float32)
        + jnp.dot(neg_weight, neg_rows, preferred_element_type=jnp.float32)
    ).astype(jnp.bfloat16)
    grad_blocks = grad_rotated.reshape(edge_count, blocks, block_size)
    grad_head = jnp.einsum(
        "ebo,bio->ebi", grad_blocks, rel_mat, preferred_element_type=jnp.float32
    ).reshape(edge_count, -1)
    grad_rel = jnp.einsum(
        "ebi,ebo->bio", head_blocks, grad_blocks, preferred_element_type=jnp.float32
    )
    return (grad_head, grad_tail, grad_negative, grad_rel)


def body(entity_table, relations, send_rows, send_count, heads, tails, negatives, span_rel):
    bucket_count = lax.axis_size("bucket")
    slot_total = send_rows.shape[3]
    capacity = slot_total // bucket_count
    edge_buckets = send_rows.shape[2]
    feat_dim = entity_table.shape[1]
    prepared = [
        prepare(entity_table, send_rows, send_count, bucket, capacity)
        for bucket in range(edge_buckets)
    ]
    fetched = []
    for bucket in range(edge_buckets):
        received = lax.all_to_all(
            prepared[bucket][0], "bucket", split_axis=0, concat_axis=0, tiled=True
        )
        fetched.append(received.reshape(slot_total, feat_dim))
    rel_grad = jnp.zeros(relations.shape, jnp.float32)
    slot_grads = []
    for bucket in range(edge_buckets):
        slot_grad = jnp.zeros((slot_total, feat_dim), jnp.float32)
        rel_id = span_rel[0, 0, bucket, 0]
        head_ids = heads[0, 0, bucket, 0]
        tail_ids = tails[0, 0, bucket, 0]
        neg_ids = negatives[0, 0, bucket, 0]
        grad_head, grad_tail, grad_negative, grad_rel = span_grads(
            fetched[bucket], relations[rel_id], head_ids, tail_ids, neg_ids
        )
        slot_grad = slot_grad.at[head_ids].add(grad_head)
        slot_grad = slot_grad.at[tail_ids].add(grad_tail)
        slot_grad = slot_grad.at[neg_ids].add(grad_negative)
        rel_grad = rel_grad.at[rel_id].add(grad_rel)
        slot_grads.append(slot_grad.astype(jnp.bfloat16).reshape(bucket_count, capacity, feat_dim))
    returned = []
    for bucket in range(edge_buckets):
        returned.append(
            lax.all_to_all(slot_grads[bucket], "bucket", split_axis=0, concat_axis=0, tiled=True)
        )
    owned = jnp.zeros((entity_table.shape[0], feat_dim), jnp.float32)
    for bucket in range(edge_buckets):
        row_ids = prepared[bucket][1]
        is_valid = prepared[bucket][2]
        widened = returned[bucket].astype(jnp.float32)
        owned = owned.at[row_ids].add(
            jnp.where(is_valid[:, :, None], widened, jnp.zeros((), jnp.float32))
        )
    owned = lax.psum(owned, "rep")
    rel_grad = lax.psum(rel_grad, ("bucket", "rep"))
    return (owned, rel_grad)


def solution(mesh):
    return jax.shard_map(
        body,
        mesh=mesh,
        in_specs=(
            P("bucket", None),
            P(),
            P("bucket", "rep", None, None),
            P("bucket", "rep", None, None),
            P("bucket", "rep", None, None, None),
            P("bucket", "rep", None, None, None),
            P("bucket", "rep", None, None, None),
            P("bucket", "rep", None, None),
        ),
        out_specs=(P("bucket", None), P()),
        check_vma=False,
    )
```

profile of v0, /device:TPU:1, one launch (start us, length us, event | category | flops | bytes accessed | tf_op | source)
XLA Modules:
  0.0 474.1 jit_solution(4170135164459107193)
XLA Ops:
  17.0 16.9 %all-to-all-start = ((bf16[128,2,512]{2,1,0:T(2,128)(2,1)}), bf16[128,2,512]{2,1,0:T(2,128)(2,1)}, u32[]{:S(2)}, u32[]{:S(2)}) async-start(bf16[128,2,512]{2,1,0:T(2,128)(2,1)} %broadcast_select_fusion.1), calls=%async_computation | async-start | bytes 524288 | tf_op jit(solution)/shard_map/all_to_all | solution.py:71
  46.0 13.6 %all-to-all-start.2 = ((bf16[128,2,512]{2,1,0:T(2,128)(2,1)}), bf16[128,2,512]{2,1,0:T(2,128)(2,1)}, u32[]{:S(2)}, u32[]{:S(2)}) async-start(bf16[128,2,512]{2,1,0:T(2,128)(2,1)} %broadcast_select_fusion), calls=%async_computation.2 | async-start | bytes 524288 | tf_op jit(solution)/shard_map/all_to_all | solution.py:71
  67.4 5.1 %gather_fusion.4 = bf16[1000,512]{1,0:T(8,128)(2,1)} fusion(bf16[256,512]{1,0:T(8,128)(2,1)S(1)} %reshape.523, s32[1024]{0:T(1024)S(1)} %pad_clamp_fusion.5), kind=kCustom, calls=%fused_computation.4 | custom fusion | bytes 2052000 | tf_op jit(solution)/shard_map/gather | solution.py:28
  87.5 5.1 %gather_fusion.9 = bf16[1000,512]{1,0:T(8,128)(2,1)} fusion(bf16[256,512]{1,0:T(8,128)(2,1)S(1)} %reshape.531, s32[1024]{0:T(1024)S(1)} %pad_clamp_fusion), kind=kCustom, calls=%fused_computation.9 | custom fusion | bytes 2052000 | tf_op jit(solution)/shard_map/gather | solution.py:28
  98.6 2.7 copy.28
  101.2 2.5 copy.35
  105.0 2.5 copy.27
  107.6 4.6 scatter_custom_fusion
  112.2 4.5 scatter_fusion
  116.7 7.5 %scatter_fusion.1 = f32[256,512]{1,0:T(8,128)S(1)} fusion(f32[256,512]{1,0:T(8,128)S(1)} %scatter_fusion, s32[1000]{0:T(1024)S(1)} %bitcast.137, f32[1000,512]{1,0:T(8,128)} %fusion.31), kind=kCustom, calls=%fused_computation.12 | custom fusion | flops 512000 | bytes 6148000 | tf_op jit(solution)/shard_map/scatter-add | solution.py:88
  125.0 13.4 %all-to-all-start.1 = ((bf16[128,2,512]{2,1,0:T(2,128)(2,1)}), bf16[128,2,512]{2,1,0:T(2,128)(2,1)S(1)}, u32[]{:S(2)}, u32[]{:S(2)}) async-start(bf16[128,2,512]{2,1,0:T(2,128)(2,1)} %reshape.527), calls=%async_computation.1 | async-start | bytes 524288 | tf_op jit(solution)/shard_map/all_to_all | solution.py:94
  143.2 4.8 %scatter_custom_fusion.4 = f32[256,512]{1,0:T(8,128)S(1)} fusion(s32[512]{0:T(512)S(1)} %bitcast.143, f32[512,512]{1,0:T(8,128)} %copy.34, f32[]{:T(128)} %constant.63.clone.1), kind=kCustom, calls=%fused_computation.43 | custom fusion | flops 262144 | bytes 524800 | tf_op jit(solution)/shard_map/scatter-add | solution.py:86
  148.1 2.5 broadcast_in_dim.37
  152.2 2.6 fusion.6
  154.8 4.5 scatter_fusion.2
  159.2 3.2 fusion.32
  162.5 7.5 %scatter_fusion.3 = f32[256,512]{1,0:T(8,128)S(1)} fusion(f32[256,512]{1,0:T(8,128)S(1)} %scatter_fusion.2, s32[1000]{0:T(1024)S(1)} %bitcast.135, f32[1000,512]{1,0:T(8,128)} %fusion.32), kind=kCustom, calls=%fused_computation.16 | custom fusion | flops 512000 | bytes 6148000 | tf_op jit(solution)/shard_map/scatter-add | solution.py:88
  170.8 13.8 %all-to-all-start.3 = ((bf16[128,2,512]{2,1,0:T(2,128)(2,1)}), bf16[128,2,512]{2,1,0:T(2,128)(2,1)}, u32[]{:S(2)}, u32[]{:S(2)}) async-start(bf16[128,2,512]{2,1,0:T(2,128)(2,1)} %reshape.535), calls=%async_computation.3 | async-start | bytes 524288 | tf_op jit(solution)/shard_map/all_to_all | solution.py:94
  186.3 10.7 %all-to-all-done.3 = bf16[128,2,512]{2,1,0:T(2,128)(2,1)} async-done(((bf16[128,2,512]{2,1,0:T(2,128)(2,1)}), bf16[128,2,512]{2,1,0:T(2,128)(2,1)}, u32[]{:S(2)}, u32[]{:S(2)}) %all-to-all-start.3) | async-done | bytes 262176 | tf_op jit(solution)/shard_map/all_to_all | solution.py:94
  198.6 4.0 scatter_custom_fusion.3
  202.6 4.9 %scatter_fusion.4 = f32[1024,512]{1,0:T(8,128)} fusion(f32[1024,512]{1,0:T(8,128)} %scatter_custom_fusion.3, s32[256]{0:T(256)S(1)} %reshape.678, f32[256,512]{1,0:T(8,128)S(1)} %reshape.680), kind=kCustom, calls=%fused_computation.17 | custom fusion | flops 131072 | bytes 1573888 | tf_op jit(solution)/shard_map/scatter-add | solution.py:101
  207.6 217.8 %all-reduce.5.cloned.1.call-done = f32[16,8,64,64]{3,2,1,0:T(8,128)} async-done(((f32[16,8,64,64]{3,2,1,0:T(8,128)}), f32[16,8,64,64]{3,2,1,0:T(8,128)}) %all-reduce.5.cloned.1.call-update) | async-done | bytes 2097168 | tf_op jit(solution)/shard_map/psum | solution.py:105
  425.4 36.4 %all-reduce.3.cloned.1.call-done = f32[1024,512]{1,0:T(8,128)} async-done(((f32[1024,512]{1,0:T(8,128)}), f32[1024,512]{1,0:T(8,128)}) %all-reduce.3.cloned.1.call-update) | async-done | bytes 2097168 | tf_op jit(solution)/shard_map/psum | solution.py:104
  461.8 3.2 copy.51
  (123 shorter events, 61.4 us)
Async XLA Ops:
  7.2 58.7 %copy-start = (bf16[16,8,64,64]{3,2,1,0:T(8,128)(2,1)S(1)}, bf16[16,8,64,64]{3,2,1,0:T(8,128)(2,1)}, u32[]{:S(2)}) copy-start(bf16[16,8,64,64]{3,2,1,0:T(8,128)(2,1)} %param.13) | copy-start | bytes 3145732
  10.7 2.3 copy-start.1
  12.8 21.1 %copy-start.18 = (s32[1,1,2,1]{2,3,1,0:T(1,128)S(1)}, s32[1,1,2,1]{2,3,1,0:T(1,128)}, u32[]{:S(2)}) copy-start(s32[1,1,2,1]{2,3,1,0:T(1,128)} %param.19) | copy-start | bytes 28
  12.8 24.2 %copy-start.16 = (s32[1,1,2,1,512]{4,3,2,1,0:T(1,128)S(1)}, s32[1,1,2,1,512]{4,3,2,1,0:T(1,128)}, u32[]{:S(2)}) copy-start(s32[1,1,2,1,512]{4,3,2,1,0:T(1,128)} %param.17) | copy-start | bytes 12292
  12.8 24.2 %copy-start.17 = (s32[1,1,2,1,512]{4,3,2,1,0:T(1,128)S(1)}, s32[1,1,2,1,512]{4,3,2,1,0:T(1,128)}, u32[]{:S(2)}) copy-start(s32[1,1,2,1,512]{4,3,2,1,0:T(1,128)} %param.16) | copy-start | bytes 12292
  12.9 24.3 %copy-start.15 = (s32[1,1,2,1,1000]{4,3,2,1,0:T(1,128)S(1)}, s32[1,1,2,1,1000]{4,3,2,1,0:T(1,128)}, u32[]{:S(2)}) copy-start(s32[1,1,2,1,1000]{4,3,2,1,0:T(1,128)} %param.18) | copy-start | bytes 24004
  17.0 29.0 %all-to-all-start = ((bf16[128,2,512]{2,1,0:T(2,128)(2,1)}), bf16[128,2,512]{2,1,0:T(2,128)(2,1)}, u32[]{:S(2)}, u32[]{:S(2)}) async-start(bf16[128,2,512]{2,1,0:T(2,128)(2,1)} %broadcast_select_fusion.1), calls=%async_computation | async-start | bytes 524288 | tf_op jit(solution)/shard_map/all_to_all | solution.py:71
  39.3 4.5 copy-start.19
  46.0 33.6 %all-to-all-start.2 = ((bf16[128,2,512]{2,1,0:T(2,128)(2,1)}), bf16[128,2,512]{2,1,0:T(2,128)(2,1)}, u32[]{:S(2)}, u32[]{:S(2)}) async-start(bf16[128,2,512]{2,1,0:T(2,128)(2,1)} %broadcast_select_fusion), calls=%async_computation.2 | async-start | bytes 524288 | tf_op jit(solution)/shard_map/all_to_all | solution.py:71
  65.8 6.7 %copy-start.2 = (bf16[512,512]{0,1:T(8,128)(2,1)}, bf16[512,512]{0,1:T(8,128)(2,1)S(1)}, u32[]{:S(2)}) copy-start(bf16[512,512]{0,1:T(8,128)(2,1)S(1)} %copy.24) | copy-start | bytes 1572868
  72.5 2.3 copy-start.14
  85.8 6.7 %copy-start.4 = (bf16[512,512]{0,1:T(8,128)(2,1)}, bf16[512,512]{0,1:T(8,128)(2,1)S(1)}, u32[]{:S(2)}) copy-start(bf16[512,512]{0,1:T(8,128)(2,1)S(1)} %copy.31) | copy-start | bytes 1572868
  93.7 3.3 copy-start.7
  93.7 3.3 copy-start.13
  98.6 5.2 %copy-start.9 = (bf16[512,512]{0,1:T(8,128)(2,1)S(1)}, bf16[512,512]{0,1:T(8,128)(2,1)}, u32[]{:S(2)}) copy-start(bf16[512,512]{0,1:T(8,128)(2,1)} %fusion) | copy-start | bytes 1572868
  125.0 45.8 %all-to-all-start.1 = ((bf16[128,2,512]{2,1,0:T(2,128)(2,1)}), bf16[128,2,512]{2,1,0:T(2,128)(2,1)S(1)}, u32[]{:S(2)}, u32[]{:S(2)}) async-start(bf16[128,2,512]{2,1,0:T(2,128)(2,1)} %reshape.527), calls=%async_computation.1 | async-start | bytes 524288 | tf_op jit(solution)/shard_map/all_to_all | solution.py:94
  138.4 287.0 %all-reduce.5.cloned.1.call-start = ((), (), s32[]{:S(2)}) async-start(), calls=%async_computation.5 | async-start | bytes 8388608 | tf_op jit(solution)/shard_map/psum | solution.py:105
  148.0 2.6 copy-start.3
  148.0 2.6 copy-start.10
  148.0 4.1 copy-start.5
  148.0 4.1 copy-start.11
  170.8 26.1 %all-to-all-start.3 = ((bf16[128,2,512]{2,1,0:T(2,128)(2,1)}), bf16[128,2,512]{2,1,0:T(2,128)(2,1)}, u32[]{:S(2)}, u32[]{:S(2)}) async-start(bf16[128,2,512]{2,1,0:T(2,128)(2,1)} %reshape.535), calls=%async_computation.3 | async-start | bytes 524288 | tf_op jit(solution)/shard_map/all_to_all | solution.py:94
  184.6 277.2 %all-reduce.3.cloned.1.call-start = ((), (), s32[]{:S(2)}) async-start(), calls=%async_computation.4 | async-start | bytes 4194304 | tf_op jit(solution)/shard_map/psum | solution.py:104
  461.8 3.2 copy-start.6
  (2 other events, 3.3 us)
Sparse Core Ops, SparseCore 0:
  154.9 270.4 all-reduce.4
  428.7 33.0 all-reduce.2
where the time goes:
time: 482 us; the launch traced here: 474 us
  waiting for transfers between devices  265 us (55%)
  starting transfers between devices  57.8 us (12%)
  local copies, waits for them, and re-layouts  56.9 us (12%)
  other arithmetic  51.7 us (11%)
  matrix products  23.9 us (5%)
  between operations  18.6 us (4%)
    psum x1, waiting for transfers between devices, body(): rel_grad = lax.psum(rel_grad, ('bucket', 'rep'))  218 us
    psum x1, waiting for transfers between devices, body(): owned = lax.psum(owned, 'rep')  36.4 us
    all_to_all x2, starting transfers between devices, body(): lax.all_to_all(prepared[bucket][0], 'bucket', split_axis=0, concat_axis=0...  30.4 us
    all_to_all x2, starting transfers between devices, body(): lax.all_to_all(slot_grads[bucket], 'bucket', split_axis=0, concat_axis=0,...  27.1 us
    scatter-add x2, other arithmetic, body(): slot_grad = slot_grad.at[neg_ids].add(grad_negative)  14.9 us
    all_to_all x2, waiting for transfers between devices, body(): lax.all_to_all(slot_grads[bucket], 'bucket', split_axis=0, concat_axis=0,...  10.7 us
    gather x2, local copies, waits for them, and re-layouts, span_grads(): neg_rows = fetched[neg_ids]  10.1 us
  transfers between devices with their start and end apart: 6, of which 4 were waited for; matrix products, arithmetic and copies ran while one was open for 15% of the time, Pallas kernels for 0%

commit v1 on v0

v1 whole, which is shorter than its diff:
```python
import functools

import jax
import jax.numpy as jnp
from jax import lax
from jax.experimental import pallas as pl
from jax.experimental.pallas import tpu as pltpu
from jax.sharding import PartitionSpec as P

F32 = jnp.float32
BF16 = jnp.bfloat16
VMEM = pl.BlockSpec(memory_space=pltpu.VMEM)


def iota(shape, dim):
    return lax.broadcasted_iota(jnp.int32, shape, dim)


def dot(a, b, ca=1, cb=0):
    return lax.dot_general(a, b, (((ca,), (cb,)), ((), ())), preferred_element_type=F32)


def onehot(mask):
    return jnp.where(mask, 1.0, 0.0).astype(BF16)


def unpack_matrix():
    g = iota((256, 256), 0)
    p = iota((256, 256), 1)
    return onehot(p == (g & 31) * 8 + (g >> 5))


def pack_matrix():
    p = iota((256, 256), 0)
    g = iota((256, 256), 1)
    return onehot(p == (g & 31) * 8 + (g >> 5))


def slot_row(ids):
    return ((ids >> 6) << 6) | ((ids & 1) << 5) | ((ids >> 1) & 31)


def pack_slots(read, write):
    matrix = pack_matrix()
    for b in range(4):
        rows = jnp.concatenate(
            [read(k, b)[:, h * 256 : h * 256 + 256] for h in range(2) for k in range(2)], axis=0
        )
        write(b, dot(matrix, rows).astype(BF16))


def unpack_slots(read, write):
    matrix = unpack_matrix()
    for b in range(4):
        rows = dot(matrix, read(b)).astype(BF16)
        for h in range(2):
            for k in range(2):
                start = h * 128 + k * 64
                write(k, b, h, rows[start : start + 64])


def send_kernel(rows_ref, count_ref, table_ref, packed_ref, ids_ref, slots):
    table = table_ref[...]
    row = iota((256, 128), 0)
    chip = (row >> 6) * 32 + (row & 31)
    other = iota((256, 128), 1)
    column = (iota((256, 1), 0) >> 5) & 1
    flat = iota((256, 256), 1)
    entity = iota((256, table.shape[0]), 1)
    ids_ref[...] = jnp.zeros_like(ids_ref)
    for k in range(2):
        counts = count_ref[k : k + 1, :].astype(F32)
        start = jnp.sum(jnp.where(other < chip, counts, 0.0), axis=1, keepdims=True)
        count = jnp.sum(jnp.where(other == chip, counts, 0.0), axis=1, keepdims=True)
        position = start.astype(jnp.int32) + column
        names = rows_ref[k : k + 1, :].astype(F32)
        ids = jnp.sum(jnp.where(flat == position, names, 0.0), axis=1, keepdims=True)
        ids = jnp.where(column < count.astype(jnp.int32), ids, -1.0)
        ids_ref[k : k + 1, :] = jnp.transpose(jnp.broadcast_to(ids, (256, 128)))[0:1, :]
        chosen = onehot(entity == ids.astype(jnp.int32))
        slots[k] = dot(chosen, table).astype(BF16)

    def write(b, rows):
        packed_ref[b * 256 : b * 256 + 256, :] = rows

    pack_slots(lambda k, b: slots[k, b * 64 : b * 64 + 64, :], write)


def step_kernel(
    rel_ref, packed_ref, first_ref, second_ref, heads_ref, tails_ref, neg_ref, out_ref, slots, diag, grads, partial
):
    def write(k, b, h, rows):
        slots[k, b * 64 : b * 64 + 64, h * 256 : h * 256 + 256] = rows

    unpack_slots(lambda b: packed_ref[b * 256 : b * 256 + 256, :], write)
    neg_count = neg_ref.shape[1]
    lane_block = iota((64, 256), 1) >> 6
    for k in range(2):
        relation = (first_ref, second_ref)[k]
        for c in range(2):
            for j in range(4):
                place = onehot(iota((64, 256), 1) == iota((64, 256), 0) + 64 * j)
                diag[k, c, 64 * j : 64 * j + 64, :] = dot(relation[0, 4 * c + j], place).astype(BF16)
        rows = slots[k]
        rotated = jnp.concatenate(
            [dot(rows[:, c * 256 : c * 256 + 256], diag[k, c]) for c in range(2)], axis=1
        ).astype(BF16)
        slot = iota((256, 512), 0)
        at_head = onehot(slot == slot_row(heads_ref[k : k + 1, :]))
        at_tail = onehot(slot == slot_row(tails_ref[k : k + 1, :]))
        edges = dot(at_head, at_tail, 1, 1)
        head_edges = jnp.sum(edges, axis=1, keepdims=True)
        at_neg = onehot(iota((256, neg_count), 0) == slot_row(neg_ref[k : k + 1, :]))
        times = dot(jnp.ones((8, neg_count), BF16), at_neg, 1, 1)[0:1, :]
        score = dot(rotated, rows, 1, 1)
        small = jnp.exp(-jnp.abs(score))
        big_side = 1.0 / (1.0 + small)
        small_side = small * big_side
        sigmoid = jnp.where(score >= 0, big_side, small_side)
        sigmoid_neg = jnp.where(score >= 0, small_side, big_side)
        weight = ((head_edges * times) * sigmoid / neg_count - edges * sigmoid_neg).astype(BF16)
        grad_rotated = dot(weight, rows).astype(BF16)
        grad_other = dot(weight, rotated, 0, 0)
        for c in range(2):
            lanes = slice(c * 256, c * 256 + 256)
            grad_head = dot(grad_rotated[:, lanes], diag[k, c], 1, 1)
            grads[k, :, lanes] = (grad_head + grad_other[:, lanes]).astype(BF16)
            outer = dot(rows[:, lanes], grad_rotated[:, lanes], 0, 0)
            total = jnp.zeros((64, 256), F32)
            for j in range(4):
                total = jnp.where(lane_block == j, outer[64 * j : 64 * j + 64, :], total)
            partial[k, :, lanes] = total.astype(BF16)

    def write_packed(b, rows):
        out_ref[b * 256 : b * 256 + 256, 0:256] = rows

    pack_slots(lambda k, b: grads[k, b * 64 : b * 64 + 64, :], write_packed)
    p = iota((256, 128), 0)
    g = iota((256, 128), 1)
    piece = p & 3
    source = ((p >> 2) & 1) * 64 + (((p >> 3) & 1) * 2 + piece) * 16 + (p >> 4)
    spread = onehot((g == source) & (piece < 2))
    named = jnp.where(((p >> 2) & 1) == 0, rel_ref[0], rel_ref[1]).astype(F32)
    for b in range(4):
        rows = jnp.concatenate(
            [partial[k, b * 16 : b * 16 + 16, q * 128 : q * 128 + 128] for k in range(2) for q in range(4)], axis=0
        )
        out_ref[b * 256 : b * 256 + 256, 256:384] = jnp.where(piece == 2, named, dot(spread, rows)).astype(BF16)


def relation_kernel(rep_ref, own_ref, peer_ref, out_ref):
    matrix = unpack_matrix()
    lane = iota((128, 128), 1)
    totals = [jnp.zeros((128, 128), F32) for q in range(2)]
    for ref in (own_ref, peer_ref):
        blocks = [dot(matrix, ref[b * 256 : b * 256 + 256, :]) for b in range(4)]

        def piece(index):
            return jnp.concatenate([rows[index * 32 : index * 32 + 32] for rows in blocks], axis=0)

        for k in range(2):
            chosen = onehot(lane == piece(4 * k + 2).astype(jnp.int32))
            for q in range(2):
                totals[q] = totals[q] + dot(chosen, piece(4 * k + q).astype(BF16), 0, 0)
    mine = jnp.where(rep_ref[0] == 0, totals[0], totals[1])[0:16].astype(BF16)
    for d in range(128):
        out_ref[d * 16 : d * 16 + 16, :] = mine


def scatter_kernel(own_ref, peer_ref, own_ids, peer_ids, out_ref, rows_ref):
    @pl.when(pl.program_id(0) == 0)
    def _():
        for r, ref in enumerate((own_ref, peer_ref)):

            def write(k, b, h, rows):
                start = (r * 2 + k) * 256 + b * 64
                rows_ref[start : start + 64, h * 256 : h * 256 + 256] = rows

            unpack_slots(lambda b: ref[b * 256 : b * 256 + 256, :], write)

    base = pl.program_id(0) * 256
    entity = iota((256, 256), 0) + base
    total = jnp.zeros(out_ref.shape, F32)
    for r, ref in enumerate((own_ids, peer_ids)):
        for k in range(2):
            start = (r * 2 + k) * 256
            hit = onehot(entity == ref[k : k + 1, :].astype(jnp.int32))
            total = total + dot(hit, rows_ref[start : start + 256, :])
    out_ref[...] = total


def assemble_kernel(rep_ref, own_ref, peer_ref, out_ref):
    g = iota((256, 256), 0)
    p = iota((256, 256), 1)
    matrix = onehot(p == ((g & 7) * 2 + ((g >> 3) & 1)) * 16 + (g >> 4))
    first = rep_ref[0] == 0
    for d in range(8):
        own = dot(matrix, own_ref[d * 256 : d * 256 + 256, :])
        peer = dot(matrix, peer_ref[d * 256 : d * 256 + 256, :])
        for q in range(2):
            rows = jnp.where(first, own, peer) if q == 0 else jnp.where(first, peer, own)
            rows = rows.reshape(16, 2, 8, 128)
            for half in range(2):
                block = half * 4 + q * 2
                out_ref[:, block, d * 8 : d * 8 + 8, :] = rows[:, half, :, 0:64]
                out_ref[:, block + 1, d * 8 : d * 8 + 8, :] = rows[:, half, :, 64:128]


def body(entity_table, relations, send_rows, send_count, heads, tails, negatives, span_rel):
    entities, width = entity_table.shape
    chips = send_count.shape[3]
    rep = lax.axis_index("rep").astype(jnp.int32).reshape(1)
    swap = [(0, 1), (1, 0)]

    packed, ids = pl.pallas_call(
        send_kernel,
        out_shape=(jax.ShapeDtypeStruct((chips * 8, 256), BF16), jax.ShapeDtypeStruct((8, 256), F32)),
        in_specs=[VMEM] * 3,
        out_specs=(VMEM, VMEM),
        scratch_shapes=[pltpu.VMEM((2, 256, width), BF16)],
        name="send_rows",
    )(send_rows[0, 0], send_count[0, 0], entity_table)
    peer_ids = lax.ppermute(ids, "rep", swap)

    received = lax.all_to_all(packed.reshape(chips, 8, 256), "bucket", 0, 0, tiled=True)

    rel_ids = span_rel.reshape(2)
    whole = lambda shape: pl.BlockSpec(shape, lambda i, rel: (0,) * len(shape))
    relation_spec = lambda k: pl.BlockSpec((1, 8, 64, 64), lambda i, rel: (rel[k], 0, 0, 0))
    returned = pl.pallas_call(
        step_kernel,
        out_shape=jax.ShapeDtypeStruct((chips * 8, 384), BF16),
        grid_spec=pltpu.PrefetchScalarGridSpec(
            num_scalar_prefetch=1,
            grid=(1,),
            in_specs=[
                whole((chips * 8, 256)),
                relation_spec(0),
                relation_spec(1),
                whole((2, heads.shape[4])),
                whole((2, tails.shape[4])),
                whole((2, negatives.shape[4])),
            ],
            out_specs=whole((chips * 8, 384)),
            scratch_shapes=[
                pltpu.VMEM((2, 256, width), BF16),
                pltpu.VMEM((2, 2, 256, 256), BF16),
                pltpu.VMEM((2, 256, width), BF16),
                pltpu.VMEM((2, 64, width), BF16),
            ],
        ),
        name="train_step",
    )(
        rel_ids,
        received.reshape(chips * 8, 256),
        relations,
        relations,
        heads.reshape(2, -1),
        tails.reshape(2, -1),
        negatives.reshape(2, -1),
    )

    own = lax.all_to_all(returned.reshape(chips, 8, 384), "bucket", 0, 0, tiled=True).reshape(chips * 8, 384)
    peer = lax.ppermute(own, "rep", swap)

    slice_spec = pl.BlockSpec((chips * 8, 128), lambda i, rep: (0, 2))
    slices = pl.pallas_call(
        relation_kernel,
        out_shape=jax.ShapeDtypeStruct((chips * 16, 128), BF16),
        grid_spec=pltpu.PrefetchScalarGridSpec(
            num_scalar_prefetch=1,
            grid=(1,),
            in_specs=[slice_spec, slice_spec],
            out_specs=pl.BlockSpec((chips * 16, 128), lambda i, rep: (0, 0)),
        ),
        name="sum_relations",
    )(rep, own, peer)
    gathered = lax.all_to_all(slices.reshape(chips, 16, 128), "bucket", 0, 0, tiled=True).reshape(chips * 16, 128)

    chunk = 256
    rows_spec = pl.BlockSpec((chips * 8, 256), lambda i: (0, 0))
    ids_spec = pl.BlockSpec((8, 256), lambda i: (0, 0))
    entity_grad = pl.pallas_call(
        scatter_kernel,
        out_shape=jax.ShapeDtypeStruct((entities, width), F32),
        grid=(entities // chunk,),
        in_specs=[rows_spec, rows_spec, ids_spec, ids_spec],
        out_specs=pl.BlockSpec((chunk, width), lambda i: (i, 0)),
        scratch_shapes=[pltpu.VMEM((1024, width), BF16)],
        name="scatter_rows",
    )(own, peer, ids, peer_ids)

    peer_gathered = lax.ppermute(gathered, "rep", swap)
    full = lambda i, rep: (0, 0)
    relation_grad = pl.pallas_call(
        assemble_kernel,
        out_shape=jax.ShapeDtypeStruct(relations.shape, F32),
        grid_spec=pltpu.PrefetchScalarGridSpec(
            num_scalar_prefetch=1,
            grid=(1,),
            in_specs=[pl.BlockSpec((chips * 16, 128), full)] * 2,
            out_specs=pl.BlockSpec(relations.shape, lambda i, rep: (0, 0, 0, 0)),
        ),
        compiler_params=pltpu.CompilerParams(vmem_limit_bytes=48 << 20),
        name="assemble_relations",
    )(rep, gathered, peer_gathered)
    return entity_grad, relation_grad


def solution(mesh):
    return jax.shard_map(
        body,
        mesh=mesh,
        in_specs=(
            P("bucket", None),
            P(),
            P("bucket", "rep", None, None),
            P("bucket", "rep", None, None),
            P("bucket", "rep", None, None, None),
            P("bucket", "rep", None, None, None),
            P("bucket", "rep", None, None, None),
            P("bucket", "rep", None, None),
        ),
        out_specs=(P("bucket", None), P()),
        check_vma=False,
    )
```

time: 482 us -> 120 us (0.25); the launches traced: 474 us -> 119 us
  waiting for transfers between devices: 265 us -> 19.1 us
  local copies, waits for them, and re-layouts: 56.9 us -> 3.51 us
  blocking collectives: 0 us -> 52.8 us
  other arithmetic: 51.7 us -> 0 us
  starting transfers between devices: 57.8 us -> 24.4 us
  matrix products: 23.9 us -> 0 us
  Pallas kernels: 0 us -> 18.6 us
  between operations: 18.6 us -> 0.69 us
    psum x2 -> x0, waiting for transfers between devices: 254 us -> none  [the longest x1 218 us: body(): rel_grad = lax.psum(rel_grad, ('bucket', 'rep'))]
    all_to_all x0 -> x2, blocking collectives: none -> 52.8 us  [the longest x1 28.7 us: body(): lax.all_to_all(returned.reshape(chips, 8, 384), 'bucket', 0, 0, tiled=True)]
    scatter-add x8 -> x0, other arithmetic: 42.2 us -> none  [the longest x2 14.9 us: body(): slot_grad = slot_grad.at[neg_ids].add(grad_negative)]
    all_to_all x4 -> x1, starting transfers between devices: 57.6 us -> 16.3 us  [body(): lax.all_to_all(packed.reshape(chips, 8, 256), 'bucket', 0, 0, tiled=True)]
    gather x18 -> x0, local copies, waits for them, and re-layouts: 29.5 us -> none  [the longest x2 10.1 us: span_grads(): neg_rows = fetched[neg_ids]]
    dot_general x12 -> x0, matrix products: 23.9 us -> none  [the longest x2 5.27 us: span_grads(): lax.dot_general(neg_weight, rotated, (((0,), (0,)), ((), ())), preferred_...]
    pallas_call x0 -> x5, Pallas kernels: none -> 18.6 us  [the longest x1 5.34 us: body(): pl.pallas_call(step_kernel, out_shape=jax.ShapeDtypeStruct((chips * 8, 38...]
    reshape x6 -> x0, local copies, waits for them, and re-layouts: 8.8 us -> none  [the longest x2 5.08 us: span_grads(): grad_head = jnp.einsum('ebo,bio->ebi', grad_blocks, rel_mat, preferred_el...]
  transfers between devices with their start and end apart: 6 -> 4, of which waited for: 4 -> 3; matrix products, arithmetic and copies ran while one was open for 15% -> 1% of each run, Pallas kernels for 0% -> 4%
where the time goes in v1:
time: 120 us; the launch traced here: 119 us
  blocking collectives  52.8 us (44%)
  starting transfers between devices  24.4 us (20%)
  waiting for transfers between devices  19.1 us (16%)
  Pallas kernels  18.6 us (16%)
  local copies, waits for them, and re-layouts  3.51 us (3%)
    all_to_all x1, blocking collectives, body(): lax.all_to_all(returned.reshape(chips, 8, 384), 'bucket', 0, 0, tiled=True)  28.7 us
    all_to_all x1, blocking collectives, body(): lax.all_to_all(slices.reshape(chips, 16, 128), 'bucket', 0, 0, tiled=True)  24 us
    all_to_all x1, starting transfers between devices, body(): lax.all_to_all(packed.reshape(chips, 8, 256), 'bucket', 0, 0, tiled=True)  16.3 us
    all_to_all x1, waiting for transfers between devices, body(): lax.all_to_all(packed.reshape(chips, 8, 256), 'bucket', 0, 0, tiled=True)  15.7 us
    pallas_call x1, Pallas kernels, body(): pl.pallas_call(step_kernel, out_shape=jax.ShapeDtypeStruct((chips * 8, 38...  5.34 us
    ppermute x1, starting transfers between devices, body(): peer = lax.ppermute(own, 'rep', swap)  5.03 us
    pallas_call x1, Pallas kernels, body(): pl.pallas_call(scatter_kernel, out_shape=jax.ShapeDtypeStruct((entities,...  4.56 us
    unnamed x18, local copies, waits for them, and re-layouts  3.51 us
  transfers between devices with their start and end apart: 4, of which 3 were waited for; matrix products, arithmetic and copies ran while one was open for 1% of the time, Pallas kernels for 4%

profile of v1, /device:TPU:1, one launch (start us, length us, event | category | flops | bytes accessed | tf_op | source)
XLA Modules:
  0.0 119.1 jit_solution(505685888050126486)
XLA Ops:
  0.6 0.0 copy-start.5
  0.6 0.0 copy-start.6
  0.7 0.0 copy-start.7
  0.7 3.3 %send_rows.1 = (bf16[1024,256]{1,0:T(8,128)(2,1)}, f32[8,256]{1,0:T(8,128)}) custom-call(s32[2,256]{1,0:T(2,128)} %bitcast.27, s32[2,128]{1,0:T(2,128)} %bitcast.28, bf16[1024,512]{1,0:T(8,128)(2,1)} %table_ref.1), custom_call_target="tpu_custom_call" | custom-call | tf_op jit(solution)/shard_map/send_rows/pallas_call | solution.py:215
  4.0 16.3 %all-to-all-start = ((bf16[128,8,256]{2,1,0:T(8,128)(2,1)}), bf16[128,8,256]{2,1,0:T(8,128)(2,1)S(1)}, u32[]{:S(2)}, u32[]{:S(2)}) async-start(bf16[128,8,256]{2,1,0:T(8,128)(2,1)} %bitcast.25), calls=%async_computation | async-start | bytes 1048576 | tf_op jit(solution)/shard_map/all_to_all | solution.py:225
  20.3 0.6 copy.16
  20.9 0.6 copy_bitcast_fusion.1
  21.5 15.7 %all-to-all-done = bf16[128,8,256]{2,1,0:T(8,128)(2,1)S(1)} async-done(((bf16[128,8,256]{2,1,0:T(8,128)(2,1)}), bf16[128,8,256]{2,1,0:T(8,128)(2,1)S(1)}, u32[]{:S(2)}, u32[]{:S(2)}) %all-to-all-start) | async-done | bytes 524320 | tf_op jit(solution)/shard_map/all_to_all | solution.py:225
  37.2 0.8 copy-done.2
  38.0 5.3 %train_step.1 = bf16[1024,384]{1,0:T(8,128)(2,1)} custom-call(s32[2]{0:T(128)} %bitcast.29, bf16[1024,256]{1,0:T(8,128)(2,1)} %bitcast.24, bf16[16,8,64,64]{3,2,1,0:T(8,128)(2,1)} %second_ref.1, bf16[16,8,64,64]{3,2,1,0:T(8,128)(2,1)} %second_ref.1, s32[2,512]{1,0:T(2,128)} %get-tuple-element.7.heads_ref, s32[2,512]{1,0:T(2,128)} %get-tuple-element.6.tails_ref, ...), custom_call_target="tpu_custom_call" | custom-call | tf_op jit(solution)/shard_map/train_step/pallas_call | solution.py:230
  43.3 28.7 %all_to_all.15 = bf16[128,8,384]{2,1,0:T(8,128)(2,1)S(1)} all-to-all(bf16[128,8,384]{2,1,0:T(8,128)(2,1)} %bitcast.22), channel_id=1, replica_groups=mesh['bucket'=128,'rep'=2] {'bucket'}, dimensions={0} | all-to-all | bytes 1572864 | tf_op jit(solution)/shard_map/all_to_all | solution.py:263
  72.1 5.0 %collective-permute-start = (bf16[1024,384]{1,0:T(8,128)(2,1)S(1)}, bf16[1024,384]{1,0:T(8,128)(2,1)S(1)}, u32[]{:S(2)}, u32[]{:S(2)}) collective-permute-start(bf16[1024,384]{1,0:T(8,128)(2,1)S(1)} %bitcast.19), channel_id=1, source_target_pairs={{0,1},{1,0},{2,3},{3,2},{4,5},{5,4},{6,7},{7,6},{8,9},{9,8},{10,11... | collective-permute-start | bytes 2359304 | tf_op jit(solution)/shard_map/ppermute | solution.py:264
  77.1 1.9 %collective-permute-done.peer_ref = bf16[1024,384]{1,0:T(8,128)(2,1)S(1)} collective-permute-done((bf16[1024,384]{1,0:T(8,128)(2,1)S(1)}, bf16[1024,384]{1,0:T(8,128)(2,1)S(1)}, u32[]{:S(2)}, u32[]{:S(2)}) %collective-permute-start) | collective-permute-done | bytes 786464 | tf_op jit(solution)/shard_map/ppermute | solution.py:264
  79.0 0.0 copy-done
  79.0 0.9 copy-done.1
  79.9 2.6 %sum_relations.1 = bf16[2048,128]{1,0:T(8,128)(2,1)} custom-call(s32[1]{0:T(128)} %bitcast.7.rep_ref, bf16[1024,384]{1,0:T(8,128)(2,1)} %bitcast.20, bf16[1024,384]{1,0:T(8,128)(2,1)} %copy-done.1), custom_call_target="tpu_custom_call" | custom-call | tf_op jit(solution)/shard_map/sum_relations/pallas_call | solution.py:267
  82.6 24.0 %all_to_all.16 = bf16[128,16,128]{2,1,0:T(8,128)(2,1)S(1)} all-to-all(bf16[128,16,128]{2,1,0:T(8,128)(2,1)} %bitcast.23), channel_id=1, replica_groups=mesh['bucket'=128,'rep'=2] {'bucket'}, dimensions={0} | all-to-all | bytes 1048576 | tf_op jit(solution)/shard_map/all_to_all | solution.py:278
  106.6 3.0 %collective-permute-start.2 = (bf16[2048,128]{1,0:T(8,128)(2,1)S(1)}, bf16[2048,128]{1,0:T(8,128)(2,1)S(1)}, u32[]{:S(2)}, u32[]{:S(2)}) collective-permute-start(bf16[2048,128]{1,0:T(8,128)(2,1)S(1)} %bitcast.17), channel_id=1, source_target_pairs={{0,1},{1,0},{2,3},{3,2},{4,5},{5,4},{6,7},{7,6},{8,9},{9,8},{10,11... | collective-permute-start | bytes 1572872 | tf_op jit(solution)/shard_map/ppermute | solution.py:293
  109.6 0.0 collective-permute-start.1
  109.6 1.5 %collective-permute-done.1.peer_ids = f32[8,256]{1,0:T(8,128)S(1)} collective-permute-done((f32[8,256]{1,0:T(8,128)S(1)}, f32[8,256]{1,0:T(8,128)S(1)}, u32[]{:S(2)}, u32[]{:S(2)}) %collective-permute-start.1) | collective-permute-done | bytes 8224 | tf_op jit(solution)/shard_map/ppermute | solution.py:223
  111.2 0.6 copy-done.4
  111.8 4.6 %scatter_rows.1 = f32[1024,512]{1,0:T(8,128)} custom-call(bf16[1024,384]{1,0:T(8,128)(2,1)} %bitcast.21, bf16[1024,384]{1,0:T(8,128)(2,1)} %copy-done.1, f32[8,256]{1,0:T(8,128)} %get-tuple-element.5.own_ids, f32[8,256]{1,0:T(8,128)} %copy-done.4), custom_call_target="tpu_custom_call" | custom-call | tf_op jit(solution)/shard_map/scatter_rows/pallas_call | solution.py:283
  116.3 0.0 collective-permute-done.2.peer_ref
  116.3 2.8 %assemble_relations.1 = f32[16,8,64,64]{3,2,1,0:T(8,128)} custom-call(s32[1]{0:T(128)} %bitcast.7.rep_ref, bf16[2048,128]{1,0:T(8,128)(2,1)S(1)} %bitcast.18, bf16[2048,128]{1,0:T(8,128)(2,1)S(1)} %collective-permute-done.2.peer_ref), custom_call_target="tpu_custom_call" | custom-call | tf_op jit(solution)/shard_map/assemble_relations/pallas_call | solution.py:295
  (9 shorter events, 0.0 us)
Async XLA Ops:
  0.6 19.7 %copy-start.5 = (s32[1,1,2,1,1000]{4,3,2,1,0:T(1,128)S(1)}, s32[1,1,2,1,1000]{4,3,2,1,0:T(1,128)}, u32[]{:S(2)}) copy-start(s32[1,1,2,1,1000]{4,3,2,1,0:T(1,128)} %param.14) | copy-start | bytes 24004
  0.6 20.3 %copy-start.6 = (s32[1,1,2,1,512]{4,3,2,1,0:T(1,128)S(1)}, s32[1,1,2,1,512]{4,3,2,1,0:T(1,128)}, u32[]{:S(2)}) copy-start(s32[1,1,2,1,512]{4,3,2,1,0:T(1,128)} %param.13) | copy-start | bytes 12292
  0.7 20.3 %copy-start.7 = (s32[1,1,2,1,512]{4,3,2,1,0:T(1,128)S(1)}, s32[1,1,2,1,512]{4,3,2,1,0:T(1,128)}, u32[]{:S(2)}) copy-start(s32[1,1,2,1,512]{4,3,2,1,0:T(1,128)} %param.12) | copy-start | bytes 12292
  4.0 33.2 %all-to-all-start = ((bf16[128,8,256]{2,1,0:T(8,128)(2,1)}), bf16[128,8,256]{2,1,0:T(8,128)(2,1)S(1)}, u32[]{:S(2)}, u32[]{:S(2)}) async-start(bf16[128,8,256]{2,1,0:T(8,128)(2,1)} %bitcast.25), calls=%async_computation | async-start | bytes 1048576 | tf_op jit(solution)/shard_map/all_to_all | solution.py:225
  37.2 0.8 copy-start.2
  43.3 66.3 %copy-start.3 = (f32[8,256]{1,0:T(8,128)S(1)}, f32[8,256]{1,0:T(8,128)}, u32[]{:S(2)}) copy-start(f32[8,256]{1,0:T(8,128)} %get-tuple-element.5.own_ids) | copy-start | bytes 24580
  72.1 6.9 %copy-start = (bf16[128,8,384]{2,1,0:T(8,128)(2,1)}, bf16[128,8,384]{2,1,0:T(8,128)(2,1)S(1)}, u32[]{:S(2)}) copy-start(bf16[128,8,384]{2,1,0:T(8,128)(2,1)S(1)} %all_to_all.15) | copy-start | bytes 2359300
  72.1 6.9 %collective-permute-start = (bf16[1024,384]{1,0:T(8,128)(2,1)S(1)}, bf16[1024,384]{1,0:T(8,128)(2,1)S(1)}, u32[]{:S(2)}, u32[]{:S(2)}) collective-permute-start(bf16[1024,384]{1,0:T(8,128)(2,1)S(1)} %bitcast.19), channel_id=1, source_target_pairs={{0,1},{1,0},{2,3},{3,2},{4,5},{5,4},{6,7},{7,6},{8,9},{9,8},{10,11... | collective-permute-start | bytes 2359304 | tf_op jit(solution)/shard_map/ppermute | solution.py:264
  79.0 0.9 copy-start.1
  106.6 9.7 %collective-permute-start.2 = (bf16[2048,128]{1,0:T(8,128)(2,1)S(1)}, bf16[2048,128]{1,0:T(8,128)(2,1)S(1)}, u32[]{:S(2)}, u32[]{:S(2)}) collective-permute-start(bf16[2048,128]{1,0:T(8,128)(2,1)S(1)} %bitcast.17), channel_id=1, source_target_pairs={{0,1},{1,0},{2,3},{3,2},{4,5},{5,4},{6,7},{7,6},{8,9},{9,8},{10,11... | collective-permute-start | bytes 1572872 | tf_op jit(solution)/shard_map/ppermute | solution.py:293
  109.6 1.5 %collective-permute-start.1 = (f32[8,256]{1,0:T(8,128)S(1)}, f32[8,256]{1,0:T(8,128)S(1)}, u32[]{:S(2)}, u32[]{:S(2)}) collective-permute-start(f32[8,256]{1,0:T(8,128)S(1)} %copy-done.3), channel_id=1, source_target_pairs={{0,1},{1,0},{2,3},{3,2},{4,5},{5,4},{6,7},{7,6},{8,9},{9,8},{10,11... | collective-permute-start | bytes 24584 | tf_op jit(solution)/shard_map/ppermute | solution.py:223
  111.2 0.6 copy-start.4

commit v2 on v1

--- a/solution.py
+++ b/solution.py
@@ -138,7 +138,7 @@
     p = iota((256, 128), 0)
     g = iota((256, 128), 1)
     piece = p & 3
-    source = ((p >> 2) & 1) * 64 + (((p >> 3) & 1) * 2 + piece) * 16 + (p >> 4)
+    source = ((p >> 2) & 1) * 64 + (((p >> 3) & 1) * 2 + piece) * 16 + ((p >> 4) & 1) * 8 + (p >> 5)
     spread = onehot((g == source) & (piece < 2))
     named = jnp.where(((p >> 2) & 1) == 0, rel_ref[0], rel_ref[1]).astype(F32)
     for b in range(4):
@@ -148,23 +148,22 @@
         out_ref[b * 256 : b * 256 + 256, 256:384] = jnp.where(piece == 2, named, dot(spread, rows)).astype(BF16)
 
 
-def relation_kernel(rep_ref, own_ref, peer_ref, out_ref):
+def relation_kernel(rep_ref, own_ref, keep_ref, give_ref):
     matrix = unpack_matrix()
     lane = iota((128, 128), 1)
     totals = [jnp.zeros((128, 128), F32) for q in range(2)]
-    for ref in (own_ref, peer_ref):
-        blocks = [dot(matrix, ref[b * 256 : b * 256 + 256, :]) for b in range(4)]
-
-        def piece(index):
-            return jnp.concatenate([rows[index * 32 : index * 32 + 32] for rows in blocks], axis=0)
-
-        for k in range(2):
-            chosen = onehot(lane == piece(4 * k + 2).astype(jnp.int32))
-            for q in range(2):
-                totals[q] = totals[q] + dot(chosen, piece(4 * k + q).astype(BF16), 0, 0)
-    mine = jnp.where(rep_ref[0] == 0, totals[0], totals[1])[0:16].astype(BF16)
-    for d in range(128):
-        out_ref[d * 16 : d * 16 + 16, :] = mine
+    blocks = [dot(matrix, own_ref[b * 256 : b * 256 + 256, :]) for b in range(4)]
+
+    def piece(index):
+        return jnp.concatenate([rows[index * 32 : index * 32 + 32] for rows in blocks], axis=0)
+
+    for k in range(2):
+        chosen = onehot(lane == piece(4 * k + 2).astype(jnp.int32))
+        for q in range(2):
+            totals[q] = totals[q] + dot(chosen, piece(4 * k + q).astype(BF16), 0, 0)
+    first = rep_ref[0] == 0
+    keep_ref[...] = jnp.where(first, totals[0], totals[1])[0:16]
+    give_ref[...] = jnp.where(first, totals[1], totals[0])[0:16]
 
 
 def scatter_kernel(own_ref, peer_ref, own_ids, peer_ids, out_ref, rows_ref):
@@ -192,18 +191,39 @@
 def assemble_kernel(rep_ref, own_ref, peer_ref, out_ref):
     g = iota((256, 256), 0)
     p = iota((256, 256), 1)
-    matrix = onehot(p == ((g & 7) * 2 + ((g >> 3) & 1)) * 16 + (g >> 4))
+    matrix = onehot(p == ((g >> 3) & 1) * 128 + (g & 7) * 16 + (g >> 4))
     first = rep_ref[0] == 0
-    for d in range(8):
-        own = dot(matrix, own_ref[d * 256 : d * 256 + 256, :])
-        peer = dot(matrix, peer_ref[d * 256 : d * 256 + 256, :])
-        for q in range(2):
-            rows = jnp.where(first, own, peer) if q == 0 else jnp.where(first, peer, own)
-            rows = rows.reshape(16, 2, 8, 128)
-            for half in range(2):
-                block = half * 4 + q * 2
-                out_ref[:, block, d * 8 : d * 8 + 8, :] = rows[:, half, :, 0:64]
-                out_ref[:, block + 1, d * 8 : d * 8 + 8, :] = rows[:, half, :, 64:128]
+    for y in range(4):
+        for m in range(2):
+            rows = slice((y * 2 + m) * 256, (y * 2 + m) * 256 + 256)
+            own = dot(matrix, own_ref[rows, :])
+            peer = dot(matrix, peer_ref[rows, :])
+            for q in range(2):
+                part = jnp.where(first, own, peer) if q == 0 else jnp.where(first, peer, own)
+                part = part.reshape(16, 2, 8, 128)
+                for half in range(2):
+                    block = half * 4 + q * 2
+                    out_ref[:, block, (y * 2 + m) * 8 : (y * 2 + m) * 8 + 8, :] = part[:, half, :, 0:64]
+                    out_ref[:, block + 1, (y * 2 + m) * 8 : (y * 2 + m) * 8 + 8, :] = part[:, half, :, 64:128]
+
+
+def chip(y, z, x):
+    return (y * 8 + z) * 4 + x
+
+
+ALONG_Z = [[chip(y, z, x) for z in range(8)] for y in range(4) for x in range(4)]
+IN_PLANE = [[chip(y, z, x) for y in range(4) for x in range(4)] for z in range(8)]
+
+
+def gather_among(rows, groups):
+    count = len(groups[0])
+    spread = jnp.broadcast_to(rows[None], (count,) + rows.shape)
+    out = lax.all_to_all(spread, "bucket", 0, 0, axis_index_groups=groups, tiled=True)
+    return out.reshape(count * rows.shape[0], rows.shape[1])
+
+
+def limit(mib):
+    return pltpu.CompilerParams(vmem_limit_bytes=mib << 20)
 
 
 def body(entity_table, relations, send_rows, send_count, heads, tails, negatives, span_rel):
@@ -218,11 +238,13 @@
         in_specs=[VMEM] * 3,
         out_specs=(VMEM, VMEM),
         scratch_shapes=[pltpu.VMEM((2, 256, width), BF16)],
+        compiler_params=limit(16),
         name="send_rows",
     )(send_rows[0, 0], send_count[0, 0], entity_table)
     peer_ids = lax.ppermute(ids, "rep", swap)
 
-    received = lax.all_to_all(packed.reshape(chips, 8, 256), "bucket", 0, 0, tiled=True)
+    received = lax.all_to_all(packed.reshape(chips, 8, 256), "bucket", 0, 0, tiled=True).reshape(chips * 8, 256)
+    received, peer_ids = lax.optimization_barrier((received, peer_ids))
 
     rel_ids = span_rel.reshape(2)
     whole = lambda shape: pl.BlockSpec(shape, lambda i, rel: (0,) * len(shape))
@@ -249,10 +271,11 @@
                 pltpu.VMEM((2, 64, width), BF16),
             ],
         ),
+        compiler_params=limit(24),
         name="train_step",
     )(
         rel_ids,
-        received.reshape(chips * 8, 256),
+        received,
         relations,
         relations,
         heads.reshape(2, -1),
@@ -261,22 +284,25 @@
     )
 
     own = lax.all_to_all(returned.reshape(chips, 8, 384), "bucket", 0, 0, tiled=True).reshape(chips * 8, 384)
-    peer = lax.ppermute(own, "rep", swap)
-
-    slice_spec = pl.BlockSpec((chips * 8, 128), lambda i, rep: (0, 2))
-    slices = pl.pallas_call(
+
+    half_sum = jax.ShapeDtypeStruct((16, 128), F32)
+    half_spec = pl.BlockSpec((16, 128), lambda i, rep: (0, 0))
+    keep, give = pl.pallas_call(
         relation_kernel,
-        out_shape=jax.ShapeDtypeStruct((chips * 16, 128), BF16),
+        out_shape=(half_sum, half_sum),
         grid_spec=pltpu.PrefetchScalarGridSpec(
             num_scalar_prefetch=1,
             grid=(1,),
-            in_specs=[slice_spec, slice_spec],
-            out_specs=pl.BlockSpec((chips * 16, 128), lambda i, rep: (0, 0)),
+            in_specs=[pl.BlockSpec((chips * 8, 128), lambda i, rep: (0, 2))],
+            out_specs=(half_spec, half_spec),
         ),
+        compiler_params=limit(16),
         name="sum_relations",
-    )(rep, own, peer)
-    gathered = lax.all_to_all(slices.reshape(chips, 16, 128), "bucket", 0, 0, tiled=True).reshape(chips * 16, 128)
-
+    )(rep, own)
+    sums = (keep + lax.ppermute(give, "rep", swap)).astype(BF16)
+    gathered = gather_among(gather_among(sums, ALONG_Z), IN_PLANE)
+
+    peer = lax.ppermute(own, "rep", swap)
     chunk = 256
     rows_spec = pl.BlockSpec((chips * 8, 256), lambda i: (0, 0))
     ids_spec = pl.BlockSpec((8, 256), lambda i: (0, 0))
@@ -287,21 +313,23 @@
         in_specs=[rows_spec, rows_spec, ids_spec, ids_spec],
         out_specs=pl.BlockSpec((chunk, width), lambda i: (i, 0)),
         scratch_shapes=[pltpu.VMEM((1024, width), BF16)],
+        compiler_params=limit(16),
+        cost_estimate=pl.CostEstimate(flops=2 * 1024 * entities * width, bytes_accessed=16 << 20, transcendentals=0),
         name="scatter_rows",
     )(own, peer, ids, peer_ids)
 
+    gathered, entity_grad = lax.optimization_barrier((gathered, entity_grad))
     peer_gathered = lax.ppermute(gathered, "rep", swap)
-    full = lambda i, rep: (0, 0)
     relation_grad = pl.pallas_call(
         assemble_kernel,
         out_shape=jax.ShapeDtypeStruct(relations.shape, F32),
         grid_spec=pltpu.PrefetchScalarGridSpec(
             num_scalar_prefetch=1,
             grid=(1,),
-            in_specs=[pl.BlockSpec((chips * 16, 128), full)] * 2,
+            in_specs=[pl.BlockSpec((chips * 16, 128), lambda i, rep: (0, 0))] * 2,
             out_specs=pl.BlockSpec(relations.shape, lambda i, rep: (0, 0, 0, 0)),
         ),
-        compiler_params=pltpu.CompilerParams(vmem_limit_bytes=48 << 20),
+        compiler_params=limit(24),
         name="assemble_relations",
     )(rep, gathered, peer_gathered)
     return entity_grad, relation_grad

time: 120 us -> 109 us (0.908)
  blocking collectives: 52.8 us -> 38.7 us
  Pallas kernels: 18.6 us -> 12 us
  waiting for transfers between devices: 19.1 us -> 24.5 us
  starting transfers between devices: 24.4 us -> 28.5 us
    all_to_all x1, blocking collectives: 24 us -> 10.3 us  [gather_among(): lax.all_to_all(spread, 'bucket', 0, 0, axis_index_groups=groups, tiled=True)]
    all_to_all x0 -> x1, waiting for transfers between devices: none -> 6.56 us  [gather_among(): lax.all_to_all(spread, 'bucket', 0, 0, axis_index_groups=groups, tiled=True)]
    all_to_all x0 -> x1, starting transfers between devices: none -> 3.57 us  [gather_among(): lax.all_to_all(spread, 'bucket', 0, 0, axis_index_groups=groups, tiled=True)]
    pallas_call x1, Pallas kernels: 5.34 us -> 3.17 us  [body(): pl.pallas_call(step_kernel, out_shape=jax.ShapeDtypeStruct((chips * 8, 38...]
    pallas_call x1, Pallas kernels: 2.65 us -> 0.5 us  [body(): pl.pallas_call(relation_kernel, out_shape=(half_sum, half_sum), grid_spec...]
    ppermute x1, waiting for transfers between devices: 1.91 us -> 0.01 us  [body(): peer = lax.ppermute(own, 'rep', swap)]
    ppermute x1, waiting for transfers between devices: 0.01 us -> 1.54 us  [body(): peer_gathered = lax.ppermute(gathered, 'rep', swap)]
    ppermute x1, waiting for transfers between devices: 1.54 us -> 0.11 us  [body(): peer_ids = lax.ppermute(ids, 'rep', swap)]
  transfers between devices with their start and end apart: 4 -> 6, of which waited for: 3 -> 5; matrix products, arithmetic and copies ran while one was open for 1% -> 1% of each run, Pallas kernels for 4% -> 4%
where the time goes in v2:
time: 109 us
  blocking collectives  38.7 us (36%)
  starting transfers between devices  28.5 us (26%)
  waiting for transfers between devices  24.5 us (22%)
  Pallas kernels  12 us (11%)
  local copies, waits for them, and re-layouts  4.35 us (4%)
    all_to_all x1, blocking collectives, body(): lax.all_to_all(returned.reshape(chips, 8, 384), 'bucket', 0, 0, tiled=True)  28.4 us
    all_to_all x1, starting transfers between devices, body(): lax.all_to_all(packed.reshape(chips, 8, 256), 'bucket', 0, 0, tiled=True)  16.3 us
    all_to_all x1, waiting for transfers between devices, body(): lax.all_to_all(packed.reshape(chips, 8, 256), 'bucket', 0, 0, tiled=True)  15 us
    all_to_all x1, blocking collectives, gather_among(): lax.all_to_all(spread, 'bucket', 0, 0, axis_index_groups=groups, tiled=True)  10.3 us
    all_to_all x1, waiting for transfers between devices, gather_among(): lax.all_to_all(spread, 'bucket', 0, 0, axis_index_groups=groups, tiled=True)  6.56 us
    ppermute x1, starting transfers between devices, body(): peer = lax.ppermute(own, 'rep', swap)  5.03 us
    all_to_all x1, starting transfers between devices, gather_among(): lax.all_to_all(spread, 'bucket', 0, 0, axis_index_groups=groups, tiled=True)  3.57 us
    pallas_call x1, Pallas kernels, body(): pl.pallas_call(scatter_kernel, out_shape=jax.ShapeDtypeStruct((entities,...  3.46 us
  transfers between devices with their start and end apart: 6, of which 5 were waited for; matrix products, arithmetic and copies ran while one was open for 1% of the time, Pallas kernels for 4%

profile of v2, /device:TPU:1, one launch (start us, length us, event | category | flops | bytes accessed | tf_op | source)
XLA Modules:
  0.0 108.8 jit_solution(14125303887107844478)
XLA Ops:
  0.7 1.4 %copy-done.1 = bf16[1024,512]{1,0:T(8,128)(2,1)S(1)} copy-done((bf16[1024,512]{1,0:T(8,128)(2,1)S(1)}, bf16[1024,512]{1,0:T(8,128)(2,1)}, u32[]{:S(2)}) %copy-start.1) | copy-done | bytes 1048600
  2.0 0.7 copy-done.2
  2.7 0.7 copy-done.3
  3.4 2.0 %send_rows.1 = (bf16[1024,256]{1,0:T(8,128)(2,1)}, f32[8,256]{1,0:T(8,128)S(1)}) custom-call(s32[2,256]{1,0:T(2,128)S(1)} %bitcast.25, s32[2,128]{1,0:T(2,128)S(1)} %bitcast.26, bf16[1024,512]{1,0:T(8,128)(2,1)S(1)} %copy-done.1), custom_call_target="tpu_custom_call" | custom-call | tf_op jit(solution)/shard_map/send_rows/pallas_call | solution.py:235
  5.4 16.3 %all-to-all-start = ((bf16[128,8,256]{2,1,0:T(8,128)(2,1)}), bf16[128,8,256]{2,1,0:T(8,128)(2,1)S(1)}, u32[]{:S(2)}, u32[]{:S(2)}) async-start(bf16[128,8,256]{2,1,0:T(8,128)(2,1)} %bitcast.4), calls=%async_computation | async-start | bytes 1048576 | tf_op jit(solution)/shard_map/all_to_all | solution.py:246
  21.8 1.0 collective-permute-start
  22.8 0.7 copy_bitcast_fusion.1
  23.5 0.1 collective-permute-done.peer_ids
  23.6 15.0 %all-to-all-done = bf16[128,8,256]{2,1,0:T(8,128)(2,1)S(1)} async-done(((bf16[128,8,256]{2,1,0:T(8,128)(2,1)}), bf16[128,8,256]{2,1,0:T(8,128)(2,1)S(1)}, u32[]{:S(2)}, u32[]{:S(2)}) %all-to-all-start) | async-done | bytes 524320 | tf_op jit(solution)/shard_map/all_to_all | solution.py:246
  38.6 3.2 %train_step.1 = bf16[1024,384]{1,0:T(8,128)(2,1)S(1)} custom-call(s32[2]{0:T(128)S(1)} %bitcast.27, bf16[1024,256]{1,0:T(8,128)(2,1)S(1)} %bitcast.23, bf16[16,8,64,64]{3,2,1,0:T(8,128)(2,1)S(1)} %copy-done, bf16[16,8,64,64]{3,2,1,0:T(8,128)(2,1)S(1)} %copy-done, s32[2,512]{1,0:T(2,128)S(1)} %get-tuple-element.19.heads_ref, ...), custom_call_target="tpu_custom_call" | custom-call | tf_op jit(solution)/shard_map/train_step/pallas_call | solution.py:252
  41.8 28.4 %all_to_all.20 = bf16[128,8,384]{2,1,0:T(8,128)(2,1)S(1)} all-to-all(bf16[128,8,384]{2,1,0:T(8,128)(2,1)S(1)} %bitcast.20), channel_id=1, replica_groups=mesh['bucket'=128,'rep'=2] {'bucket'}, dimensions={0} | all-to-all | bytes 1572864 | tf_op jit(solution)/shard_map/all_to_all | solution.py:286
  70.2 5.0 %collective-permute-start.2 = (bf16[1024,384]{1,0:T(8,128)(2,1)S(1)}, bf16[1024,384]{1,0:T(8,128)(2,1)S(1)}, u32[]{:S(2)}, u32[]{:S(2)}) collective-permute-start(bf16[1024,384]{1,0:T(8,128)(2,1)S(1)} %bitcast.17), channel_id=1, source_target_pairs={{0,1},{1,0},{2,3},{3,2},{4,5},{5,4},{6,7},{7,6},{8,9},{9,8},{10,11... | collective-permute-start | bytes 2359304 | tf_op jit(solution)/shard_map/ppermute | solution.py:305
  75.3 0.5 sum_relations.1
  75.8 0.1 collective-permute-start.1
  75.9 1.3 %collective-permute-done.1 = f32[16,128]{1,0:T(8,128)S(1)} collective-permute-done((f32[16,128]{1,0:T(8,128)S(1)}, f32[16,128]{1,0:T(8,128)S(1)}, u32[]{:S(2)}, u32[]{:S(2)}) %collective-permute-start.1) | collective-permute-done | bytes 8224 | tf_op jit(solution)/shard_map/ppermute | solution.py:302
  77.2 10.3 %all_to_all.21 = bf16[8,16,128]{2,1,0:T(8,128)(2,1)S(1)} all-to-all(bf16[8,16,128]{2,1,0:T(8,128)(2,1)S(1)} %broadcast_in_dim.6), channel_id=1, replica_groups={{0,8,16,24,32,40,48,56},{2,10,18,26,34,42,50,58},{4,12,20,28,36,44,52,6..., dimensions={0} | all-to-all | bytes 65536 | tf_op jit(solution)/shard_map/all_to_all | solution.py:221
  87.5 0.9 broadcast_in_dim.15
  88.4 3.6 %all-to-all-start.3 = ((bf16[16,128,128]{2,1,0:T(8,128)(2,1)}), bf16[16,128,128]{2,1,0:T(8,128)(2,1)S(1)}, u32[]{:S(2)}, u32[]{:S(2)}) async-start(bf16[16,128,128]{2,1,0:T(8,128)(2,1)} %broadcast_in_dim.15), calls=%async_computation.3 | async-start | bytes 1048576 | tf_op jit(solution)/shard_map/all_to_all | solution.py:221
  92.0 0.0 collective-permute-done.2.peer_ref
  92.0 3.5 %scatter_rows.1 = f32[1024,512]{1,0:T(8,128)} custom-call(bf16[1024,384]{1,0:T(8,128)(2,1)S(1)} %bitcast.19, bf16[1024,384]{1,0:T(8,128)(2,1)S(1)} %collective-permute-done.2.peer_ref, f32[8,256]{1,0:T(8,128)S(1)} %get-tuple-element.11.own_ids, f32[8,256]{1,0:T(8,128)S(1)} %collective-permute-done.peer_ids), custom_call_target="tpu_custom_call" | custom-call | flops 1073741824 | bytes 16777216 | tf_op jit(solution)/shard_map/scatter_rows/pallas_call | solution.py:309
  95.4 6.6 %all-to-all-done.3 = bf16[16,128,128]{2,1,0:T(8,128)(2,1)S(1)} async-done(((bf16[16,128,128]{2,1,0:T(8,128)(2,1)}), bf16[16,128,128]{2,1,0:T(8,128)(2,1)S(1)}, u32[]{:S(2)}, u32[]{:S(2)}) %all-to-all-start.3) | async-done | bytes 524320 | tf_op jit(solution)/shard_map/all_to_all | solution.py:221
  102.0 2.5 %collective-permute-start.3 = (bf16[2048,128]{1,0:T(8,128)(2,1)S(1)}, bf16[2048,128]{1,0:T(8,128)(2,1)S(1)}, u32[]{:S(2)}, u32[]{:S(2)}) collective-permute-start(bf16[2048,128]{1,0:T(8,128)(2,1)S(1)} %bitcast.21), channel_id=1, source_target_pairs={{0,1},{1,0},{2,3},{3,2},{4,5},{5,4},{6,7},{7,6},{8,9},{9,8},{10,11... | collective-permute-start | bytes 1572872 | tf_op jit(solution)/shard_map/ppermute | solution.py:322
  104.4 1.5 %collective-permute-done.3.peer_ref = bf16[2048,128]{1,0:T(8,128)(2,1)S(1)} collective-permute-done((bf16[2048,128]{1,0:T(8,128)(2,1)S(1)}, bf16[2048,128]{1,0:T(8,128)(2,1)S(1)}, u32[]{:S(2)}, u32[]{:S(2)}) %collective-permute-start.3) | collective-permute-done | bytes 524320 | tf_op jit(solution)/shard_map/ppermute | solution.py:322
  106.0 2.8 %assemble_relations.1 = f32[16,8,64,64]{3,2,1,0:T(8,128)} custom-call(s32[1]{0:T(128)} %bitcast.rep_ref, bf16[2048,128]{1,0:T(8,128)(2,1)S(1)} %bitcast.22, bf16[2048,128]{1,0:T(8,128)(2,1)S(1)} %collective-permute-done.3.peer_ref), custom_call_target="tpu_custom_call" | custom-call | tf_op jit(solution)/shard_map/assemble_relations/pallas_call | solution.py:323
  (12 shorter events, 0.0 us)
Async XLA Ops:
  0.6 38.0 %copy-start = (bf16[16,8,64,64]{3,2,1,0:T(8,128)(2,1)S(1)}, bf16[16,8,64,64]{3,2,1,0:T(8,128)(2,1)}, u32[]{:S(2)}) copy-start(bf16[16,8,64,64]{3,2,1,0:T(8,128)(2,1)} %second_ref.1) | copy-start | bytes 3145732
  0.6 1.4 %copy-start.1 = (bf16[1024,512]{1,0:T(8,128)(2,1)S(1)}, bf16[1024,512]{1,0:T(8,128)(2,1)}, u32[]{:S(2)}) copy-start(bf16[1024,512]{1,0:T(8,128)(2,1)} %table_ref.1) | copy-start | bytes 3145732
  2.0 0.7 copy-start.2
  2.7 0.7 copy-start.3
  3.4 20.1 %copy-start.5 = (s32[1,1,2,1,1000]{4,3,2,1,0:T(1,128)S(1)}, s32[1,1,2,1,1000]{4,3,2,1,0:T(1,128)}, u32[]{:S(2)}) copy-start(s32[1,1,2,1,1000]{4,3,2,1,0:T(1,128)} %param.14) | copy-start | bytes 24004
  3.4 35.3 %copy-start.4 = (s32[1,1,2,1]{2,3,1,0:T(1,128)S(1)}, s32[1,1,2,1]{2,3,1,0:T(1,128)}, u32[]{:S(2)}) copy-start(s32[1,1,2,1]{2,3,1,0:T(1,128)} %param.15) | copy-start | bytes 28
  5.4 33.2 %all-to-all-start = ((bf16[128,8,256]{2,1,0:T(8,128)(2,1)}), bf16[128,8,256]{2,1,0:T(8,128)(2,1)S(1)}, u32[]{:S(2)}, u32[]{:S(2)}) async-start(bf16[128,8,256]{2,1,0:T(8,128)(2,1)} %bitcast.4), calls=%async_computation | async-start | bytes 1048576 | tf_op jit(solution)/shard_map/all_to_all | solution.py:246
  21.8 1.9 %collective-permute-start = (f32[8,256]{1,0:T(8,128)S(1)}, f32[8,256]{1,0:T(8,128)S(1)}, u32[]{:S(2)}, u32[]{:S(2)}) collective-permute-start(f32[8,256]{1,0:T(8,128)S(1)} %get-tuple-element.11.own_ids), channel_id=1, source_target_pairs={{0,1},{1,0},{2,3},{3,2},{4,5},{5,4},{6,7},{7,6},{8,9},{9,8},{10,11... | collective-permute-start | bytes 24584 | tf_op jit(solution)/shard_map/ppermute | solution.py:244
  70.2 21.7 %collective-permute-start.2 = (bf16[1024,384]{1,0:T(8,128)(2,1)S(1)}, bf16[1024,384]{1,0:T(8,128)(2,1)S(1)}, u32[]{:S(2)}, u32[]{:S(2)}) collective-permute-start(bf16[1024,384]{1,0:T(8,128)(2,1)S(1)} %bitcast.17), channel_id=1, source_target_pairs={{0,1},{1,0},{2,3},{3,2},{4,5},{5,4},{6,7},{7,6},{8,9},{9,8},{10,11... | collective-permute-start | bytes 2359304 | tf_op jit(solution)/shard_map/ppermute | solution.py:305
  75.8 1.4 %collective-permute-start.1 = (f32[16,128]{1,0:T(8,128)S(1)}, f32[16,128]{1,0:T(8,128)S(1)}, u32[]{:S(2)}, u32[]{:S(2)}) collective-permute-start(f32[16,128]{1,0:T(8,128)S(1)} %get-tuple-element.14), channel_id=1, source_target_pairs={{0,1},{1,0},{2,3},{3,2},{4,5},{5,4},{6,7},{7,6},{8,9},{9,8},{10,11... | collective-permute-start | bytes 24584 | tf_op jit(solution)/shard_map/ppermute | solution.py:302
  88.4 13.6 %all-to-all-start.3 = ((bf16[16,128,128]{2,1,0:T(8,128)(2,1)}), bf16[16,128,128]{2,1,0:T(8,128)(2,1)S(1)}, u32[]{:S(2)}, u32[]{:S(2)}) async-start(bf16[16,128,128]{2,1,0:T(8,128)(2,1)} %broadcast_in_dim.15), calls=%async_computation.3 | async-start | bytes 1048576 | tf_op jit(solution)/shard_map/all_to_all | solution.py:221
  102.0 4.0 %collective-permute-start.3 = (bf16[2048,128]{1,0:T(8,128)(2,1)S(1)}, bf16[2048,128]{1,0:T(8,128)(2,1)S(1)}, u32[]{:S(2)}, u32[]{:S(2)}) collective-permute-start(bf16[2048,128]{1,0:T(8,128)(2,1)S(1)} %bitcast.21), channel_id=1, source_target_pairs={{0,1},{1,0},{2,3},{3,2},{4,5},{5,4},{6,7},{7,6},{8,9},{9,8},{10,11... | collective-permute-start | bytes 1572872 | tf_op jit(solution)/shard_map/ppermute | solution.py:322

commit v3 on v2

--- a/solution.py
+++ b/solution.py
@@ -10,6 +10,7 @@
 F32 = jnp.float32
 BF16 = jnp.bfloat16
 VMEM = pl.BlockSpec(memory_space=pltpu.VMEM)
+HBM = pl.BlockSpec(memory_space=pltpu.HBM)
 
 
 def iota(shape, dim):
@@ -59,66 +60,105 @@
                 write(k, b, h, rows[start : start + 64])
 
 
-def send_kernel(rows_ref, count_ref, table_ref, packed_ref, ids_ref, slots):
-    table = table_ref[...]
+def send_kernel(
+    rows_hbm, count_hbm, table_ref, packed_ref, ids_ref, rows_ref, count_ref, table, slots, packed, list_sem, in_sem, out_sem
+):
+    part = table.shape[0] // 4
+    lists = [
+        pltpu.make_async_copy(rows_hbm, rows_ref, list_sem.at[0]),
+        pltpu.make_async_copy(count_hbm, count_ref, list_sem.at[1]),
+    ]
+    for copy in lists:
+        copy.start()
+
+    def fetch(n):
+        rows = pl.ds(n * part, part)
+        return pltpu.make_async_copy(table_ref.at[rows], table.at[rows], in_sem.at[n])
+
+    def send(b):
+        rows = pl.ds(b * 256, 256)
+        return pltpu.make_async_copy(packed.at[rows], packed_ref.at[rows], out_sem.at[b])
+
+    for n in range(4):
+        fetch(n).start()
     row = iota((256, 128), 0)
-    chip = (row >> 6) * 32 + (row & 31)
+    dest = (row >> 6) * 32 + (row & 31)
     other = iota((256, 128), 1)
     column = (iota((256, 1), 0) >> 5) & 1
     flat = iota((256, 256), 1)
-    entity = iota((256, table.shape[0]), 1)
+    entity = iota((256, part), 1)
     ids_ref[...] = jnp.zeros_like(ids_ref)
+    wanted = []
+    for copy in lists:
+        copy.wait()
     for k in range(2):
         counts = count_ref[k : k + 1, :].astype(F32)
-        start = jnp.sum(jnp.where(other < chip, counts, 0.0), axis=1, keepdims=True)
-        count = jnp.sum(jnp.where(other == chip, counts, 0.0), axis=1, keepdims=True)
+        start = jnp.sum(jnp.where(other < dest, counts, 0.0), axis=1, keepdims=True)
+        count = jnp.sum(jnp.where(other == dest, counts, 0.0), axis=1, keepdims=True)
         position = start.astype(jnp.int32) + column
         names = rows_ref[k : k + 1, :].astype(F32)
         ids = jnp.sum(jnp.where(flat == position, names, 0.0), axis=1, keepdims=True)
         ids = jnp.where(column < count.astype(jnp.int32), ids, -1.0)
         ids_ref[k : k + 1, :] = jnp.transpose(jnp.broadcast_to(ids, (256, 128)))[0:1, :]
-        chosen = onehot(entity == ids.astype(jnp.int32))
-        slots[k] = dot(chosen, table).astype(BF16)
+        wanted.append(ids.astype(jnp.int32))
+    totals = [jnp.zeros(slots.shape[1:], F32) for k in range(2)]
+    for n in range(4):
+        fetch(n).wait()
+        rows = table[n * part : n * part + part, :]
+        for k in range(2):
+            totals[k] = totals[k] + dot(onehot(entity + n * part == wanted[k]), rows)
+    for k in range(2):
+        slots[k] = totals[k].astype(BF16)
 
     def write(b, rows):
-        packed_ref[b * 256 : b * 256 + 256, :] = rows
+        packed[b * 256 : b * 256 + 256, :] = rows
+        send(b).start()
 
     pack_slots(lambda k, b: slots[k, b * 64 : b * 64 + 64, :], write)
-
-
-def step_kernel(
-    rel_ref, packed_ref, first_ref, second_ref, heads_ref, tails_ref, neg_ref, out_ref, slots, diag, grads, partial
-):
-    def write(k, b, h, rows):
-        slots[k, b * 64 : b * 64 + 64, h * 256 : h * 256 + 256] = rows
-
-    unpack_slots(lambda b: packed_ref[b * 256 : b * 256 + 256, :], write)
+    for b in range(4):
+        send(b).wait()
+
+
+def count_kernel(rel_ref, first_ref, second_ref, heads_ref, tails_ref, neg_ref, names_ref, diag_ref, edges_ref, pairs_ref):
     neg_count = neg_ref.shape[1]
-    lane_block = iota((64, 256), 1) >> 6
+    names_ref[...] = jnp.where(iota((8, 128), 0) == 0, rel_ref[0], rel_ref[1]).astype(F32)
     for k in range(2):
         relation = (first_ref, second_ref)[k]
         for c in range(2):
             for j in range(4):
                 place = onehot(iota((64, 256), 1) == iota((64, 256), 0) + 64 * j)
-                diag[k, c, 64 * j : 64 * j + 64, :] = dot(relation[0, 4 * c + j], place).astype(BF16)
-        rows = slots[k]
-        rotated = jnp.concatenate(
-            [dot(rows[:, c * 256 : c * 256 + 256], diag[k, c]) for c in range(2)], axis=1
-        ).astype(BF16)
-        slot = iota((256, 512), 0)
+                diag_ref[k, c, 64 * j : 64 * j + 64, :] = dot(relation[0, 4 * c + j], place).astype(BF16)
+        slot = iota((256, heads_ref.shape[1]), 0)
         at_head = onehot(slot == slot_row(heads_ref[k : k + 1, :]))
         at_tail = onehot(slot == slot_row(tails_ref[k : k + 1, :]))
         edges = dot(at_head, at_tail, 1, 1)
         head_edges = jnp.sum(edges, axis=1, keepdims=True)
         at_neg = onehot(iota((256, neg_count), 0) == slot_row(neg_ref[k : k + 1, :]))
         times = dot(jnp.ones((8, neg_count), BF16), at_neg, 1, 1)[0:1, :]
+        edges_ref[k] = edges
+        pairs_ref[k] = head_edges * times
+
+
+def step_kernel(
+    neg_count, packed_ref, names, diag, edges, pairs, out_ref, slots, grads, partial
+):
+    def write(k, b, h, rows):
+        slots[k, b * 64 : b * 64 + 64, h * 256 : h * 256 + 256] = rows
+
+    unpack_slots(lambda b: packed_ref[b * 256 : b * 256 + 256, :], write)
+    lane_block = iota((64, 256), 1) >> 6
+    for k in range(2):
+        rows = slots[k]
+        rotated = jnp.concatenate(
+            [dot(rows[:, c * 256 : c * 256 + 256], diag[k, c]) for c in range(2)], axis=1
+        ).astype(BF16)
         score = dot(rotated, rows, 1, 1)
         small = jnp.exp(-jnp.abs(score))
         big_side = 1.0 / (1.0 + small)
         small_side = small * big_side
         sigmoid = jnp.where(score >= 0, big_side, small_side)
         sigmoid_neg = jnp.where(score >= 0, small_side, big_side)
-        weight = ((head_edges * times) * sigmoid / neg_count - edges * sigmoid_neg).astype(BF16)
+        weight = (pairs[k] * sigmoid / neg_count - edges[k] * sigmoid_neg).astype(BF16)
         grad_rotated = dot(weight, rows).astype(BF16)
         grad_other = dot(weight, rotated, 0, 0)
         for c in range(2):
@@ -131,21 +171,21 @@
                 total = jnp.where(lane_block == j, outer[64 * j : 64 * j + 64, :], total)
             partial[k, :, lanes] = total.astype(BF16)
 
-    def write_packed(b, rows):
-        out_ref[b * 256 : b * 256 + 256, 0:256] = rows
-
-    pack_slots(lambda k, b: grads[k, b * 64 : b * 64 + 64, :], write_packed)
     p = iota((256, 128), 0)
     g = iota((256, 128), 1)
     piece = p & 3
     source = ((p >> 2) & 1) * 64 + (((p >> 3) & 1) * 2 + piece) * 16 + ((p >> 4) & 1) * 8 + (p >> 5)
     spread = onehot((g == source) & (piece < 2))
-    named = jnp.where(((p >> 2) & 1) == 0, rel_ref[0], rel_ref[1]).astype(F32)
-    for b in range(4):
+    named = jnp.where(((p >> 2) & 1) == 0, names[0:1, :], names[1:2, :])
+
+    def write_packed(b, rows):
+        out_ref[b * 256 : b * 256 + 256, 0:256] = rows
         rows = jnp.concatenate(
             [partial[k, b * 16 : b * 16 + 16, q * 128 : q * 128 + 128] for k in range(2) for q in range(4)], axis=0
         )
         out_ref[b * 256 : b * 256 + 256, 256:384] = jnp.where(piece == 2, named, dot(spread, rows)).astype(BF16)
+
+    pack_slots(lambda k, b: grads[k, b * 64 : b * 64 + 64, :], write_packed)
 
 
 def relation_kernel(rep_ref, own_ref, keep_ref, give_ref):
@@ -188,31 +228,30 @@
     out_ref[...] = total
 
 
-def assemble_kernel(rep_ref, own_ref, peer_ref, out_ref):
+def assemble_kernel(place_ref, *refs):
+    pieces, out_ref = refs[:4], refs[-1]
     g = iota((256, 256), 0)
     p = iota((256, 256), 1)
-    matrix = onehot(p == ((g >> 3) & 1) * 128 + (g & 7) * 16 + (g >> 4))
-    first = rep_ref[0] == 0
-    for y in range(4):
-        for m in range(2):
-            rows = slice((y * 2 + m) * 256, (y * 2 + m) * 256 + 256)
-            own = dot(matrix, own_ref[rows, :])
-            peer = dot(matrix, peer_ref[rows, :])
-            for q in range(2):
-                part = jnp.where(first, own, peer) if q == 0 else jnp.where(first, peer, own)
-                part = part.reshape(16, 2, 8, 128)
-                for half in range(2):
-                    block = half * 4 + q * 2
-                    out_ref[:, block, (y * 2 + m) * 8 : (y * 2 + m) * 8 + 8, :] = part[:, half, :, 0:64]
-                    out_ref[:, block + 1, (y * 2 + m) * 8 : (y * 2 + m) * 8 + 8, :] = part[:, half, :, 64:128]
+    matrix = onehot(p == (g & 15) * 16 + (g >> 4))
+    for shift in range(4):
+
+        @pl.when(pl.program_id(0) == shift)
+        def _():
+            for y in range(2):
+                rows = dot(matrix, pieces[shift][y * 256 : y * 256 + 256, :]).reshape(16, 2, 8, 128)
+                for side in range(2):
+                    out_ref[:, 0, 0, side, 2 * y : 2 * y + 2, 0] = rows[:, :, :, 64 * side : 64 * side + 64]
 
 
 def chip(y, z, x):
     return (y * 8 + z) * 4 + x
 
 
-ALONG_Z = [[chip(y, z, x) for z in range(8)] for y in range(4) for x in range(4)]
-IN_PLANE = [[chip(y, z, x) for y in range(4) for x in range(4)] for z in range(8)]
+ACROSS_YZ = [[chip(y, z, x) for y in range(4) for z in range(8)] for x in range(4)]
+
+
+def along_x(step):
+    return [(chip(y, z, x), chip(y, z, (x + step) % 4)) for y in range(4) for z in range(8) for x in range(4)]
 
 
 def gather_among(rows, groups):
@@ -222,6 +261,33 @@
     return out.reshape(count * rows.shape[0], rows.shape[1])
 
 
+def assemble(place, pieces, into):
+    view = (16, 2, 2, 2, 4, 2, 8, 64)
+
+    def where(shift, place):
+        x = (place[0] - shift) & 3
+        return (0, x & 1, place[1], 0, 0, x >> 1, 0, 0)
+
+    arrays = list(pieces) + ([] if into is None else [into])
+    specs = [pl.BlockSpec(pieces[0].shape, lambda shift, place: (0, 0))] * 4
+    if into is not None:
+        specs.append(pl.BlockSpec(memory_space=pl.ANY))
+    return pl.pallas_call(
+        assemble_kernel,
+        out_shape=jax.ShapeDtypeStruct(view, F32),
+        grid_spec=pltpu.PrefetchScalarGridSpec(
+            num_scalar_prefetch=1,
+            grid=(4,),
+            in_specs=specs,
+            out_specs=pl.BlockSpec((16, 1, 1, 2, 4, 1, 8, 64), where),
+        ),
+        input_output_aliases={} if into is None else {5: 0},
+        compiler_params=limit(8),
+        cost_estimate=pl.CostEstimate(flops=1 << 27, bytes_accessed=3 << 20, transcendentals=0),
+        name="assemble_relations",
+    )(place, *arrays)
+
+
 def limit(mib):
     return pltpu.CompilerParams(vmem_limit_bytes=mib << 20)
 
@@ -235,53 +301,62 @@
     packed, ids = pl.pallas_call(
         send_kernel,
         out_shape=(jax.ShapeDtypeStruct((chips * 8, 256), BF16), jax.ShapeDtypeStruct((8, 256), F32)),
-        in_specs=[VMEM] * 3,
-        out_specs=(VMEM, VMEM),
-        scratch_shapes=[pltpu.VMEM((2, 256, width), BF16)],
-        compiler_params=limit(16),
+        in_specs=[HBM, HBM, HBM],
+        out_specs=(HBM, VMEM),
+        scratch_shapes=[
+            pltpu.VMEM(send_rows.shape[2:], jnp.int32),
+            pltpu.VMEM(send_count.shape[2:], jnp.int32),
+            pltpu.VMEM((entities, width), BF16),
+            pltpu.VMEM((2, 256, width), BF16),
+            pltpu.VMEM((chips * 8, 256), BF16),
+            pltpu.SemaphoreType.DMA((2,)),
+            pltpu.SemaphoreType.DMA((4,)),
+            pltpu.SemaphoreType.DMA((4,)),
+        ],
         name="send_rows",
     )(send_rows[0, 0], send_count[0, 0], entity_table)
     peer_ids = lax.ppermute(ids, "rep", swap)
 
     received = lax.all_to_all(packed.reshape(chips, 8, 256), "bucket", 0, 0, tiled=True).reshape(chips * 8, 256)
-    received, peer_ids = lax.optimization_barrier((received, peer_ids))
-
     rel_ids = span_rel.reshape(2)
+    neg_count = negatives.shape[4]
     whole = lambda shape: pl.BlockSpec(shape, lambda i, rel: (0,) * len(shape))
     relation_spec = lambda k: pl.BlockSpec((1, 8, 64, 64), lambda i, rel: (rel[k], 0, 0, 0))
-    returned = pl.pallas_call(
-        step_kernel,
-        out_shape=jax.ShapeDtypeStruct((chips * 8, 384), BF16),
+    shapes = ((8, 128), (2, 2, 256, 256), (2, 256, 256), (2, 256, 256))
+    counts = pl.pallas_call(
+        count_kernel,
+        out_shape=tuple(jax.ShapeDtypeStruct(shape, t) for shape, t in zip(shapes, (F32, BF16, F32, F32))),
         grid_spec=pltpu.PrefetchScalarGridSpec(
             num_scalar_prefetch=1,
             grid=(1,),
             in_specs=[
-                whole((chips * 8, 256)),
                 relation_spec(0),
                 relation_spec(1),
                 whole((2, heads.shape[4])),
                 whole((2, tails.shape[4])),
-                whole((2, negatives.shape[4])),
+                whole((2, neg_count)),
             ],
-            out_specs=whole((chips * 8, 384)),
-            scratch_shapes=[
-                pltpu.VMEM((2, 256, width), BF16),
-                pltpu.VMEM((2, 2, 256, 256), BF16),
-                pltpu.VMEM((2, 256, width), BF16),
-                pltpu.VMEM((2, 64, width), BF16),
-            ],
+            out_specs=tuple(whole(shape) for shape in shapes),
         ),
+        compiler_params=limit(16),
+        cost_estimate=pl.CostEstimate(flops=1 << 28, bytes_accessed=4 << 20, transcendentals=0),
+        name="count_edges",
+    )(rel_ids, relations, relations, heads.reshape(2, -1), tails.reshape(2, -1), negatives.reshape(2, -1))
+
+    received, peer_ids, *counts = lax.optimization_barrier((received, peer_ids, *counts))
+    returned = pl.pallas_call(
+        functools.partial(step_kernel, neg_count),
+        out_shape=jax.ShapeDtypeStruct((chips * 8, 384), BF16),
+        in_specs=[VMEM] * 5,
+        out_specs=VMEM,
+        scratch_shapes=[
+            pltpu.VMEM((2, 256, width), BF16),
+            pltpu.VMEM((2, 256, width), BF16),
+            pltpu.VMEM((2, 64, width), BF16),
+        ],
         compiler_params=limit(24),
         name="train_step",
-    )(
-        rel_ids,
-        received,
-        relations,
-        relations,
-        heads.reshape(2, -1),
-        tails.reshape(2, -1),
-        negatives.reshape(2, -1),
-    )
+    )(received, *counts)
 
     own = lax.all_to_all(returned.reshape(chips, 8, 384), "bucket", 0, 0, tiled=True).reshape(chips * 8, 384)
 
@@ -300,7 +375,8 @@
         name="sum_relations",
     )(rep, own)
     sums = (keep + lax.ppermute(give, "rep", swap)).astype(BF16)
-    gathered = gather_among(gather_among(sums, ALONG_Z), IN_PLANE)
+    column = gather_among(sums, ACROSS_YZ)
+    pieces = [column] + [lax.ppermute(column, "bucket", along_x(step)) for step in (1, 2, 3)]
 
     peer = lax.ppermute(own, "rep", swap)
     chunk = 256
@@ -318,20 +394,12 @@
         name="scatter_rows",
     )(own, peer, ids, peer_ids)
 
-    gathered, entity_grad = lax.optimization_barrier((gathered, entity_grad))
-    peer_gathered = lax.ppermute(gathered, "rep", swap)
-    relation_grad = pl.pallas_call(
-        assemble_kernel,
-        out_shape=jax.ShapeDtypeStruct(relations.shape, F32),
-        grid_spec=pltpu.PrefetchScalarGridSpec(
-            num_scalar_prefetch=1,
-            grid=(1,),
-            in_specs=[pl.BlockSpec((chips * 16, 128), lambda i, rep: (0, 0))] * 2,
-            out_specs=pl.BlockSpec(relations.shape, lambda i, rep: (0, 0, 0, 0)),
-        ),
-        compiler_params=limit(24),
-        name="assemble_relations",
-    )(rep, gathered, peer_gathered)
+    *pieces, entity_grad = lax.optimization_barrier((*pieces, entity_grad))
+    peer_pieces = [lax.ppermute(piece, "rep", swap) for piece in pieces]
+    x = lax.axis_index("bucket").astype(jnp.int32).reshape(1) & 3
+    relation_grad = assemble(jnp.concatenate([x, rep]), pieces, None)
+    relation_grad = assemble(jnp.concatenate([x, 1 - rep]), peer_pieces, relation_grad)
+    relation_grad = relation_grad.reshape(relations.shape)
     return entity_grad, relation_grad
 
 

time: 109 us -> 107 us (0.982)
  waiting for transfers between devices: 24.5 us -> 14.1 us
  Pallas kernels: 12 us -> 17.5 us
  blocking collectives: 38.7 us -> 41.6 us
    all_to_all x1 -> x0, waiting for transfers between devices: 6.56 us -> none  [gather_among(): lax.all_to_all(spread, 'bucket', 0, 0, axis_index_groups=groups, tiled=True)]
    all_to_all x1, waiting for transfers between devices: 15 us -> 10.9 us  [body(): lax.all_to_all(packed.reshape(chips, 8, 256), 'bucket', 0, 0, tiled=True)]
    pallas_call x2 -> x4, Pallas kernels: 5.95 us -> 9.7 us  [the longest x2 6.35 us: assemble(): pl.pallas_call(assemble_kernel, out_shape=jax.ShapeDtypeStruct(view, F32)...]
    ppermute x1 -> x7, starting transfers between devices: 2.47 us -> 6.17 us  [the longest x4 4.04 us: body(): peer_pieces = [lax.ppermute(piece, 'rep', swap) for piece in pieces]]
    all_to_all x1 -> x0, starting transfers between devices: 3.57 us -> none  [gather_among(): lax.all_to_all(spread, 'bucket', 0, 0, axis_index_groups=groups, tiled=True)]
    all_to_all x1, blocking collectives: 10.3 us -> 13.2 us  [gather_among(): lax.all_to_all(spread, 'bucket', 0, 0, axis_index_groups=groups, tiled=True)]
    pallas_call x1, Pallas kernels: 2.05 us -> 3.81 us  [body(): pl.pallas_call(send_kernel, out_shape=(jax.ShapeDtypeStruct((chips * 8, 2...]
    unnamed x14 -> x8, local copies, waits for them, and re-layouts: 3.45 us -> 3.66 us
  transfers between devices with their start and end apart: 6 -> 11, of which waited for: 5 -> 4; matrix products, arithmetic and copies ran while one was open for 1% -> 1% of each run, Pallas kernels for 4% -> 8%
where the time goes in v3:
time: 107 us; the launch traced here: 106 us
  blocking collectives  41.6 us (39%)
  starting transfers between devices  28.7 us (27%)
  Pallas kernels  17.5 us (16%)
  waiting for transfers between devices  14.1 us (13%)
  local copies, waits for them, and re-layouts  3.68 us (3%)
    all_to_all x1, blocking collectives, body(): lax.all_to_all(returned.reshape(chips, 8, 384), 'bucket', 0, 0, tiled=True)  28.4 us
    all_to_all x1, starting transfers between devices, body(): lax.all_to_all(packed.reshape(chips, 8, 256), 'bucket', 0, 0, tiled=True)  16.3 us
    all_to_all x1, blocking collectives, gather_among(): lax.all_to_all(spread, 'bucket', 0, 0, axis_index_groups=groups, tiled=True)  13.2 us
    all_to_all x1, waiting for transfers between devices, body(): lax.all_to_all(packed.reshape(chips, 8, 256), 'bucket', 0, 0, tiled=True)  10.9 us
    pallas_call x2, Pallas kernels, assemble(): pl.pallas_call(assemble_kernel, out_shape=jax.ShapeDtypeStruct(view, F32)...  6.35 us
    ppermute x1, starting transfers between devices, body(): peer = lax.ppermute(own, 'rep', swap)  5.03 us
    ppermute x4, starting transfers between devices, body(): peer_pieces = [lax.ppermute(piece, 'rep', swap) for piece in pieces]  4.04 us
    pallas_call x1, Pallas kernels, body(): pl.pallas_call(send_kernel, out_shape=(jax.ShapeDtypeStruct((chips * 8, 2...  3.81 us
  transfers between devices with their start and end apart: 11, of which 4 were waited for; matrix products, arithmetic and copies ran while one was open for 1% of the time, Pallas kernels for 8%

profile of v3, /device:TPU:1, one launch (start us, length us, event | category | flops | bytes accessed | tf_op | source)
XLA Modules:
  0.0 106.4 jit_solution(7129308230963812542)
XLA Ops:
  0.6 3.8 %send_rows.1 = (bf16[1024,256]{1,0:T(8,128)(2,1)}, f32[8,256]{1,0:T(8,128)}) custom-call(s32[2,256]{1,0:T(2,128)} %bitcast.32, s32[2,128]{1,0:T(2,128)} %bitcast.33, bf16[1024,512]{1,0:T(8,128)(2,1)} %table_ref.1), custom_call_target="tpu_custom_call" | custom-call | tf_op jit(solution)/shard_map/send_rows/pallas_call | solution.py:301
  4.4 16.3 %all-to-all-start = ((bf16[128,8,256]{2,1,0:T(8,128)(2,1)}), bf16[128,8,256]{2,1,0:T(8,128)(2,1)S(1)}, u32[]{:S(2)}, u32[]{:S(2)}) async-start(bf16[128,8,256]{2,1,0:T(8,128)(2,1)} %bitcast.31), calls=%async_computation | async-start | bytes 1048576 | tf_op jit(solution)/shard_map/all_to_all | solution.py:320
  20.8 1.0 collective-permute-start
  21.8 0.7 copy.17
  22.5 0.7 copy_bitcast_fusion.1
  23.3 1.6 %copy-done = bf16[16,8,64,64]{3,2,1,0:T(8,128)(2,1)S(1)} copy-done((bf16[16,8,64,64]{3,2,1,0:T(8,128)(2,1)S(1)}, bf16[16,8,64,64]{3,2,1,0:T(8,128)(2,1)}, u32[]{:S(2)}) %copy-start) | copy-done | bytes 1048600
  24.8 0.7 copy-done.1
  25.5 1.3 %count_edges.1 = (f32[8,128]{1,0:T(8,128)S(1)}, bf16[2,2,256,256]{3,2,1,0:T(8,128)(2,1)S(1)}, f32[2,256,256]{2,1,0:T(8,128)S(1)}, f32[2,256,256]{2,1,0:T(8,128)S(1)}) custom-call(s32[2]{0:T(128)S(1)} %bitcast.29, bf16[16,8,64,64]{3,2,1,0:T(8,128)(2,1)S(1)} %copy-done, bf16[16,8,64,64]{3,2,1,0:T(8,128)(2,1)S(1)} %copy-done, ...), custom_call_target="tpu_custom_call" | custom-call | flops 268435456 | bytes 4194304 | tf_op jit(solution)/shard_map/count_edges/pallas_call | solution.py:326
  26.8 10.9 %all-to-all-done = bf16[128,8,256]{2,1,0:T(8,128)(2,1)S(1)} async-done(((bf16[128,8,256]{2,1,0:T(8,128)(2,1)}), bf16[128,8,256]{2,1,0:T(8,128)(2,1)S(1)}, u32[]{:S(2)}, u32[]{:S(2)}) %all-to-all-start) | async-done | bytes 524320 | tf_op jit(solution)/shard_map/all_to_all | solution.py:320
  37.7 2.1 %train_step.1 = bf16[1024,384]{1,0:T(8,128)(2,1)S(1)} custom-call(bf16[1024,256]{1,0:T(8,128)(2,1)S(1)} %bitcast.22, f32[8,128]{1,0:T(8,128)S(1)} %get-tuple-element.28.names, bf16[2,2,256,256]{3,2,1,0:T(8,128)(2,1)S(1)} %get-tuple-element.29.diag, f32[2,256,256]{2,1,0:T(8,128)S(1)} %get-tuple-element.30.edges, f32[2,256,256]{2,1,0:T(8,128)S(1)} %get-tuple-element.31.pairs), custom_call_target="tpu_custom_call" | custom-call | tf_op jit(solution)/shard_map/train_step/pallas_call | solution.py:347
  39.7 28.4 %all_to_all.15 = bf16[128,8,384]{2,1,0:T(8,128)(2,1)S(1)} all-to-all(bf16[128,8,384]{2,1,0:T(8,128)(2,1)S(1)} %bitcast.21), channel_id=1, replica_groups=mesh['bucket'=128,'rep'=2] {'bucket'}, dimensions={0} | all-to-all | bytes 1572864 | tf_op jit(solution)/shard_map/all_to_all | solution.py:361
  68.2 5.0 %collective-permute-start.5 = (bf16[1024,384]{1,0:T(8,128)(2,1)S(1)}, bf16[1024,384]{1,0:T(8,128)(2,1)S(1)}, u32[]{:S(2)}, u32[]{:S(2)}) collective-permute-start(bf16[1024,384]{1,0:T(8,128)(2,1)S(1)} %bitcast.18), channel_id=1, source_target_pairs={{0,1},{1,0},{2,3},{3,2},{4,5},{5,4},{6,7},{7,6},{8,9},{9,8},{10,11... | collective-permute-start | bytes 2359304 | tf_op jit(solution)/shard_map/ppermute | solution.py:381
  73.2 0.5 sum_relations.1
  73.8 1.3 %collective-permute-done.1 = f32[16,128]{1,0:T(8,128)S(1)} collective-permute-done((f32[16,128]{1,0:T(8,128)S(1)}, f32[16,128]{1,0:T(8,128)S(1)}, u32[]{:S(2)}, u32[]{:S(2)}) %collective-permute-start.1) | collective-permute-done | bytes 8224 | tf_op jit(solution)/shard_map/ppermute | solution.py:377
  75.1 13.2 %all_to_all.16 = bf16[32,16,128]{2,1,0:T(8,128)(2,1)S(1)} all-to-all(bf16[32,16,128]{2,1,0:T(8,128)(2,1)S(1)} %broadcast_in_dim.2), channel_id=1, replica_groups={{0,8,16,24,32,40,48,56,64,72,80,88,96,104,112,120,128,136,144,152,160,1..., dimensions={0} | all-to-all | bytes 262144 | tf_op jit(solution)/shard_map/all_to_all | solution.py:260
  88.3 0.8 collective-permute-start.4
  89.1 1.3 %collective-permute-start.3 = (bf16[512,128]{1,0:T(8,128)(2,1)S(1)}, bf16[512,128]{1,0:T(8,128)(2,1)S(1)}, u32[]{:S(2)}, u32[]{:S(2)}) collective-permute-start(bf16[512,128]{1,0:T(8,128)(2,1)S(1)} %bitcast.24), channel_id=1, source_target_pairs={{0,4},{2,6},{4,0},{6,2},{8,12},{10,14},{12,8},{14,10},{16,20},{18,... | collective-permute-start | bytes 393224 | tf_op jit(solution)/shard_map/ppermute | solution.py:379
  90.5 3.5 %scatter_rows.1 = f32[1024,512]{1,0:T(8,128)} custom-call(bf16[1024,384]{1,0:T(8,128)(2,1)S(1)} %bitcast.20, bf16[1024,384]{1,0:T(8,128)(2,1)S(1)} %collective-permute-done.5.peer_ref, f32[8,256]{1,0:T(8,128)S(1)} %copy-done.2, f32[8,256]{1,0:T(8,128)S(1)} %collective-permute-done.peer_ids), custom_call_target="tpu_custom_call" | custom-call | flops 1073741824 | bytes 16777216 | tf_op jit(solution)/shard_map/scatter_rows/pallas_call | solution.py:385
  93.9 0.6 collective-permute-done.3.refs_2_
  94.5 1.4 %collective-permute-done.2.refs_1_ = bf16[512,128]{1,0:T(8,128)(2,1)S(1)} collective-permute-done((bf16[512,128]{1,0:T(8,128)(2,1)S(1)}, bf16[512,128]{1,0:T(8,128)(2,1)S(1)}, u32[]{:S(2)}, u32[]{:S(2)}) %collective-permute-start.2) | collective-permute-done | bytes 131104 | tf_op jit(solution)/shard_map/ppermute | solution.py:379
  95.9 3.5 %collective-permute-start.6 = (bf16[512,128]{1,0:T(8,128)(2,1)S(1)}, bf16[512,128]{1,0:T(8,128)(2,1)S(1)}, u32[]{:S(2)}, u32[]{:S(2)}) collective-permute-start(bf16[512,128]{1,0:T(8,128)(2,1)S(1)} %bitcast.26), channel_id=1, source_target_pairs={{0,1},{1,0},{2,3},{3,2},{4,5},{5,4},{6,7},{7,6},{8,9},{9,8},{10,11... | collective-permute-start | bytes 393224 | tf_op jit(solution)/shard_map/ppermute | solution.py:398
  99.4 0.5 collective-permute-start.8
  100.0 3.2 %assemble_relations.2.refs_4_ = f32[16,2,2,2,4,2,8,64]{7,6,5,4,3,2,1,0:T(8,128)} custom-call(s32[2]{0:T(128)S(1)} %get-tuple-element.43.place_ref, bf16[512,128]{1,0:T(8,128)(2,1)S(1)} %bitcast.27, bf16[512,128]{1,0:T(8,128)(2,1)S(1)} %collective-permute-done.2.refs_1_, bf16[512,128]{1,0:T(8,128)(2,1)S(1)} %collective-permute-done.3.refs_2_, ...), custom_call_target="tpu_custom_call" | custom-call | flops 134217728 | bytes 3145728 | tf_op jit(solution)/shard_map/assemble_relations/pallas_call | solution.py:275
  103.2 3.2 %assemble_relations.3 = f32[16,2,2,2,4,2,8,64]{7,6,5,4,3,2,1,0:T(8,128)} custom-call(s32[2]{0:T(128)S(1)} %get-tuple-element.42.place_ref, bf16[512,128]{1,0:T(8,128)(2,1)S(1)} %collective-permute-done.6.refs_0_, bf16[512,128]{1,0:T(8,128)(2,1)S(1)} %collective-permute-done.7.refs_1_, ...), custom_call_target="tpu_custom_call", output_to_operand_aliasing={{}: (5, {})} | custom-call | flops 134217728 | bytes 3145728 | tf_op jit(solution)/shard_map/assemble_relations/pallas_call | solution.py:275
  (18 shorter events, 0.2 us)
Async XLA Ops:
  4.4 33.2 %all-to-all-start = ((bf16[128,8,256]{2,1,0:T(8,128)(2,1)}), bf16[128,8,256]{2,1,0:T(8,128)(2,1)S(1)}, u32[]{:S(2)}, u32[]{:S(2)}) async-start(bf16[128,8,256]{2,1,0:T(8,128)(2,1)} %bitcast.31), calls=%async_computation | async-start | bytes 1048576 | tf_op jit(solution)/shard_map/all_to_all | solution.py:320
  20.8 6.0 %collective-permute-start = (f32[8,256]{1,0:T(8,128)}, f32[8,256]{1,0:T(8,128)S(1)}, u32[]{:S(2)}, u32[]{:S(2)}) collective-permute-start(f32[8,256]{1,0:T(8,128)} %get-tuple-element.22.own_ids), channel_id=1, source_target_pairs={{0,1},{1,0},{2,3},{3,2},{4,5},{5,4},{6,7},{7,6},{8,9},{9,8},{10,11... | collective-permute-start | bytes 24584 | tf_op jit(solution)/shard_map/ppermute | solution.py:318
  23.3 1.6 %copy-start = (bf16[16,8,64,64]{3,2,1,0:T(8,128)(2,1)S(1)}, bf16[16,8,64,64]{3,2,1,0:T(8,128)(2,1)}, u32[]{:S(2)}) copy-start(bf16[16,8,64,64]{3,2,1,0:T(8,128)(2,1)} %second_ref.1) | copy-start | bytes 3145732
  24.8 0.7 copy-start.1
  25.5 65.0 %copy-start.2 = (f32[8,256]{1,0:T(8,128)S(1)}, f32[8,256]{1,0:T(8,128)}, u32[]{:S(2)}) copy-start(f32[8,256]{1,0:T(8,128)} %get-tuple-element.22.own_ids) | copy-start | bytes 24580
  68.2 22.3 %collective-permute-start.5 = (bf16[1024,384]{1,0:T(8,128)(2,1)S(1)}, bf16[1024,384]{1,0:T(8,128)(2,1)S(1)}, u32[]{:S(2)}, u32[]{:S(2)}) collective-permute-start(bf16[1024,384]{1,0:T(8,128)(2,1)S(1)} %bitcast.18), channel_id=1, source_target_pairs={{0,1},{1,0},{2,3},{3,2},{4,5},{5,4},{6,7},{7,6},{8,9},{9,8},{10,11... | collective-permute-start | bytes 2359304 | tf_op jit(solution)/shard_map/ppermute | solution.py:381
  73.7 1.4 %collective-permute-start.1 = (f32[16,128]{1,0:T(8,128)S(1)}, f32[16,128]{1,0:T(8,128)S(1)}, u32[]{:S(2)}, u32[]{:S(2)}) collective-permute-start(f32[16,128]{1,0:T(8,128)S(1)} %get-tuple-element.33), channel_id=1, source_target_pairs={{0,1},{1,0},{2,3},{3,2},{4,5},{5,4},{6,7},{7,6},{8,9},{9,8},{10,11... | collective-permute-start | bytes 24584 | tf_op jit(solution)/shard_map/ppermute | solution.py:377
  88.3 5.6 %collective-permute-start.4 = (bf16[512,128]{1,0:T(8,128)(2,1)S(1)}, bf16[512,128]{1,0:T(8,128)(2,1)S(1)}, u32[]{:S(2)}, u32[]{:S(2)}) collective-permute-start(bf16[512,128]{1,0:T(8,128)(2,1)S(1)} %bitcast.23), channel_id=1, source_target_pairs={{0,6},{2,0},{4,2},{6,4},{8,14},{10,8},{12,10},{14,12},{16,22},{18,... | collective-permute-start | bytes 393224 | tf_op jit(solution)/shard_map/ppermute | solution.py:379
  89.1 5.4 %collective-permute-start.3 = (bf16[512,128]{1,0:T(8,128)(2,1)S(1)}, bf16[512,128]{1,0:T(8,128)(2,1)S(1)}, u32[]{:S(2)}, u32[]{:S(2)}) collective-permute-start(bf16[512,128]{1,0:T(8,128)(2,1)S(1)} %bitcast.24), channel_id=1, source_target_pairs={{0,4},{2,6},{4,0},{6,2},{8,12},{10,14},{12,8},{14,10},{16,20},{18,... | collective-permute-start | bytes 393224 | tf_op jit(solution)/shard_map/ppermute | solution.py:379
  90.5 5.4 %collective-permute-start.2 = (bf16[512,128]{1,0:T(8,128)(2,1)S(1)}, bf16[512,128]{1,0:T(8,128)(2,1)S(1)}, u32[]{:S(2)}, u32[]{:S(2)}) collective-permute-start(bf16[512,128]{1,0:T(8,128)(2,1)S(1)} %bitcast.25), channel_id=1, source_target_pairs={{0,2},{2,4},{4,6},{6,0},{8,10},{10,12},{12,14},{14,8},{16,18},{18,... | collective-permute-start | bytes 393224 | tf_op jit(solution)/shard_map/ppermute | solution.py:379
  95.9 7.3 %collective-permute-start.6 = (bf16[512,128]{1,0:T(8,128)(2,1)S(1)}, bf16[512,128]{1,0:T(8,128)(2,1)S(1)}, u32[]{:S(2)}, u32[]{:S(2)}) collective-permute-start(bf16[512,128]{1,0:T(8,128)(2,1)S(1)} %bitcast.26), channel_id=1, source_target_pairs={{0,1},{1,0},{2,3},{3,2},{4,5},{5,4},{6,7},{7,6},{8,9},{9,8},{10,11... | collective-permute-start | bytes 393224 | tf_op jit(solution)/shard_map/ppermute | solution.py:398
  99.4 3.8 %collective-permute-start.7 = (bf16[512,128]{1,0:T(8,128)(2,1)S(1)}, bf16[512,128]{1,0:T(8,128)(2,1)S(1)}, u32[]{:S(2)}, u32[]{:S(2)}) collective-permute-start(bf16[512,128]{1,0:T(8,128)(2,1)S(1)} %collective-permute-done.2.refs_1_), channel_id=1, source_target_pairs={{0,1},{1,0},{2,3},{3,2},{4,5},{5,4},{6,7},{7,6},{8,9},{9,8},{10,11... | collective-permute-start | bytes 393224 | tf_op jit(solution)/shard_map/ppermute | solution.py:398
  99.4 3.8 %collective-permute-start.8 = (bf16[512,128]{1,0:T(8,128)(2,1)S(1)}, bf16[512,128]{1,0:T(8,128)(2,1)S(1)}, u32[]{:S(2)}, u32[]{:S(2)}) collective-permute-start(bf16[512,128]{1,0:T(8,128)(2,1)S(1)} %collective-permute-done.3.refs_2_), channel_id=1, source_target_pairs={{0,1},{1,0},{2,3},{3,2},{4,5},{5,4},{6,7},{7,6},{8,9},{9,8},{10,11... | collective-permute-start | bytes 393224 | tf_op jit(solution)/shard_map/ppermute | solution.py:398
  99.9 3.3 %collective-permute-start.9 = (bf16[512,128]{1,0:T(8,128)(2,1)S(1)}, bf16[512,128]{1,0:T(8,128)(2,1)S(1)}, u32[]{:S(2)}, u32[]{:S(2)}) collective-permute-start(bf16[512,128]{1,0:T(8,128)(2,1)S(1)} %collective-permute-done.4.refs_3_), channel_id=1, source_target_pairs={{0,1},{1,0},{2,3},{3,2},{4,5},{5,4},{6,7},{7,6},{8,9},{9,8},{10,11... | collective-permute-start | bytes 393224 | tf_op jit(solution)/shard_map/ppermute | solution.py:398

commit v4 on v3

--- a/solution.py
+++ b/solution.py
@@ -81,66 +81,65 @@
 
     for n in range(4):
         fetch(n).start()
-    row = iota((256, 128), 0)
+    row = iota((512, 128), 0) & 255
     dest = (row >> 6) * 32 + (row & 31)
-    other = iota((256, 128), 1)
-    column = (iota((256, 1), 0) >> 5) & 1
-    flat = iota((256, 256), 1)
-    entity = iota((256, part), 1)
-    ids_ref[...] = jnp.zeros_like(ids_ref)
-    wanted = []
+    other = iota((512, 128), 1)
+    column = (iota((512, 1), 0) >> 5) & 1
     for copy in lists:
         copy.wait()
-    for k in range(2):
-        counts = count_ref[k : k + 1, :].astype(F32)
-        start = jnp.sum(jnp.where(other < dest, counts, 0.0), axis=1, keepdims=True)
-        count = jnp.sum(jnp.where(other == dest, counts, 0.0), axis=1, keepdims=True)
-        position = start.astype(jnp.int32) + column
-        names = rows_ref[k : k + 1, :].astype(F32)
-        ids = jnp.sum(jnp.where(flat == position, names, 0.0), axis=1, keepdims=True)
-        ids = jnp.where(column < count.astype(jnp.int32), ids, -1.0)
-        ids_ref[k : k + 1, :] = jnp.transpose(jnp.broadcast_to(ids, (256, 128)))[0:1, :]
-        wanted.append(ids.astype(jnp.int32))
-    totals = [jnp.zeros(slots.shape[1:], F32) for k in range(2)]
+
+    def both(ref):
+        values = ref[...].astype(F32)
+        return jnp.concatenate(
+            [jnp.broadcast_to(values[k : k + 1], (256, values.shape[1])) for k in range(2)], axis=0
+        )
+
+    counts = both(count_ref)
+    start = jnp.sum(jnp.where(other < dest, counts, 0.0), axis=1, keepdims=True)
+    count = jnp.sum(jnp.where(other == dest, counts, 0.0), axis=1, keepdims=True)
+    position = start.astype(jnp.int32) + column
+    ids = jnp.sum(jnp.where(iota((512, 256), 1) == position, both(rows_ref), 0.0), axis=1, keepdims=True)
+    ids = jnp.where(column < count.astype(jnp.int32), ids, -1.0)
+    wanted = ids.astype(jnp.int32)
+    entity = iota((512, part), 1)
+    total = jnp.zeros((512, table.shape[1]), F32)
     for n in range(4):
         fetch(n).wait()
-        rows = table[n * part : n * part + part, :]
-        for k in range(2):
-            totals[k] = totals[k] + dot(onehot(entity + n * part == wanted[k]), rows)
+        total = total + dot(onehot(entity + n * part == wanted), table[n * part : n * part + part, :])
+    slots[...] = total.astype(BF16)
+    ids_ref[...] = jnp.zeros_like(ids_ref)
     for k in range(2):
-        slots[k] = totals[k].astype(BF16)
+        spread = jnp.broadcast_to(ids[k * 256 : k * 256 + 256], (256, 128))
+        ids_ref[k : k + 1, :] = jnp.transpose(spread)[0:1, :]
 
     def write(b, rows):
         packed[b * 256 : b * 256 + 256, :] = rows
         send(b).start()
 
-    pack_slots(lambda k, b: slots[k, b * 64 : b * 64 + 64, :], write)
+    pack_slots(lambda k, b: slots[k * 256 + b * 64 : k * 256 + b * 64 + 64, :], write)
     for b in range(4):
         send(b).wait()
 
 
-def count_kernel(rel_ref, first_ref, second_ref, heads_ref, tails_ref, neg_ref, names_ref, diag_ref, edges_ref, pairs_ref):
+def count_kernel(rel_ref, relation_ref, heads_ref, tails_ref, neg_ref, names_ref, diag_ref, edges_ref, times_ref):
     neg_count = neg_ref.shape[1]
     names_ref[...] = jnp.where(iota((8, 128), 0) == 0, rel_ref[0], rel_ref[1]).astype(F32)
     for k in range(2):
-        relation = (first_ref, second_ref)[k]
         for c in range(2):
             for j in range(4):
                 place = onehot(iota((64, 256), 1) == iota((64, 256), 0) + 64 * j)
-                diag_ref[k, c, 64 * j : 64 * j + 64, :] = dot(relation[0, 4 * c + j], place).astype(BF16)
+                diag_ref[k, c, 64 * j : 64 * j + 64, :] = dot(relation_ref[k, 4 * c + j], place).astype(BF16)
         slot = iota((256, heads_ref.shape[1]), 0)
         at_head = onehot(slot == slot_row(heads_ref[k : k + 1, :]))
         at_tail = onehot(slot == slot_row(tails_ref[k : k + 1, :]))
         edges = dot(at_head, at_tail, 1, 1)
-        head_edges = jnp.sum(edges, axis=1, keepdims=True)
         at_neg = onehot(iota((256, neg_count), 0) == slot_row(neg_ref[k : k + 1, :]))
-        times = dot(jnp.ones((8, neg_count), BF16), at_neg, 1, 1)[0:1, :]
         edges_ref[k] = edges
-        pairs_ref[k] = head_edges * times
+        times_ref[k] = dot(jnp.ones((8, neg_count), BF16), at_neg, 1, 1)
 
 
 def step_kernel(
-    neg_count, packed_ref, names, diag, edges, pairs, out_ref, slots, grads, partial
+    neg_count, packed_ref, names, diag, edges, times, out_ref, slots, grads, partial
 ):
     def write(k, b, h, rows):
         slots[k, b * 64 : b * 64 + 64, h * 256 : h * 256 + 256] = rows
@@ -158,7 +157,8 @@
         small_side = small * big_side
         sigmoid = jnp.where(score >= 0, big_side, small_side)
         sigmoid_neg = jnp.where(score >= 0, small_side, big_side)
-        weight = (pairs[k] * sigmoid / neg_count - edges[k] * sigmoid_neg).astype(BF16)
+        pairs = jnp.sum(edges[k], axis=1, keepdims=True) * times[k][0:1, :]
+        weight = (pairs * sigmoid / neg_count - edges[k] * sigmoid_neg).astype(BF16)
         grad_rotated = dot(weight, rows).astype(BF16)
         grad_other = dot(weight, rotated, 0, 0)
         for c in range(2):
@@ -169,20 +169,26 @@
             total = jnp.zeros((64, 256), F32)
             for j in range(4):
                 total = jnp.where(lane_block == j, outer[64 * j : 64 * j + 64, :], total)
-            partial[k, :, lanes] = total.astype(BF16)
+            partial[k, :, lanes] = total
 
     p = iota((256, 128), 0)
     g = iota((256, 128), 1)
     piece = p & 3
-    source = ((p >> 2) & 1) * 64 + (((p >> 3) & 1) * 2 + piece) * 16 + ((p >> 4) & 1) * 8 + (p >> 5)
+    source = ((p >> 2) & 1) * 64 + piece * 32 + ((p >> 3) & 3) * 8 + (p >> 5)
     spread = onehot((g == source) & (piece < 2))
     named = jnp.where(((p >> 2) & 1) == 0, names[0:1, :], names[1:2, :])
 
     def write_packed(b, rows):
         out_ref[b * 256 : b * 256 + 256, 0:256] = rows
         rows = jnp.concatenate(
-            [partial[k, b * 16 : b * 16 + 16, q * 128 : q * 128 + 128] for k in range(2) for q in range(4)], axis=0
-        )
+            [
+                partial[k, q * 32 + b * 8 : q * 32 + b * 8 + 8, x * 128 : x * 128 + 128]
+                for k in range(2)
+                for q in range(2)
+                for x in range(4)
+            ],
+            axis=0,
+        ).astype(BF16)
         out_ref[b * 256 : b * 256 + 256, 256:384] = jnp.where(piece == 2, named, dot(spread, rows)).astype(BF16)
 
     pack_slots(lambda k, b: grads[k, b * 64 : b * 64 + 64, :], write_packed)
@@ -228,19 +234,43 @@
     out_ref[...] = total
 
 
-def assemble_kernel(place_ref, *refs):
-    pieces, out_ref = refs[:4], refs[-1]
+def order_kernel(rows_ref, out_ref):
     g = iota((256, 256), 0)
     p = iota((256, 256), 1)
     matrix = onehot(p == (g & 15) * 16 + (g >> 4))
-    for shift in range(4):
-
-        @pl.when(pl.program_id(0) == shift)
-        def _():
-            for y in range(2):
-                rows = dot(matrix, pieces[shift][y * 256 : y * 256 + 256, :]).reshape(16, 2, 8, 128)
-                for side in range(2):
-                    out_ref[:, 0, 0, side, 2 * y : 2 * y + 2, 0] = rows[:, :, :, 64 * side : 64 * side + 64]
+    for y in range(2):
+        out_ref[y * 256 : y * 256 + 256, :] = dot(matrix, rows_ref[y * 256 : y * 256 + 256, :]).astype(BF16)
+
+
+def widen(piece, result):
+    for y in range(2):
+        rows = piece[y * 256 : y * 256 + 256, :].astype(F32).reshape(16, 16, 128)
+        for side in range(2):
+            result[:, side, y * 16 : y * 16 + 16] = rows[:, :, 64 * side : 64 * side + 64]
+
+
+def widen_kernel(*refs):
+    for n, piece in enumerate(refs[:-1]):
+        widen(piece, refs[-1].at[n])
+
+
+def lay_out_kernel(count, ready, xs_ref, qs_ref, *refs):
+    pieces = refs[:count]
+    out_ref, result, sem = refs[-3:]
+    copies = []
+
+    def send(n, source):
+        copy = pltpu.make_async_copy(source, out_ref.at[:, xs_ref[n], :, qs_ref[n]], sem.at[n])
+        copy.start()
+        copies.append(copy)
+
+    for n in range(ready):
+        send(count + n, refs[count].at[n])
+    for n in range(count):
+        widen(pieces[n], result.at[n])
+        send(n, result.at[n])
+    for copy in copies:
+        copy.wait()
 
 
 def chip(y, z, x):
@@ -261,31 +291,27 @@
     return out.reshape(count * rows.shape[0], rows.shape[1])
 
 
-def assemble(place, pieces, into):
-    view = (16, 2, 2, 2, 4, 2, 8, 64)
-
-    def where(shift, place):
-        x = (place[0] - shift) & 3
-        return (0, x & 1, place[1], 0, 0, x >> 1, 0, 0)
-
-    arrays = list(pieces) + ([] if into is None else [into])
-    specs = [pl.BlockSpec(pieces[0].shape, lambda shift, place: (0, 0))] * 4
-    if into is not None:
-        specs.append(pl.BlockSpec(memory_space=pl.ANY))
+WIDE = (16, 2, 32, 64)
+
+
+def lay_out(pieces, wide, xs, qs, into):
+    view = (16, 4, 2, 2, 32, 64)
+    count = len(pieces)
+    ready = 0 if wide is None else wide.shape[0]
+    arrays = list(pieces) + ([] if wide is None else [wide])
+    earlier = [] if into is None else [into]
+    scalars = pl.BlockSpec(memory_space=pltpu.SMEM)
     return pl.pallas_call(
-        assemble_kernel,
+        functools.partial(lay_out_kernel, count, ready),
         out_shape=jax.ShapeDtypeStruct(view, F32),
-        grid_spec=pltpu.PrefetchScalarGridSpec(
-            num_scalar_prefetch=1,
-            grid=(4,),
-            in_specs=specs,
-            out_specs=pl.BlockSpec((16, 1, 1, 2, 4, 1, 8, 64), where),
-        ),
-        input_output_aliases={} if into is None else {5: 0},
+        in_specs=[scalars] * 2 + [VMEM] * len(arrays) + [HBM] * len(earlier),
+        out_specs=HBM,
+        scratch_shapes=[pltpu.VMEM((count,) + WIDE, F32), pltpu.SemaphoreType.DMA((count + ready,))],
+        input_output_aliases={2 + len(arrays): 0} if earlier else {},
         compiler_params=limit(8),
-        cost_estimate=pl.CostEstimate(flops=1 << 27, bytes_accessed=3 << 20, transcendentals=0),
-        name="assemble_relations",
-    )(place, *arrays)
+        cost_estimate=pl.CostEstimate(flops=1 << 20, bytes_accessed=count << 20, transcendentals=0),
+        name="lay_out_relations",
+    )(xs, qs, *arrays, *earlier)
 
 
 def limit(mib):
@@ -307,7 +333,7 @@
             pltpu.VMEM(send_rows.shape[2:], jnp.int32),
             pltpu.VMEM(send_count.shape[2:], jnp.int32),
             pltpu.VMEM((entities, width), BF16),
-            pltpu.VMEM((2, 256, width), BF16),
+            pltpu.VMEM((512, width), BF16),
             pltpu.VMEM((chips * 8, 256), BF16),
             pltpu.SemaphoreType.DMA((2,)),
             pltpu.SemaphoreType.DMA((4,)),
@@ -320,28 +346,17 @@
     received = lax.all_to_all(packed.reshape(chips, 8, 256), "bucket", 0, 0, tiled=True).reshape(chips * 8, 256)
     rel_ids = span_rel.reshape(2)
     neg_count = negatives.shape[4]
-    whole = lambda shape: pl.BlockSpec(shape, lambda i, rel: (0,) * len(shape))
-    relation_spec = lambda k: pl.BlockSpec((1, 8, 64, 64), lambda i, rel: (rel[k], 0, 0, 0))
-    shapes = ((8, 128), (2, 2, 256, 256), (2, 256, 256), (2, 256, 256))
+    used = jnp.concatenate([lax.dynamic_slice_in_dim(relations, rel_ids[k], 1) for k in range(2)])
+    shapes = ((8, 128), (2, 2, 256, 256), (2, 256, 256), (2, 8, 256))
     counts = pl.pallas_call(
         count_kernel,
         out_shape=tuple(jax.ShapeDtypeStruct(shape, t) for shape, t in zip(shapes, (F32, BF16, F32, F32))),
-        grid_spec=pltpu.PrefetchScalarGridSpec(
-            num_scalar_prefetch=1,
-            grid=(1,),
-            in_specs=[
-                relation_spec(0),
-                relation_spec(1),
-                whole((2, heads.shape[4])),
-                whole((2, tails.shape[4])),
-                whole((2, neg_count)),
-            ],
-            out_specs=tuple(whole(shape) for shape in shapes),
-        ),
+        in_specs=[pl.BlockSpec(memory_space=pltpu.SMEM)] + [VMEM] * 4,
+        out_specs=(VMEM,) * 4,
         compiler_params=limit(16),
         cost_estimate=pl.CostEstimate(flops=1 << 28, bytes_accessed=4 << 20, transcendentals=0),
         name="count_edges",
-    )(rel_ids, relations, relations, heads.reshape(2, -1), tails.reshape(2, -1), negatives.reshape(2, -1))
+    )(rel_ids, used, heads.reshape(2, -1), tails.reshape(2, -1), negatives.reshape(2, -1))
 
     received, peer_ids, *counts = lax.optimization_barrier((received, peer_ids, *counts))
     returned = pl.pallas_call(
@@ -352,7 +367,7 @@
         scratch_shapes=[
             pltpu.VMEM((2, 256, width), BF16),
             pltpu.VMEM((2, 256, width), BF16),
-            pltpu.VMEM((2, 64, width), BF16),
+            pltpu.VMEM((2, 64, width), F32),
         ],
         compiler_params=limit(24),
         name="train_step",
@@ -376,8 +391,6 @@
     )(rep, own)
     sums = (keep + lax.ppermute(give, "rep", swap)).astype(BF16)
     column = gather_among(sums, ACROSS_YZ)
-    pieces = [column] + [lax.ppermute(column, "bucket", along_x(step)) for step in (1, 2, 3)]
-
     peer = lax.ppermute(own, "rep", swap)
     chunk = 256
     rows_spec = pl.BlockSpec((chips * 8, 256), lambda i: (0, 0))
@@ -394,11 +407,37 @@
         name="scatter_rows",
     )(own, peer, ids, peer_ids)
 
-    *pieces, entity_grad = lax.optimization_barrier((*pieces, entity_grad))
-    peer_pieces = [lax.ppermute(piece, "rep", swap) for piece in pieces]
-    x = lax.axis_index("bucket").astype(jnp.int32).reshape(1) & 3
-    relation_grad = assemble(jnp.concatenate([x, rep]), pieces, None)
-    relation_grad = assemble(jnp.concatenate([x, 1 - rep]), peer_pieces, relation_grad)
+    column, entity_grad = lax.optimization_barrier((column, entity_grad))
+    column = pl.pallas_call(
+        order_kernel,
+        out_shape=jax.ShapeDtypeStruct(column.shape, BF16),
+        in_specs=[VMEM],
+        out_specs=VMEM,
+        compiler_params=limit(8),
+        name="order_column",
+    )(column)
+    pieces = [column] + [lax.ppermute(column, "bucket", along_x(step)) for step in (1, 2, 3)]
+
+    x = lax.axis_index("bucket").astype(jnp.int32) & 3
+    xs = (x - jnp.arange(4, dtype=jnp.int32)) & 3
+    own_q = jnp.broadcast_to(rep, (4,))
+    relation_grad = lay_out(pieces[:1], None, xs[:1], own_q[:1], None)
+    peer_pieces = []
+    for n in range(4):
+        pieces[n], relation_grad = lax.optimization_barrier((pieces[n], relation_grad))
+        peer_pieces.append(lax.ppermute(pieces[n], "rep", swap))
+    wide = pl.pallas_call(
+        widen_kernel,
+        out_shape=jax.ShapeDtypeStruct((3,) + WIDE, F32),
+        in_specs=[VMEM] * 3,
+        out_specs=VMEM,
+        compiler_params=limit(8),
+        cost_estimate=pl.CostEstimate(flops=1 << 20, bytes_accessed=3 << 20, transcendentals=0),
+        name="widen_own",
+    )(*pieces[1:])
+    relation_grad = lay_out(
+        peer_pieces, wide, jnp.concatenate([xs, xs[1:]]), jnp.concatenate([1 - own_q, own_q[1:]]), relation_grad
+    )
     relation_grad = relation_grad.reshape(relations.shape)
     return entity_grad, relation_grad
 

time: 107 us -> 105 us (0.981)
  blocking collectives: 41.6 us -> 28.4 us
  starting transfers between devices: 28.7 us -> 36.9 us
  between operations: 0.71 us -> 5.01 us
  Pallas kernels: 17.5 us -> 14.7 us
  waiting for transfers between devices: 14.1 us -> 16.5 us
  local copies, waits for them, and re-layouts: 3.68 us -> 2.44 us
    all_to_all x1 -> x0, blocking collectives: 13.2 us -> none  [gather_among(): lax.all_to_all(spread, 'bucket', 0, 0, axis_index_groups=groups, tiled=True)]
    all_to_all x0 -> x1, waiting for transfers between devices: none -> 5.68 us  [gather_among(): lax.all_to_all(spread, 'bucket', 0, 0, axis_index_groups=groups, tiled=True)]
    all_to_all x0 -> x1, starting transfers between devices: none -> 4.25 us  [gather_among(): lax.all_to_all(spread, 'bucket', 0, 0, axis_index_groups=groups, tiled=True)]
    unnamed x8 -> x12, local copies, waits for them, and re-layouts: 3.66 us -> 0.03 us
    ppermute x4, starting transfers between devices: 4.04 us -> 6.71 us  [body(): peer_pieces.append(lax.ppermute(pieces[n], 'rep', swap))]
    pallas_call x2 -> x4, Pallas kernels: 6.35 us -> 3.78 us  [the longest x2 3.38 us: lay_out(): pl.pallas_call(functools.partial(lay_out_kernel, count, ready), out_shape...]
    all_to_all x1, waiting for transfers between devices: 10.9 us -> 8.79 us  [body(): lax.all_to_all(packed.reshape(chips, 8, 256), 'bucket', 0, 0, tiled=True)]
    ppermute x3, waiting for transfers between devices: 1.93 us -> 0.01 us  [body(): lax.ppermute(column, 'bucket', along_x(step))]
  transfers between devices with their start and end apart: 11 -> 12, of which waited for: 4 -> 6; matrix products, arithmetic and copies ran while one was open for 1% -> 2% of each run, Pallas kernels for 8% -> 6%
where the time goes in v4:
time: 105 us; the launch traced here: 104 us
  starting transfers between devices  36.9 us (35%)
  blocking collectives  28.4 us (27%)
  waiting for transfers between devices  16.5 us (16%)
  Pallas kernels  14.7 us (14%)
  between operations  5.01 us (5%)
  local copies, waits for them, and re-layouts  2.44 us (2%)
    all_to_all x1, blocking collectives, body(): lax.all_to_all(returned.reshape(chips, 8, 384), 'bucket', 0, 0, tiled=True)  28.4 us
    all_to_all x1, starting transfers between devices, body(): lax.all_to_all(packed.reshape(chips, 8, 256), 'bucket', 0, 0, tiled=True)  16.4 us
    all_to_all x1, waiting for transfers between devices, body(): lax.all_to_all(packed.reshape(chips, 8, 256), 'bucket', 0, 0, tiled=True)  8.79 us
    ppermute x4, starting transfers between devices, body(): peer_pieces.append(lax.ppermute(pieces[n], 'rep', swap))  6.71 us
    all_to_all x1, waiting for transfers between devices, gather_among(): lax.all_to_all(spread, 'bucket', 0, 0, axis_index_groups=groups, tiled=True)  5.68 us
    ppermute x1, starting transfers between devices, body(): peer = lax.ppermute(own, 'rep', swap)  5.03 us
    all_to_all x1, starting transfers between devices, gather_among(): lax.all_to_all(spread, 'bucket', 0, 0, axis_index_groups=groups, tiled=True)  4.25 us
    pallas_call x1, Pallas kernels, body(): pl.pallas_call(send_kernel, out_shape=(jax.ShapeDtypeStruct((chips * 8, 2...  3.71 us
  transfers between devices with their start and end apart: 12, of which 6 were waited for; matrix products, arithmetic and copies ran while one was open for 2% of the time, Pallas kernels for 6%

profile of v4, /device:TPU:1, one launch (start us, length us, event | category | flops | bytes accessed | tf_op | source)
XLA Modules:
  0.0 104.2 jit_solution(6728464529143759740)
XLA Ops:
  0.7 3.7 %send_rows.1 = (bf16[1024,256]{1,0:T(8,128)(2,1)}, f32[8,256]{1,0:T(8,128)}) custom-call(s32[2,256]{1,0:T(2,128)} %bitcast.31, s32[2,128]{1,0:T(2,128)} %bitcast.32, bf16[1024,512]{1,0:T(8,128)(2,1)} %table_ref.1), custom_call_target="tpu_custom_call" | custom-call | tf_op jit(solution)/shard_map/send_rows/pallas_call | solution.py:327
  4.4 16.4 %all-to-all-start = ((bf16[128,8,256]{2,1,0:T(8,128)(2,1)}), bf16[128,8,256]{2,1,0:T(8,128)(2,1)S(1)}, u32[]{:S(2)}, u32[]{:S(2)}) async-start(bf16[128,8,256]{2,1,0:T(8,128)(2,1)} %bitcast.30), calls=%async_computation | async-start | bytes 1048576 | tf_op jit(solution)/shard_map/all_to_all | solution.py:346
  20.8 1.0 %collective-permute-start = (f32[8,256]{1,0:T(8,128)}, f32[8,256]{1,0:T(8,128)S(1)}, u32[]{:S(2)}, u32[]{:S(2)}) collective-permute-start(f32[8,256]{1,0:T(8,128)} %get-tuple-element.27.own_ids), channel_id=1, source_target_pairs={{0,1},{1,0},{2,3},{3,2},{4,5},{5,4},{6,7},{7,6},{8,9},{9,8},{10,11... | collective-permute-start | bytes 24584 | tf_op jit(solution)/shard_map/ppermute | solution.py:344
  21.8 0.7 fusion
  26.5 1.0 constant_dynamic-slice_fusion.1
  27.6 1.2 %count_edges.1 = (f32[8,128]{1,0:T(8,128)S(1)}, bf16[2,2,256,256]{3,2,1,0:T(8,128)(2,1)S(1)}, f32[2,256,256]{2,1,0:T(8,128)S(1)}, f32[2,8,256]{2,1,0:T(8,128)S(1)}) custom-call(s32[2]{0:T(128)S(1)} %bitcast.27, bf16[2,8,64,64]{3,2,1,0:T(8,128)(2,1)S(1)} %pad_maximum_fusion.relation_ref, s32[2,512]{1,0:T(2,128)S(1)} %get-tuple-element.55.heads_ref, ...), custom_call_target="tpu_custom_call" | custom-call | flops 268435456 | bytes 4194304 | tf_op jit(solution)/shard_map/count_edges/pallas_call | solution.py:351
  28.8 8.8 %all-to-all-done = bf16[128,8,256]{2,1,0:T(8,128)(2,1)S(1)} async-done(((bf16[128,8,256]{2,1,0:T(8,128)(2,1)}), bf16[128,8,256]{2,1,0:T(8,128)(2,1)S(1)}, u32[]{:S(2)}, u32[]{:S(2)}) %all-to-all-start) | async-done | bytes 524320 | tf_op jit(solution)/shard_map/all_to_all | solution.py:346
  37.6 2.1 %train_step.1 = bf16[1024,384]{1,0:T(8,128)(2,1)S(1)} custom-call(bf16[1024,256]{1,0:T(8,128)(2,1)S(1)} %bitcast.24, f32[8,128]{1,0:T(8,128)S(1)} %get-tuple-element.33.names, bf16[2,2,256,256]{3,2,1,0:T(8,128)(2,1)S(1)} %get-tuple-element.34.diag, f32[2,256,256]{2,1,0:T(8,128)S(1)} %get-tuple-element.35.edges, f32[2,8,256]{2,1,0:T(8,128)S(1)} %get-tuple-element.36.times), custom_call_target="tpu_custom_call" | custom-call | tf_op jit(solution)/shard_map/train_step/pallas_call | solution.py:362
  39.7 28.4 %all_to_all.15 = bf16[128,8,384]{2,1,0:T(8,128)(2,1)S(1)} all-to-all(bf16[128,8,384]{2,1,0:T(8,128)(2,1)S(1)} %bitcast.23), channel_id=1, replica_groups=mesh['bucket'=128,'rep'=2] {'bucket'}, dimensions={0} | all-to-all | bytes 1572864 | tf_op jit(solution)/shard_map/all_to_all | solution.py:376
  68.1 5.0 %collective-permute-start.2 = (bf16[1024,384]{1,0:T(8,128)(2,1)S(1)}, bf16[1024,384]{1,0:T(8,128)(2,1)S(1)}, u32[]{:S(2)}, u32[]{:S(2)}) collective-permute-start(bf16[1024,384]{1,0:T(8,128)(2,1)S(1)} %bitcast.20), channel_id=1, source_target_pairs={{0,1},{1,0},{2,3},{3,2},{4,5},{5,4},{6,7},{7,6},{8,9},{9,8},{10,11... | collective-permute-start | bytes 2359304 | tf_op jit(solution)/shard_map/ppermute | solution.py:394
  73.2 0.5 sum_relations.1
  73.8 1.3 %collective-permute-done.1 = f32[16,128]{1,0:T(8,128)S(1)} collective-permute-done((f32[16,128]{1,0:T(8,128)S(1)}, f32[16,128]{1,0:T(8,128)S(1)}, u32[]{:S(2)}, u32[]{:S(2)}) %collective-permute-start.1) | collective-permute-done | bytes 8224 | tf_op jit(solution)/shard_map/ppermute | solution.py:392
  75.1 0.7 broadcast_in_dim.2
  75.8 4.2 %all-to-all-start.2 = ((bf16[32,16,128]{2,1,0:T(8,128)(2,1)}), bf16[32,16,128]{2,1,0:T(8,128)(2,1)S(1)}, u32[]{:S(2)}, u32[]{:S(2)}) async-start(bf16[32,16,128]{2,1,0:T(8,128)(2,1)} %broadcast_in_dim.2), calls=%async_computation.2 | async-start | bytes 262144 | tf_op jit(solution)/shard_map/all_to_all | solution.py:290
  80.0 3.5 %scatter_rows.1 = f32[1024,512]{1,0:T(8,128)} custom-call(bf16[1024,384]{1,0:T(8,128)(2,1)S(1)} %bitcast.22, bf16[1024,384]{1,0:T(8,128)(2,1)S(1)} %collective-permute-done.2.peer_ref, f32[8,256]{1,0:T(8,128)S(1)} %copy-done.1, f32[8,256]{1,0:T(8,128)S(1)} %collective-permute-done.peer_ids), custom_call_target="tpu_custom_call" | custom-call | flops 1073741824 | bytes 16777216 | tf_op jit(solution)/shard_map/scatter_rows/pallas_call | solution.py:398
  83.5 5.7 %all-to-all-done.2 = bf16[32,16,128]{2,1,0:T(8,128)(2,1)S(1)} async-done(((bf16[32,16,128]{2,1,0:T(8,128)(2,1)}), bf16[32,16,128]{2,1,0:T(8,128)(2,1)S(1)}, u32[]{:S(2)}, u32[]{:S(2)}) %all-to-all-start.2) | async-done | bytes 131104 | tf_op jit(solution)/shard_map/all_to_all | solution.py:290
  89.4 0.4 collective-permute-start.4
  89.8 1.6 %collective-permute-start.6 = (bf16[512,128]{1,0:T(8,128)(2,1)S(1)}, bf16[512,128]{1,0:T(8,128)(2,1)S(1)}, u32[]{:S(2)}, u32[]{:S(2)}) collective-permute-start(bf16[512,128]{1,0:T(8,128)(2,1)S(1)} %order_column.1.refs_0_), channel_id=1, source_target_pairs={{0,4},{2,6},{4,0},{6,2},{8,12},{10,14},{12,8},{14,10},{16,20},{18,... | collective-permute-start | bytes 393224 | tf_op jit(solution)/shard_map/ppermute | solution.py:419
  91.5 1.4 %collective-permute-start.8 = (bf16[512,128]{1,0:T(8,128)(2,1)S(1)}, bf16[512,128]{1,0:T(8,128)(2,1)S(1)}, u32[]{:S(2)}, u32[]{:S(2)}) collective-permute-start(bf16[512,128]{1,0:T(8,128)(2,1)S(1)} %order_column.1.refs_0_), channel_id=1, source_target_pairs={{0,6},{2,0},{4,2},{6,4},{8,14},{10,8},{12,10},{14,12},{16,22},{18,... | collective-permute-start | bytes 393224 | tf_op jit(solution)/shard_map/ppermute | solution.py:419
  92.9 0.9 lay_out_relations.2.refs_5_
  93.8 3.0 %collective-permute-start.3 = (bf16[512,128]{1,0:T(8,128)(2,1)S(1)}, bf16[512,128]{1,0:T(8,128)(2,1)S(1)}, u32[]{:S(2)}, u32[]{:S(2)}) collective-permute-start(bf16[512,128]{1,0:T(8,128)(2,1)S(1)} %order_column.1.refs_0_), channel_id=1, source_target_pairs={{0,1},{1,0},{2,3},{3,2},{4,5},{5,4},{6,7},{7,6},{8,9},{9,8},{10,11... | collective-permute-start | bytes 393224 | tf_op jit(solution)/shard_map/ppermute | solution.py:428
  96.9 3.2 %collective-permute-start.9 = (bf16[512,128]{1,0:T(8,128)(2,1)S(1)}, bf16[512,128]{1,0:T(8,128)(2,1)S(1)}, u32[]{:S(2)}, u32[]{:S(2)}) collective-permute-start(bf16[512,128]{1,0:T(8,128)(2,1)S(1)} %collective-permute-done.8.refs_2_), channel_id=1, source_target_pairs={{0,1},{1,0},{2,3},{3,2},{4,5},{5,4},{6,7},{7,6},{8,9},{9,8},{10,11... | collective-permute-start | bytes 393224 | tf_op jit(solution)/shard_map/ppermute | solution.py:428
  100.0 0.5 collective-permute-start.5
  101.6 2.4 %lay_out_relations.3 = f32[16,4,2,2,32,64]{5,4,3,2,1,0:T(8,128)} custom-call(s32[7]{0:T(128)S(1)} %pad_add_fusion.xs_ref, s32[7]{0:T(128)S(1)} %concatenate.11.qs_ref, bf16[512,128]{1,0:T(8,128)(2,1)S(1)} %collective-permute-done.3.refs_0_, bf16[512,128]{1,0:T(8,128)(2,1)S(1)} %collective-permute-done.5.refs_1_, ...), custom_call_target="tpu_custom_call", output_to_operand_aliasing={{}: (7, {})} | custom-call | flops 1048576 | bytes 4194304 | tf_op jit(solution)/shard_map/lay_out_relations/pallas_call | solution.py:304
  (32 shorter events, 1.4 us)
Async XLA Ops:
  0.6 21.2 %copy-start = (s32[1,1,2,1]{2,3,1,0:T(1,128)S(1)}, s32[1,1,2,1]{2,3,1,0:T(1,128)}, u32[]{:S(2)}) copy-start(s32[1,1,2,1]{2,3,1,0:T(1,128)} %param.15) | copy-start | bytes 28
  0.6 24.5 %copy-start.2 = (s32[1,1,2,1,1000]{4,3,2,1,0:T(1,128)S(1)}, s32[1,1,2,1,1000]{4,3,2,1,0:T(1,128)}, u32[]{:S(2)}) copy-start(s32[1,1,2,1,1000]{4,3,2,1,0:T(1,128)} %param.14) | copy-start | bytes 24004
  0.7 26.9 %copy-start.3 = (s32[1,1,2,1,512]{4,3,2,1,0:T(1,128)S(1)}, s32[1,1,2,1,512]{4,3,2,1,0:T(1,128)}, u32[]{:S(2)}) copy-start(s32[1,1,2,1,512]{4,3,2,1,0:T(1,128)} %param.13) | copy-start | bytes 12292
  0.7 26.9 %copy-start.4 = (s32[1,1,2,1,512]{4,3,2,1,0:T(1,128)S(1)}, s32[1,1,2,1,512]{4,3,2,1,0:T(1,128)}, u32[]{:S(2)}) copy-start(s32[1,1,2,1,512]{4,3,2,1,0:T(1,128)} %param.12) | copy-start | bytes 12292
  4.4 33.2 %all-to-all-start = ((bf16[128,8,256]{2,1,0:T(8,128)(2,1)}), bf16[128,8,256]{2,1,0:T(8,128)(2,1)S(1)}, u32[]{:S(2)}, u32[]{:S(2)}) async-start(bf16[128,8,256]{2,1,0:T(8,128)(2,1)} %bitcast.30), calls=%async_computation | async-start | bytes 1048576 | tf_op jit(solution)/shard_map/all_to_all | solution.py:346
  20.8 8.1 %collective-permute-start = (f32[8,256]{1,0:T(8,128)}, f32[8,256]{1,0:T(8,128)S(1)}, u32[]{:S(2)}, u32[]{:S(2)}) collective-permute-start(f32[8,256]{1,0:T(8,128)} %get-tuple-element.27.own_ids), channel_id=1, source_target_pairs={{0,1},{1,0},{2,3},{3,2},{4,5},{5,4},{6,7},{7,6},{8,9},{9,8},{10,11... | collective-permute-start | bytes 24584 | tf_op jit(solution)/shard_map/ppermute | solution.py:344
  37.6 42.4 %copy-start.1 = (f32[8,256]{1,0:T(8,128)S(1)}, f32[8,256]{1,0:T(8,128)}, u32[]{:S(2)}) copy-start(f32[8,256]{1,0:T(8,128)} %get-tuple-element.27.own_ids) | copy-start | bytes 24580
  68.1 11.9 %collective-permute-start.2 = (bf16[1024,384]{1,0:T(8,128)(2,1)S(1)}, bf16[1024,384]{1,0:T(8,128)(2,1)S(1)}, u32[]{:S(2)}, u32[]{:S(2)}) collective-permute-start(bf16[1024,384]{1,0:T(8,128)(2,1)S(1)} %bitcast.20), channel_id=1, source_target_pairs={{0,1},{1,0},{2,3},{3,2},{4,5},{5,4},{6,7},{7,6},{8,9},{9,8},{10,11... | collective-permute-start | bytes 2359304 | tf_op jit(solution)/shard_map/ppermute | solution.py:394
  73.7 1.4 %collective-permute-start.1 = (f32[16,128]{1,0:T(8,128)S(1)}, f32[16,128]{1,0:T(8,128)S(1)}, u32[]{:S(2)}, u32[]{:S(2)}) collective-permute-start(f32[16,128]{1,0:T(8,128)S(1)} %get-tuple-element.38), channel_id=1, source_target_pairs={{0,1},{1,0},{2,3},{3,2},{4,5},{5,4},{6,7},{7,6},{8,9},{9,8},{10,11... | collective-permute-start | bytes 24584 | tf_op jit(solution)/shard_map/ppermute | solution.py:392
  75.8 13.4 %all-to-all-start.2 = ((bf16[32,16,128]{2,1,0:T(8,128)(2,1)}), bf16[32,16,128]{2,1,0:T(8,128)(2,1)S(1)}, u32[]{:S(2)}, u32[]{:S(2)}) async-start(bf16[32,16,128]{2,1,0:T(8,128)(2,1)} %broadcast_in_dim.2), calls=%async_computation.2 | async-start | bytes 262144 | tf_op jit(solution)/shard_map/all_to_all | solution.py:290
  89.4 7.4 %collective-permute-start.4 = (bf16[512,128]{1,0:T(8,128)(2,1)S(1)}, bf16[512,128]{1,0:T(8,128)(2,1)S(1)}, u32[]{:S(2)}, u32[]{:S(2)}) collective-permute-start(bf16[512,128]{1,0:T(8,128)(2,1)S(1)} %order_column.1.refs_0_), channel_id=1, source_target_pairs={{0,2},{2,4},{4,6},{6,0},{8,10},{10,12},{12,14},{14,8},{16,18},{18,... | collective-permute-start | bytes 393224 | tf_op jit(solution)/shard_map/ppermute | solution.py:419
  89.8 7.0 %collective-permute-start.6 = (bf16[512,128]{1,0:T(8,128)(2,1)S(1)}, bf16[512,128]{1,0:T(8,128)(2,1)S(1)}, u32[]{:S(2)}, u32[]{:S(2)}) collective-permute-start(bf16[512,128]{1,0:T(8,128)(2,1)S(1)} %order_column.1.refs_0_), channel_id=1, source_target_pairs={{0,4},{2,6},{4,0},{6,2},{8,12},{10,14},{12,8},{14,10},{16,20},{18,... | collective-permute-start | bytes 393224 | tf_op jit(solution)/shard_map/ppermute | solution.py:419
  91.5 5.4 %collective-permute-start.8 = (bf16[512,128]{1,0:T(8,128)(2,1)S(1)}, bf16[512,128]{1,0:T(8,128)(2,1)S(1)}, u32[]{:S(2)}, u32[]{:S(2)}) collective-permute-start(bf16[512,128]{1,0:T(8,128)(2,1)S(1)} %order_column.1.refs_0_), channel_id=1, source_target_pairs={{0,6},{2,0},{4,2},{6,4},{8,14},{10,8},{12,10},{14,12},{16,22},{18,... | collective-permute-start | bytes 393224 | tf_op jit(solution)/shard_map/ppermute | solution.py:419
  93.8 7.1 %collective-permute-start.3 = (bf16[512,128]{1,0:T(8,128)(2,1)S(1)}, bf16[512,128]{1,0:T(8,128)(2,1)S(1)}, u32[]{:S(2)}, u32[]{:S(2)}) collective-permute-start(bf16[512,128]{1,0:T(8,128)(2,1)S(1)} %order_column.1.refs_0_), channel_id=1, source_target_pairs={{0,1},{1,0},{2,3},{3,2},{4,5},{5,4},{6,7},{7,6},{8,9},{9,8},{10,11... | collective-permute-start | bytes 393224 | tf_op jit(solution)/shard_map/ppermute | solution.py:428
  96.9 4.1 %collective-permute-start.9 = (bf16[512,128]{1,0:T(8,128)(2,1)S(1)}, bf16[512,128]{1,0:T(8,128)(2,1)S(1)}, u32[]{:S(2)}, u32[]{:S(2)}) collective-permute-start(bf16[512,128]{1,0:T(8,128)(2,1)S(1)} %collective-permute-done.8.refs_2_), channel_id=1, source_target_pairs={{0,1},{1,0},{2,3},{3,2},{4,5},{5,4},{6,7},{7,6},{8,9},{9,8},{10,11... | collective-permute-start | bytes 393224 | tf_op jit(solution)/shard_map/ppermute | solution.py:428
  100.0 1.3 %collective-permute-start.7 = (bf16[512,128]{1,0:T(8,128)(2,1)S(1)}, bf16[512,128]{1,0:T(8,128)(2,1)S(1)}, u32[]{:S(2)}, u32[]{:S(2)}) collective-permute-start(bf16[512,128]{1,0:T(8,128)(2,1)S(1)} %collective-permute-done.6.refs_1_), channel_id=1, source_target_pairs={{0,1},{1,0},{2,3},{3,2},{4,5},{5,4},{6,7},{7,6},{8,9},{9,8},{10,11... | collective-permute-start | bytes 393224 | tf_op jit(solution)/shard_map/ppermute | solution.py:428
  100.0 1.5 %collective-permute-start.5 = (bf16[512,128]{1,0:T(8,128)(2,1)S(1)}, bf16[512,128]{1,0:T(8,128)(2,1)S(1)}, u32[]{:S(2)}, u32[]{:S(2)}) collective-permute-start(bf16[512,128]{1,0:T(8,128)(2,1)S(1)} %collective-permute-done.4.refs_0_), channel_id=1, source_target_pairs={{0,1},{1,0},{2,3},{3,2},{4,5},{5,4},{6,7},{7,6},{8,9},{9,8},{10,11... | collective-permute-start | bytes 393224 | tf_op jit(solution)/shard_map/ppermute | solution.py:428

commit v5 on v4

--- a/solution.py
+++ b/solution.py
@@ -358,7 +358,14 @@
         name="count_edges",
     )(rel_ids, used, heads.reshape(2, -1), tails.reshape(2, -1), negatives.reshape(2, -1))
 
-    received, peer_ids, *counts = lax.optimization_barrier((received, peer_ids, *counts))
+    x = lax.axis_index("bucket").astype(jnp.int32) & 3
+    xs = (x - jnp.array([0, 1, 2, 3, 1, 2, 3], jnp.int32)) & 3
+    own_q = jnp.broadcast_to(rep, (1,))
+    qs = jnp.where(jnp.arange(7) < 4, 1 - rep, rep)
+    first_x = xs[:1]
+    places = (first_x, own_q, xs, qs)
+    received, peer_ids, places, *counts = lax.optimization_barrier((received, peer_ids, places, *counts))
+    first_x, own_q, xs, qs = places
     returned = pl.pallas_call(
         functools.partial(step_kernel, neg_count),
         out_shape=jax.ShapeDtypeStruct((chips * 8, 384), BF16),
@@ -391,6 +398,16 @@
     )(rep, own)
     sums = (keep + lax.ppermute(give, "rep", swap)).astype(BF16)
     column = gather_among(sums, ACROSS_YZ)
+    column = pl.pallas_call(
+        order_kernel,
+        out_shape=jax.ShapeDtypeStruct(column.shape, BF16),
+        in_specs=[VMEM],
+        out_specs=VMEM,
+        compiler_params=limit(8),
+        name="order_column",
+    )(column)
+    pieces = [column] + [lax.ppermute(column, "bucket", along_x(step)) for step in (1, 2, 3)]
+
     peer = lax.ppermute(own, "rep", swap)
     chunk = 256
     rows_spec = pl.BlockSpec((chips * 8, 256), lambda i: (0, 0))
@@ -407,24 +424,10 @@
         name="scatter_rows",
     )(own, peer, ids, peer_ids)
 
-    column, entity_grad = lax.optimization_barrier((column, entity_grad))
-    column = pl.pallas_call(
-        order_kernel,
-        out_shape=jax.ShapeDtypeStruct(column.shape, BF16),
-        in_specs=[VMEM],
-        out_specs=VMEM,
-        compiler_params=limit(8),
-        name="order_column",
-    )(column)
-    pieces = [column] + [lax.ppermute(column, "bucket", along_x(step)) for step in (1, 2, 3)]
-
-    x = lax.axis_index("bucket").astype(jnp.int32) & 3
-    xs = (x - jnp.arange(4, dtype=jnp.int32)) & 3
-    own_q = jnp.broadcast_to(rep, (4,))
-    relation_grad = lay_out(pieces[:1], None, xs[:1], own_q[:1], None)
+    relation_grad = lay_out(pieces[:1], None, first_x, own_q, None)
     peer_pieces = []
     for n in range(4):
-        pieces[n], relation_grad = lax.optimization_barrier((pieces[n], relation_grad))
+        pieces[n], entity_grad, relation_grad = lax.optimization_barrier((pieces[n], entity_grad, relation_grad))
         peer_pieces.append(lax.ppermute(pieces[n], "rep", swap))
     wide = pl.pallas_call(
         widen_kernel,
@@ -435,9 +438,7 @@
         cost_estimate=pl.CostEstimate(flops=1 << 20, bytes_accessed=3 << 20, transcendentals=0),
         name="widen_own",
     )(*pieces[1:])
-    relation_grad = lay_out(
-        peer_pieces, wide, jnp.concatenate([xs, xs[1:]]), jnp.concatenate([1 - own_q, own_q[1:]]), relation_grad
-    )
+    relation_grad = lay_out(peer_pieces, wide, xs, qs, relation_grad)
     relation_grad = relation_grad.reshape(relations.shape)
     return entity_grad, relation_grad
 

time: 105 us -> 104 us (level)
  blocking collectives: 28.4 us -> 41.6 us
  starting transfers between devices: 36.9 us -> 29.4 us
  waiting for transfers between devices: 16.5 us -> 11.6 us
    all_to_all x0 -> x1, blocking collectives: none -> 13.2 us  [gather_among(): lax.all_to_all(spread, 'bucket', 0, 0, axis_index_groups=groups, tiled=True)]
    all_to_all x1 -> x0, waiting for transfers between devices: 5.68 us -> none  [gather_among(): lax.all_to_all(spread, 'bucket', 0, 0, axis_index_groups=groups, tiled=True)]
    all_to_all x1 -> x0, starting transfers between devices: 4.25 us -> none  [gather_among(): lax.all_to_all(spread, 'bucket', 0, 0, axis_index_groups=groups, tiled=True)]
    ppermute x4, starting transfers between devices: 6.71 us -> 3.63 us  [body(): peer_pieces.append(lax.ppermute(pieces[n], 'rep', swap))]
  transfers between devices with their start and end apart: 12 -> 11, of which waited for: 6 -> 6; matrix products, arithmetic and copies ran while one was open for 2% -> 2% of each run, Pallas kernels for 6% -> 6%
where the time goes in v5:
time: 104 us
  blocking collectives  41.6 us (40%)
  starting transfers between devices  29.4 us (28%)
  Pallas kernels  14.8 us (14%)
  waiting for transfers between devices  11.6 us (11%)
  between operations  4.68 us (4%)
  local copies, waits for them, and re-layouts  1.64 us (2%)
    all_to_all x1, blocking collectives, body(): lax.all_to_all(returned.reshape(chips, 8, 384), 'bucket', 0, 0, tiled=True)  28.4 us
    all_to_all x1, starting transfers between devices, body(): lax.all_to_all(packed.reshape(chips, 8, 256), 'bucket', 0, 0, tiled=True)  16.3 us
    all_to_all x1, blocking collectives, gather_among(): lax.all_to_all(spread, 'bucket', 0, 0, axis_index_groups=groups, tiled=True)  13.2 us
    all_to_all x1, waiting for transfers between devices, body(): lax.all_to_all(packed.reshape(chips, 8, 256), 'bucket', 0, 0, tiled=True)  9.18 us
    ppermute x1, starting transfers between devices, body(): peer = lax.ppermute(own, 'rep', swap)  5.03 us
    pallas_call x1, Pallas kernels, body(): pl.pallas_call(send_kernel, out_shape=(jax.ShapeDtypeStruct((chips * 8, 2...  3.73 us
    ppermute x4, starting transfers between devices, body(): peer_pieces.append(lax.ppermute(pieces[n], 'rep', swap))  3.63 us
    pallas_call x1, Pallas kernels, body(): pl.pallas_call(scatter_kernel, out_shape=jax.ShapeDtypeStruct((entities,...  3.46 us
  transfers between devices with their start and end apart: 11, of which 6 were waited for; matrix products, arithmetic and copies ran while one was open for 2% of the time, Pallas kernels for 6%

profile of v5, /device:TPU:1, one launch (start us, length us, event | category | flops | bytes accessed | tf_op | source)
XLA Modules:
  0.0 103.7 jit_solution(15550110365661193327)
XLA Ops:
  0.7 3.7 %send_rows.1 = (bf16[1024,256]{1,0:T(8,128)(2,1)}, f32[8,256]{1,0:T(8,128)}) custom-call(s32[2,256]{1,0:T(2,128)} %bitcast.32, s32[2,128]{1,0:T(2,128)} %bitcast.33, bf16[1024,512]{1,0:T(8,128)(2,1)} %table_ref.1), custom_call_target="tpu_custom_call" | custom-call | tf_op jit(solution)/shard_map/send_rows/pallas_call | solution.py:327
  4.4 16.3 %all-to-all-start = ((bf16[128,8,256]{2,1,0:T(8,128)(2,1)}), bf16[128,8,256]{2,1,0:T(8,128)(2,1)S(1)}, u32[]{:S(2)}, u32[]{:S(2)}) async-start(bf16[128,8,256]{2,1,0:T(8,128)(2,1)} %bitcast.31), calls=%async_computation | async-start | bytes 1048576 | tf_op jit(solution)/shard_map/all_to_all | solution.py:346
  20.8 1.0 %collective-permute-start = (f32[8,256]{1,0:T(8,128)}, f32[8,256]{1,0:T(8,128)S(1)}, u32[]{:S(2)}, u32[]{:S(2)}) collective-permute-start(f32[8,256]{1,0:T(8,128)} %get-tuple-element.33.own_ids), channel_id=1, source_target_pairs={{0,1},{1,0},{2,3},{3,2},{4,5},{5,4},{6,7},{7,6},{8,9},{9,8},{10,11... | collective-permute-start | bytes 24584 | tf_op jit(solution)/shard_map/ppermute | solution.py:344
  21.8 0.6 fusion
  26.1 1.0 constant_dynamic-slice_fusion.1
  27.2 1.2 %count_edges.1 = (f32[8,128]{1,0:T(8,128)S(1)}, bf16[2,2,256,256]{3,2,1,0:T(8,128)(2,1)S(1)}, f32[2,256,256]{2,1,0:T(8,128)S(1)}, f32[2,8,256]{2,1,0:T(8,128)S(1)}) custom-call(s32[2]{0:T(128)S(1)} %bitcast.29, bf16[2,8,64,64]{3,2,1,0:T(8,128)(2,1)S(1)} %pad_maximum_fusion.relation_ref, s32[2,512]{1,0:T(2,128)S(1)} %get-tuple-element.67.heads_ref, ...), custom_call_target="tpu_custom_call" | custom-call | flops 268435456 | bytes 4194304 | tf_op jit(solution)/shard_map/count_edges/pallas_call | solution.py:351
  28.4 9.2 %all-to-all-done = bf16[128,8,256]{2,1,0:T(8,128)(2,1)S(1)} async-done(((bf16[128,8,256]{2,1,0:T(8,128)(2,1)}), bf16[128,8,256]{2,1,0:T(8,128)(2,1)S(1)}, u32[]{:S(2)}, u32[]{:S(2)}) %all-to-all-start) | async-done | bytes 524320 | tf_op jit(solution)/shard_map/all_to_all | solution.py:346
  37.6 2.1 %train_step.1 = bf16[1024,384]{1,0:T(8,128)(2,1)S(1)} custom-call(bf16[1024,256]{1,0:T(8,128)(2,1)S(1)} %bitcast.25, f32[8,128]{1,0:T(8,128)S(1)} %get-tuple-element.39.names, bf16[2,2,256,256]{3,2,1,0:T(8,128)(2,1)S(1)} %get-tuple-element.40.diag, f32[2,256,256]{2,1,0:T(8,128)S(1)} %get-tuple-element.41.edges, f32[2,8,256]{2,1,0:T(8,128)S(1)} %get-tuple-element.42.times), custom_call_target="tpu_custom_call" | custom-call | tf_op jit(solution)/shard_map/train_step/pallas_call | solution.py:369
  39.7 28.4 %all_to_all.15 = bf16[128,8,384]{2,1,0:T(8,128)(2,1)S(1)} all-to-all(bf16[128,8,384]{2,1,0:T(8,128)(2,1)S(1)} %bitcast.24), channel_id=1, replica_groups=mesh['bucket'=128,'rep'=2] {'bucket'}, dimensions={0} | all-to-all | bytes 1572864 | tf_op jit(solution)/shard_map/all_to_all | solution.py:383
  68.1 5.0 %collective-permute-start.5 = (bf16[1024,384]{1,0:T(8,128)(2,1)S(1)}, bf16[1024,384]{1,0:T(8,128)(2,1)S(1)}, u32[]{:S(2)}, u32[]{:S(2)}) collective-permute-start(bf16[1024,384]{1,0:T(8,128)(2,1)S(1)} %bitcast.21), channel_id=1, source_target_pairs={{0,1},{1,0},{2,3},{3,2},{4,5},{5,4},{6,7},{7,6},{8,9},{9,8},{10,11... | collective-permute-start | bytes 2359304 | tf_op jit(solution)/shard_map/ppermute | solution.py:411
  73.2 0.5 sum_relations.1
  73.8 1.3 %collective-permute-done.1 = f32[16,128]{1,0:T(8,128)S(1)} collective-permute-done((f32[16,128]{1,0:T(8,128)S(1)}, f32[16,128]{1,0:T(8,128)S(1)}, u32[]{:S(2)}, u32[]{:S(2)}) %collective-permute-start.1) | collective-permute-done | bytes 8224 | tf_op jit(solution)/shard_map/ppermute | solution.py:399
  75.1 13.2 %all_to_all.16 = bf16[32,16,128]{2,1,0:T(8,128)(2,1)S(1)} all-to-all(bf16[32,16,128]{2,1,0:T(8,128)(2,1)S(1)} %broadcast_in_dim.27), channel_id=1, replica_groups={{0,8,16,24,32,40,48,56,64,72,80,88,96,104,112,120,128,136,144,152,160,1..., dimensions={0} | all-to-all | bytes 262144 | tf_op jit(solution)/shard_map/all_to_all | solution.py:290
  88.3 0.2 order_column.1.refs_0_
  88.6 0.4 collective-permute-start.4
  89.0 1.6 %collective-permute-start.3 = (bf16[512,128]{1,0:T(8,128)(2,1)S(1)}, bf16[512,128]{1,0:T(8,128)(2,1)S(1)}, u32[]{:S(2)}, u32[]{:S(2)}) collective-permute-start(bf16[512,128]{1,0:T(8,128)(2,1)S(1)} %order_column.1.refs_0_), channel_id=1, source_target_pairs={{0,4},{2,6},{4,0},{6,2},{8,12},{10,14},{12,8},{14,10},{16,20},{18,... | collective-permute-start | bytes 393224 | tf_op jit(solution)/shard_map/ppermute | solution.py:409
  90.6 1.2 %collective-permute-start.2 = (bf16[512,128]{1,0:T(8,128)(2,1)S(1)}, bf16[512,128]{1,0:T(8,128)(2,1)S(1)}, u32[]{:S(2)}, u32[]{:S(2)}) collective-permute-start(bf16[512,128]{1,0:T(8,128)(2,1)S(1)} %order_column.1.refs_0_), channel_id=1, source_target_pairs={{0,6},{2,0},{4,2},{6,4},{8,14},{10,8},{12,10},{14,12},{16,22},{18,... | collective-permute-start | bytes 393224 | tf_op jit(solution)/shard_map/ppermute | solution.py:409
  91.8 0.9 lay_out_relations.2.refs_5_
  92.8 3.5 %scatter_rows.1 = f32[1024,512]{1,0:T(8,128)} custom-call(bf16[1024,384]{1,0:T(8,128)(2,1)S(1)} %bitcast.23, bf16[1024,384]{1,0:T(8,128)(2,1)S(1)} %collective-permute-done.5.peer_ref, f32[8,256]{1,0:T(8,128)S(1)} %copy-done.1, f32[8,256]{1,0:T(8,128)S(1)} %collective-permute-done.peer_ids), custom_call_target="tpu_custom_call" | custom-call | flops 1073741824 | bytes 16777216 | tf_op jit(solution)/shard_map/scatter_rows/pallas_call | solution.py:415
  96.2 3.0 %collective-permute-start.9 = (bf16[512,128]{1,0:T(8,128)(2,1)S(1)}, bf16[512,128]{1,0:T(8,128)(2,1)S(1)}, u32[]{:S(2)}, u32[]{:S(2)}) collective-permute-start(bf16[512,128]{1,0:T(8,128)(2,1)S(1)} %collective-permute-done.2.refs_2_), channel_id=1, source_target_pairs={{0,1},{1,0},{2,3},{3,2},{4,5},{5,4},{6,7},{7,6},{8,9},{9,8},{10,11... | collective-permute-start | bytes 393224 | tf_op jit(solution)/shard_map/ppermute | solution.py:431
  99.4 0.4 collective-permute-start.7
  100.3 0.4 collective-permute-done.8.refs_2_
  100.8 0.3 collective-permute-done.6.refs_0_
  101.1 2.4 %lay_out_relations.3 = f32[16,4,2,2,32,64]{5,4,3,2,1,0:T(8,128)} custom-call(s32[7]{0:T(128)S(1)} %get-tuple-element.55.xs_ref, s32[7]{0:T(128)S(1)} %get-tuple-element.56.qs_ref, bf16[512,128]{1,0:T(8,128)(2,1)S(1)} %collective-permute-done.6.refs_0_, bf16[512,128]{1,0:T(8,128)(2,1)S(1)} %collective-permute-done.7.refs_1_, ...), custom_call_target="tpu_custom_call", output_to_operand_aliasing={{}: (7, {})} | custom-call | flops 1048576 | bytes 4194304 | tf_op jit(solution)/shard_map/lay_out_relations/pallas_call | solution.py:304
  (29 shorter events, 1.0 us)
Async XLA Ops:
  0.6 26.5 %copy-start.5 = (s32[7]{0:T(128)S(1)}, s32[7]{0:T(128)}, u32[]{:S(2)}) copy-start(s32[7]{0:T(128)} %constant.28) | copy-start | bytes 88
  0.6 21.2 %copy-start = (s32[1,1,2,1]{2,3,1,0:T(1,128)S(1)}, s32[1,1,2,1]{2,3,1,0:T(1,128)}, u32[]{:S(2)}) copy-start(s32[1,1,2,1]{2,3,1,0:T(1,128)} %param.16) | copy-start | bytes 28
  0.7 24.2 %copy-start.2 = (s32[1,1,2,1,1000]{4,3,2,1,0:T(1,128)S(1)}, s32[1,1,2,1,1000]{4,3,2,1,0:T(1,128)}, u32[]{:S(2)}) copy-start(s32[1,1,2,1,1000]{4,3,2,1,0:T(1,128)} %param.15) | copy-start | bytes 24004
  0.7 26.5 %copy-start.3 = (s32[1,1,2,1,512]{4,3,2,1,0:T(1,128)S(1)}, s32[1,1,2,1,512]{4,3,2,1,0:T(1,128)}, u32[]{:S(2)}) copy-start(s32[1,1,2,1,512]{4,3,2,1,0:T(1,128)} %param.14) | copy-start | bytes 12292
  0.7 26.5 %copy-start.4 = (s32[1,1,2,1,512]{4,3,2,1,0:T(1,128)S(1)}, s32[1,1,2,1,512]{4,3,2,1,0:T(1,128)}, u32[]{:S(2)}) copy-start(s32[1,1,2,1,512]{4,3,2,1,0:T(1,128)} %param.13) | copy-start | bytes 12292
  4.4 33.2 %all-to-all-start = ((bf16[128,8,256]{2,1,0:T(8,128)(2,1)}), bf16[128,8,256]{2,1,0:T(8,128)(2,1)S(1)}, u32[]{:S(2)}, u32[]{:S(2)}) async-start(bf16[128,8,256]{2,1,0:T(8,128)(2,1)} %bitcast.31), calls=%async_computation | async-start | bytes 1048576 | tf_op jit(solution)/shard_map/all_to_all | solution.py:346
  20.8 7.7 %collective-permute-start = (f32[8,256]{1,0:T(8,128)}, f32[8,256]{1,0:T(8,128)S(1)}, u32[]{:S(2)}, u32[]{:S(2)}) collective-permute-start(f32[8,256]{1,0:T(8,128)} %get-tuple-element.33.own_ids), channel_id=1, source_target_pairs={{0,1},{1,0},{2,3},{3,2},{4,5},{5,4},{6,7},{7,6},{8,9},{9,8},{10,11... | collective-permute-start | bytes 24584 | tf_op jit(solution)/shard_map/ppermute | solution.py:344
  68.1 24.6 %collective-permute-start.5 = (bf16[1024,384]{1,0:T(8,128)(2,1)S(1)}, bf16[1024,384]{1,0:T(8,128)(2,1)S(1)}, u32[]{:S(2)}, u32[]{:S(2)}) collective-permute-start(bf16[1024,384]{1,0:T(8,128)(2,1)S(1)} %bitcast.21), channel_id=1, source_target_pairs={{0,1},{1,0},{2,3},{3,2},{4,5},{5,4},{6,7},{7,6},{8,9},{9,8},{10,11... | collective-permute-start | bytes 2359304 | tf_op jit(solution)/shard_map/ppermute | solution.py:411
  73.7 1.4 %collective-permute-start.1 = (f32[16,128]{1,0:T(8,128)S(1)}, f32[16,128]{1,0:T(8,128)S(1)}, u32[]{:S(2)}, u32[]{:S(2)}) collective-permute-start(f32[16,128]{1,0:T(8,128)S(1)} %get-tuple-element.44), channel_id=1, source_target_pairs={{0,1},{1,0},{2,3},{3,2},{4,5},{5,4},{6,7},{7,6},{8,9},{9,8},{10,11... | collective-permute-start | bytes 24584 | tf_op jit(solution)/shard_map/ppermute | solution.py:399
  88.6 4.2 %copy-start.1 = (f32[8,256]{1,0:T(8,128)S(1)}, f32[8,256]{1,0:T(8,128)}, u32[]{:S(2)}) copy-start(f32[8,256]{1,0:T(8,128)} %get-tuple-element.33.own_ids) | copy-start | bytes 24580
  88.6 7.7 %collective-permute-start.4 = (bf16[512,128]{1,0:T(8,128)(2,1)S(1)}, bf16[512,128]{1,0:T(8,128)(2,1)S(1)}, u32[]{:S(2)}, u32[]{:S(2)}) collective-permute-start(bf16[512,128]{1,0:T(8,128)(2,1)S(1)} %order_column.1.refs_0_), channel_id=1, source_target_pairs={{0,2},{2,4},{4,6},{6,0},{8,10},{10,12},{12,14},{14,8},{16,18},{18,... | collective-permute-start | bytes 393224 | tf_op jit(solution)/shard_map/ppermute | solution.py:409
  89.0 7.3 %collective-permute-start.3 = (bf16[512,128]{1,0:T(8,128)(2,1)S(1)}, bf16[512,128]{1,0:T(8,128)(2,1)S(1)}, u32[]{:S(2)}, u32[]{:S(2)}) collective-permute-start(bf16[512,128]{1,0:T(8,128)(2,1)S(1)} %order_column.1.refs_0_), channel_id=1, source_target_pairs={{0,4},{2,6},{4,0},{6,2},{8,12},{10,14},{12,8},{14,10},{16,20},{18,... | collective-permute-start | bytes 393224 | tf_op jit(solution)/shard_map/ppermute | solution.py:409
  90.6 5.6 %collective-permute-start.2 = (bf16[512,128]{1,0:T(8,128)(2,1)S(1)}, bf16[512,128]{1,0:T(8,128)(2,1)S(1)}, u32[]{:S(2)}, u32[]{:S(2)}) collective-permute-start(bf16[512,128]{1,0:T(8,128)(2,1)S(1)} %order_column.1.refs_0_), channel_id=1, source_target_pairs={{0,6},{2,0},{4,2},{6,4},{8,14},{10,8},{12,10},{14,12},{16,22},{18,... | collective-permute-start | bytes 393224 | tf_op jit(solution)/shard_map/ppermute | solution.py:409
  96.2 4.0 %collective-permute-start.9 = (bf16[512,128]{1,0:T(8,128)(2,1)S(1)}, bf16[512,128]{1,0:T(8,128)(2,1)S(1)}, u32[]{:S(2)}, u32[]{:S(2)}) collective-permute-start(bf16[512,128]{1,0:T(8,128)(2,1)S(1)} %collective-permute-done.2.refs_2_), channel_id=1, source_target_pairs={{0,1},{1,0},{2,3},{3,2},{4,5},{5,4},{6,7},{7,6},{8,9},{9,8},{10,11... | collective-permute-start | bytes 393224 | tf_op jit(solution)/shard_map/ppermute | solution.py:431
  99.3 1.3 %collective-permute-start.8 = (bf16[512,128]{1,0:T(8,128)(2,1)S(1)}, bf16[512,128]{1,0:T(8,128)(2,1)S(1)}, u32[]{:S(2)}, u32[]{:S(2)}) collective-permute-start(bf16[512,128]{1,0:T(8,128)(2,1)S(1)} %collective-permute-done.3.refs_1_), channel_id=1, source_target_pairs={{0,1},{1,0},{2,3},{3,2},{4,5},{5,4},{6,7},{7,6},{8,9},{9,8},{10,11... | collective-permute-start | bytes 393224 | tf_op jit(solution)/shard_map/ppermute | solution.py:431
  99.4 1.4 %collective-permute-start.7 = (bf16[512,128]{1,0:T(8,128)(2,1)S(1)}, bf16[512,128]{1,0:T(8,128)(2,1)S(1)}, u32[]{:S(2)}, u32[]{:S(2)}) collective-permute-start(bf16[512,128]{1,0:T(8,128)(2,1)S(1)} %collective-permute-done.4.refs_0_), channel_id=1, source_target_pairs={{0,1},{1,0},{2,3},{3,2},{4,5},{5,4},{6,7},{7,6},{8,9},{9,8},{10,11... | collective-permute-start | bytes 393224 | tf_op jit(solution)/shard_map/ppermute | solution.py:431
  99.8 1.3 %collective-permute-start.6 = (bf16[512,128]{1,0:T(8,128)(2,1)S(1)}, bf16[512,128]{1,0:T(8,128)(2,1)S(1)}, u32[]{:S(2)}, u32[]{:S(2)}) collective-permute-start(bf16[512,128]{1,0:T(8,128)(2,1)S(1)} %order_column.1.refs_0_), channel_id=1, source_target_pairs={{0,1},{1,0},{2,3},{3,2},{4,5},{5,4},{6,7},{7,6},{8,9},{9,8},{10,11... | collective-permute-start | bytes 393224 | tf_op jit(solution)/shard_map/ppermute | solution.py:431

commit v6 on v5

--- a/solution.py
+++ b/solution.py
@@ -223,15 +223,12 @@
 
             unpack_slots(lambda b: ref[b * 256 : b * 256 + 256, :], write)
 
-    base = pl.program_id(0) * 256
-    entity = iota((256, 256), 0) + base
-    total = jnp.zeros(out_ref.shape, F32)
-    for r, ref in enumerate((own_ids, peer_ids)):
-        for k in range(2):
-            start = (r * 2 + k) * 256
-            hit = onehot(entity == ref[k : k + 1, :].astype(jnp.int32))
-            total = total + dot(hit, rows_ref[start : start + 256, :])
-    out_ref[...] = total
+    count = out_ref.shape[0]
+    entity = iota((count, 256), 0) + pl.program_id(0) * count
+    hits = [
+        onehot(entity == ref[k : k + 1, :].astype(jnp.int32)) for ref in (own_ids, peer_ids) for k in range(2)
+    ]
+    out_ref[...] = dot(jnp.concatenate(hits, axis=1), rows_ref[...])
 
 
 def order_kernel(rows_ref, out_ref):
@@ -409,7 +406,7 @@
     pieces = [column] + [lax.ppermute(column, "bucket", along_x(step)) for step in (1, 2, 3)]
 
     peer = lax.ppermute(own, "rep", swap)
-    chunk = 256
+    chunk = 512
     rows_spec = pl.BlockSpec((chips * 8, 256), lambda i: (0, 0))
     ids_spec = pl.BlockSpec((8, 256), lambda i: (0, 0))
     entity_grad = pl.pallas_call(

time: 104 us -> 104 us (level)
  transfers between devices with their start and end apart: 11 -> 11, of which waited for: 6 -> 7; matrix products, arithmetic and copies ran while one was open for 2% -> 2% of each run, Pallas kernels for 6% -> 6%
where the time goes in v6:
time: 104 us
  blocking collectives  41.6 us (40%)
  starting transfers between devices  29.5 us (28%)
  Pallas kernels  14.3 us (14%)
  waiting for transfers between devices  11.9 us (11%)
  between operations  4.68 us (4%)
  local copies, waits for them, and re-layouts  1.64 us (2%)
    all_to_all x1, blocking collectives, body(): lax.all_to_all(returned.reshape(chips, 8, 384), 'bucket', 0, 0, tiled=True)  28.4 us
    all_to_all x1, starting transfers between devices, body(): lax.all_to_all(packed.reshape(chips, 8, 256), 'bucket', 0, 0, tiled=True)  16.3 us
    all_to_all x1, blocking collectives, gather_among(): lax.all_to_all(spread, 'bucket', 0, 0, axis_index_groups=groups, tiled=True)  13.2 us
    all_to_all x1, waiting for transfers between devices, body(): lax.all_to_all(packed.reshape(chips, 8, 256), 'bucket', 0, 0, tiled=True)  9.18 us
    ppermute x1, starting transfers between devices, body(): peer = lax.ppermute(own, 'rep', swap)  5.03 us
    ppermute x4, starting transfers between devices, body(): peer_pieces.append(lax.ppermute(pieces[n], 'rep', swap))  3.75 us
    pallas_call x1, Pallas kernels, body(): pl.pallas_call(send_kernel, out_shape=(jax.ShapeDtypeStruct((chips * 8, 2...  3.73 us
    pallas_call x2, Pallas kernels, lay_out(): pl.pallas_call(functools.partial(lay_out_kernel, count, ready), out_shape...  3.37 us
  transfers between devices with their start and end apart: 11, of which 7 were waited for; matrix products, arithmetic and copies ran while one was open for 2% of the time, Pallas kernels for 6%

profile of v6, /device:TPU:1, one launch (start us, length us, event | category | flops | bytes accessed | tf_op | source)
XLA Modules:
  0.0 103.6 jit_solution(18091518163405168565)
XLA Ops:
  0.7 3.7 %send_rows.1 = (bf16[1024,256]{1,0:T(8,128)(2,1)}, f32[8,256]{1,0:T(8,128)}) custom-call(s32[2,256]{1,0:T(2,128)} %bitcast.32, s32[2,128]{1,0:T(2,128)} %bitcast.33, bf16[1024,512]{1,0:T(8,128)(2,1)} %table_ref.1), custom_call_target="tpu_custom_call" | custom-call | tf_op jit(solution)/shard_map/send_rows/pallas_call | solution.py:324
  4.4 16.3 %all-to-all-start = ((bf16[128,8,256]{2,1,0:T(8,128)(2,1)}), bf16[128,8,256]{2,1,0:T(8,128)(2,1)S(1)}, u32[]{:S(2)}, u32[]{:S(2)}) async-start(bf16[128,8,256]{2,1,0:T(8,128)(2,1)} %bitcast.31), calls=%async_computation | async-start | bytes 1048576 | tf_op jit(solution)/shard_map/all_to_all | solution.py:343
  20.8 1.0 %collective-permute-start = (f32[8,256]{1,0:T(8,128)}, f32[8,256]{1,0:T(8,128)S(1)}, u32[]{:S(2)}, u32[]{:S(2)}) collective-permute-start(f32[8,256]{1,0:T(8,128)} %get-tuple-element.33.own_ids), channel_id=1, source_target_pairs={{0,1},{1,0},{2,3},{3,2},{4,5},{5,4},{6,7},{7,6},{8,9},{9,8},{10,11... | collective-permute-start | bytes 24584 | tf_op jit(solution)/shard_map/ppermute | solution.py:341
  21.8 0.6 fusion
  26.1 1.0 constant_dynamic-slice_fusion.1
  27.2 1.2 %count_edges.1 = (f32[8,128]{1,0:T(8,128)S(1)}, bf16[2,2,256,256]{3,2,1,0:T(8,128)(2,1)S(1)}, f32[2,256,256]{2,1,0:T(8,128)S(1)}, f32[2,8,256]{2,1,0:T(8,128)S(1)}) custom-call(s32[2]{0:T(128)S(1)} %bitcast.29, bf16[2,8,64,64]{3,2,1,0:T(8,128)(2,1)S(1)} %pad_maximum_fusion.relation_ref, s32[2,512]{1,0:T(2,128)S(1)} %get-tuple-element.67.heads_ref, ...), custom_call_target="tpu_custom_call" | custom-call | flops 268435456 | bytes 4194304 | tf_op jit(solution)/shard_map/count_edges/pallas_call | solution.py:348
  28.4 9.2 %all-to-all-done = bf16[128,8,256]{2,1,0:T(8,128)(2,1)S(1)} async-done(((bf16[128,8,256]{2,1,0:T(8,128)(2,1)}), bf16[128,8,256]{2,1,0:T(8,128)(2,1)S(1)}, u32[]{:S(2)}, u32[]{:S(2)}) %all-to-all-start) | async-done | bytes 524320 | tf_op jit(solution)/shard_map/all_to_all | solution.py:343
  37.6 2.1 %train_step.1 = bf16[1024,384]{1,0:T(8,128)(2,1)S(1)} custom-call(bf16[1024,256]{1,0:T(8,128)(2,1)S(1)} %bitcast.25, f32[8,128]{1,0:T(8,128)S(1)} %get-tuple-element.39.names, bf16[2,2,256,256]{3,2,1,0:T(8,128)(2,1)S(1)} %get-tuple-element.40.diag, f32[2,256,256]{2,1,0:T(8,128)S(1)} %get-tuple-element.41.edges, f32[2,8,256]{2,1,0:T(8,128)S(1)} %get-tuple-element.42.times), custom_call_target="tpu_custom_call" | custom-call | tf_op jit(solution)/shard_map/train_step/pallas_call | solution.py:366
  39.7 28.4 %all_to_all.15 = bf16[128,8,384]{2,1,0:T(8,128)(2,1)S(1)} all-to-all(bf16[128,8,384]{2,1,0:T(8,128)(2,1)S(1)} %bitcast.24), channel_id=1, replica_groups=mesh['bucket'=128,'rep'=2] {'bucket'}, dimensions={0} | all-to-all | bytes 1572864 | tf_op jit(solution)/shard_map/all_to_all | solution.py:380
  68.1 5.0 %collective-permute-start.5 = (bf16[1024,384]{1,0:T(8,128)(2,1)S(1)}, bf16[1024,384]{1,0:T(8,128)(2,1)S(1)}, u32[]{:S(2)}, u32[]{:S(2)}) collective-permute-start(bf16[1024,384]{1,0:T(8,128)(2,1)S(1)} %bitcast.21), channel_id=1, source_target_pairs={{0,1},{1,0},{2,3},{3,2},{4,5},{5,4},{6,7},{7,6},{8,9},{9,8},{10,11... | collective-permute-start | bytes 2359304 | tf_op jit(solution)/shard_map/ppermute | solution.py:408
  73.2 0.5 sum_relations.1
  73.8 1.3 %collective-permute-done.1 = f32[16,128]{1,0:T(8,128)S(1)} collective-permute-done((f32[16,128]{1,0:T(8,128)S(1)}, f32[16,128]{1,0:T(8,128)S(1)}, u32[]{:S(2)}, u32[]{:S(2)}) %collective-permute-start.1) | collective-permute-done | bytes 8224 | tf_op jit(solution)/shard_map/ppermute | solution.py:396
  75.1 13.2 %all_to_all.16 = bf16[32,16,128]{2,1,0:T(8,128)(2,1)S(1)} all-to-all(bf16[32,16,128]{2,1,0:T(8,128)(2,1)S(1)} %broadcast_in_dim.27), channel_id=1, replica_groups={{0,8,16,24,32,40,48,56,64,72,80,88,96,104,112,120,128,136,144,152,160,1..., dimensions={0} | all-to-all | bytes 262144 | tf_op jit(solution)/shard_map/all_to_all | solution.py:287
  88.6 0.4 collective-permute-start.4
  89.0 1.6 %collective-permute-start.3 = (bf16[512,128]{1,0:T(8,128)(2,1)S(1)}, bf16[512,128]{1,0:T(8,128)(2,1)S(1)}, u32[]{:S(2)}, u32[]{:S(2)}) collective-permute-start(bf16[512,128]{1,0:T(8,128)(2,1)S(1)} %order_column.1.refs_0_), channel_id=1, source_target_pairs={{0,4},{2,6},{4,0},{6,2},{8,12},{10,14},{12,8},{14,10},{16,20},{18,... | collective-permute-start | bytes 393224 | tf_op jit(solution)/shard_map/ppermute | solution.py:406
  90.6 1.2 %collective-permute-start.2 = (bf16[512,128]{1,0:T(8,128)(2,1)S(1)}, bf16[512,128]{1,0:T(8,128)(2,1)S(1)}, u32[]{:S(2)}, u32[]{:S(2)}) collective-permute-start(bf16[512,128]{1,0:T(8,128)(2,1)S(1)} %order_column.1.refs_0_), channel_id=1, source_target_pairs={{0,6},{2,0},{4,2},{6,4},{8,14},{10,8},{12,10},{14,12},{16,22},{18,... | collective-permute-start | bytes 393224 | tf_op jit(solution)/shard_map/ppermute | solution.py:406
  91.8 0.9 lay_out_relations.2.refs_5_
  92.8 3.0 %scatter_rows.1 = f32[1024,512]{1,0:T(8,128)} custom-call(bf16[1024,384]{1,0:T(8,128)(2,1)S(1)} %bitcast.23, bf16[1024,384]{1,0:T(8,128)(2,1)S(1)} %collective-permute-done.5.peer_ref, f32[8,256]{1,0:T(8,128)S(1)} %copy-done.1, f32[8,256]{1,0:T(8,128)S(1)} %collective-permute-done.peer_ids), custom_call_target="tpu_custom_call" | custom-call | flops 1073741824 | bytes 16777216 | tf_op jit(solution)/shard_map/scatter_rows/pallas_call | solution.py:412
  95.9 3.2 %collective-permute-start.9 = (bf16[512,128]{1,0:T(8,128)(2,1)S(1)}, bf16[512,128]{1,0:T(8,128)(2,1)S(1)}, u32[]{:S(2)}, u32[]{:S(2)}) collective-permute-start(bf16[512,128]{1,0:T(8,128)(2,1)S(1)} %collective-permute-done.2.refs_2_), channel_id=1, source_target_pairs={{0,1},{1,0},{2,3},{3,2},{4,5},{5,4},{6,7},{7,6},{8,9},{9,8},{10,11... | collective-permute-start | bytes 393224 | tf_op jit(solution)/shard_map/ppermute | solution.py:428
  99.2 0.5 collective-permute-start.7
  99.9 0.3 collective-permute-done.9.refs_3_
  100.2 0.4 collective-permute-done.8.refs_2_
  100.7 0.3 collective-permute-done.6.refs_0_
  101.0 2.4 %lay_out_relations.3 = f32[16,4,2,2,32,64]{5,4,3,2,1,0:T(8,128)} custom-call(s32[7]{0:T(128)S(1)} %get-tuple-element.55.xs_ref, s32[7]{0:T(128)S(1)} %get-tuple-element.56.qs_ref, bf16[512,128]{1,0:T(8,128)(2,1)S(1)} %collective-permute-done.6.refs_0_, bf16[512,128]{1,0:T(8,128)(2,1)S(1)} %collective-permute-done.7.refs_1_, ...), custom_call_target="tpu_custom_call", output_to_operand_aliasing={{}: (7, {})} | custom-call | flops 1048576 | bytes 4194304 | tf_op jit(solution)/shard_map/lay_out_relations/pallas_call | solution.py:301
  (29 shorter events, 1.0 us)
Async XLA Ops:
  0.6 26.5 %copy-start.5 = (s32[7]{0:T(128)S(1)}, s32[7]{0:T(128)}, u32[]{:S(2)}) copy-start(s32[7]{0:T(128)} %constant.28) | copy-start | bytes 88
  0.6 21.2 %copy-start = (s32[1,1,2,1]{2,3,1,0:T(1,128)S(1)}, s32[1,1,2,1]{2,3,1,0:T(1,128)}, u32[]{:S(2)}) copy-start(s32[1,1,2,1]{2,3,1,0:T(1,128)} %param.16) | copy-start | bytes 28
  0.7 24.2 %copy-start.2 = (s32[1,1,2,1,1000]{4,3,2,1,0:T(1,128)S(1)}, s32[1,1,2,1,1000]{4,3,2,1,0:T(1,128)}, u32[]{:S(2)}) copy-start(s32[1,1,2,1,1000]{4,3,2,1,0:T(1,128)} %param.15) | copy-start | bytes 24004
  0.7 26.5 %copy-start.3 = (s32[1,1,2,1,512]{4,3,2,1,0:T(1,128)S(1)}, s32[1,1,2,1,512]{4,3,2,1,0:T(1,128)}, u32[]{:S(2)}) copy-start(s32[1,1,2,1,512]{4,3,2,1,0:T(1,128)} %param.14) | copy-start | bytes 12292
  0.7 26.5 %copy-start.4 = (s32[1,1,2,1,512]{4,3,2,1,0:T(1,128)S(1)}, s32[1,1,2,1,512]{4,3,2,1,0:T(1,128)}, u32[]{:S(2)}) copy-start(s32[1,1,2,1,512]{4,3,2,1,0:T(1,128)} %param.13) | copy-start | bytes 12292
  4.4 33.2 %all-to-all-start = ((bf16[128,8,256]{2,1,0:T(8,128)(2,1)}), bf16[128,8,256]{2,1,0:T(8,128)(2,1)S(1)}, u32[]{:S(2)}, u32[]{:S(2)}) async-start(bf16[128,8,256]{2,1,0:T(8,128)(2,1)} %bitcast.31), calls=%async_computation | async-start | bytes 1048576 | tf_op jit(solution)/shard_map/all_to_all | solution.py:343
  20.8 7.7 %collective-permute-start = (f32[8,256]{1,0:T(8,128)}, f32[8,256]{1,0:T(8,128)S(1)}, u32[]{:S(2)}, u32[]{:S(2)}) collective-permute-start(f32[8,256]{1,0:T(8,128)} %get-tuple-element.33.own_ids), channel_id=1, source_target_pairs={{0,1},{1,0},{2,3},{3,2},{4,5},{5,4},{6,7},{7,6},{8,9},{9,8},{10,11... | collective-permute-start | bytes 24584 | tf_op jit(solution)/shard_map/ppermute | solution.py:341
  68.1 24.6 %collective-permute-start.5 = (bf16[1024,384]{1,0:T(8,128)(2,1)S(1)}, bf16[1024,384]{1,0:T(8,128)(2,1)S(1)}, u32[]{:S(2)}, u32[]{:S(2)}) collective-permute-start(bf16[1024,384]{1,0:T(8,128)(2,1)S(1)} %bitcast.21), channel_id=1, source_target_pairs={{0,1},{1,0},{2,3},{3,2},{4,5},{5,4},{6,7},{7,6},{8,9},{9,8},{10,11... | collective-permute-start | bytes 2359304 | tf_op jit(solution)/shard_map/ppermute | solution.py:408
  73.7 1.4 %collective-permute-start.1 = (f32[16,128]{1,0:T(8,128)S(1)}, f32[16,128]{1,0:T(8,128)S(1)}, u32[]{:S(2)}, u32[]{:S(2)}) collective-permute-start(f32[16,128]{1,0:T(8,128)S(1)} %get-tuple-element.44), channel_id=1, source_target_pairs={{0,1},{1,0},{2,3},{3,2},{4,5},{5,4},{6,7},{7,6},{8,9},{9,8},{10,11... | collective-permute-start | bytes 24584 | tf_op jit(solution)/shard_map/ppermute | solution.py:396
  88.6 4.2 %copy-start.1 = (f32[8,256]{1,0:T(8,128)S(1)}, f32[8,256]{1,0:T(8,128)}, u32[]{:S(2)}) copy-start(f32[8,256]{1,0:T(8,128)} %get-tuple-element.33.own_ids) | copy-start | bytes 24580
  88.6 7.2 %collective-permute-start.4 = (bf16[512,128]{1,0:T(8,128)(2,1)S(1)}, bf16[512,128]{1,0:T(8,128)(2,1)S(1)}, u32[]{:S(2)}, u32[]{:S(2)}) collective-permute-start(bf16[512,128]{1,0:T(8,128)(2,1)S(1)} %order_column.1.refs_0_), channel_id=1, source_target_pairs={{0,2},{2,4},{4,6},{6,0},{8,10},{10,12},{12,14},{14,8},{16,18},{18,... | collective-permute-start | bytes 393224 | tf_op jit(solution)/shard_map/ppermute | solution.py:406
  89.0 6.8 %collective-permute-start.3 = (bf16[512,128]{1,0:T(8,128)(2,1)S(1)}, bf16[512,128]{1,0:T(8,128)(2,1)S(1)}, u32[]{:S(2)}, u32[]{:S(2)}) collective-permute-start(bf16[512,128]{1,0:T(8,128)(2,1)S(1)} %order_column.1.refs_0_), channel_id=1, source_target_pairs={{0,4},{2,6},{4,0},{6,2},{8,12},{10,14},{12,8},{14,10},{16,20},{18,... | collective-permute-start | bytes 393224 | tf_op jit(solution)/shard_map/ppermute | solution.py:406
  90.6 5.3 %collective-permute-start.2 = (bf16[512,128]{1,0:T(8,128)(2,1)S(1)}, bf16[512,128]{1,0:T(8,128)(2,1)S(1)}, u32[]{:S(2)}, u32[]{:S(2)}) collective-permute-start(bf16[512,128]{1,0:T(8,128)(2,1)S(1)} %order_column.1.refs_0_), channel_id=1, source_target_pairs={{0,6},{2,0},{4,2},{6,4},{8,14},{10,8},{12,10},{14,12},{16,22},{18,... | collective-permute-start | bytes 393224 | tf_op jit(solution)/shard_map/ppermute | solution.py:406
  95.9 4.2 %collective-permute-start.9 = (bf16[512,128]{1,0:T(8,128)(2,1)S(1)}, bf16[512,128]{1,0:T(8,128)(2,1)S(1)}, u32[]{:S(2)}, u32[]{:S(2)}) collective-permute-start(bf16[512,128]{1,0:T(8,128)(2,1)S(1)} %collective-permute-done.2.refs_2_), channel_id=1, source_target_pairs={{0,1},{1,0},{2,3},{3,2},{4,5},{5,4},{6,7},{7,6},{8,9},{9,8},{10,11... | collective-permute-start | bytes 393224 | tf_op jit(solution)/shard_map/ppermute | solution.py:428
  99.2 1.3 %collective-permute-start.8 = (bf16[512,128]{1,0:T(8,128)(2,1)S(1)}, bf16[512,128]{1,0:T(8,128)(2,1)S(1)}, u32[]{:S(2)}, u32[]{:S(2)}) collective-permute-start(bf16[512,128]{1,0:T(8,128)(2,1)S(1)} %collective-permute-done.3.refs_1_), channel_id=1, source_target_pairs={{0,1},{1,0},{2,3},{3,2},{4,5},{5,4},{6,7},{7,6},{8,9},{9,8},{10,11... | collective-permute-start | bytes 393224 | tf_op jit(solution)/shard_map/ppermute | solution.py:428
  99.2 1.5 %collective-permute-start.7 = (bf16[512,128]{1,0:T(8,128)(2,1)S(1)}, bf16[512,128]{1,0:T(8,128)(2,1)S(1)}, u32[]{:S(2)}, u32[]{:S(2)}) collective-permute-start(bf16[512,128]{1,0:T(8,128)(2,1)S(1)} %collective-permute-done.4.refs_0_), channel_id=1, source_target_pairs={{0,1},{1,0},{2,3},{3,2},{4,5},{5,4},{6,7},{7,6},{8,9},{9,8},{10,11... | collective-permute-start | bytes 393224 | tf_op jit(solution)/shard_map/ppermute | solution.py:428
  99.7 1.3 %collective-permute-start.6 = (bf16[512,128]{1,0:T(8,128)(2,1)S(1)}, bf16[512,128]{1,0:T(8,128)(2,1)S(1)}, u32[]{:S(2)}, u32[]{:S(2)}) collective-permute-start(bf16[512,128]{1,0:T(8,128)(2,1)S(1)} %order_column.1.refs_0_), channel_id=1, source_target_pairs={{0,1},{1,0},{2,3},{3,2},{4,5},{5,4},{6,7},{7,6},{8,9},{9,8},{10,11... | collective-permute-start | bytes 393224 | tf_op jit(solution)/shard_map/ppermute | solution.py:428

commit v7 on v6

--- a/solution.py
+++ b/solution.py
@@ -157,8 +157,8 @@
         small_side = small * big_side
         sigmoid = jnp.where(score >= 0, big_side, small_side)
         sigmoid_neg = jnp.where(score >= 0, small_side, big_side)
-        pairs = jnp.sum(edges[k], axis=1, keepdims=True) * times[k][0:1, :]
-        weight = (pairs * sigmoid / neg_count - edges[k] * sigmoid_neg).astype(BF16)
+        pairs = jnp.sum(edges[k], axis=1, keepdims=True) * (times[k][0:1, :] / neg_count)
+        weight = (pairs * sigmoid - edges[k] * sigmoid_neg).astype(BF16)
         grad_rotated = dot(weight, rows).astype(BF16)
         grad_other = dot(weight, rotated, 0, 0)
         for c in range(2):

time: 104 us -> 104 us (level)
  no operation moved by 1% of the time
where the time goes in v7:
time: 104 us
  blocking collectives  41.6 us (40%)
  starting transfers between devices  29.5 us (28%)
  Pallas kernels  14.2 us (14%)
  waiting for transfers between devices  11.9 us (11%)
  between operations  4.68 us (4%)
  local copies, waits for them, and re-layouts  1.64 us (2%)
    all_to_all x1, blocking collectives, body(): lax.all_to_all(returned.reshape(chips, 8, 384), 'bucket', 0, 0, tiled=True)  28.4 us
    all_to_all x1, starting transfers between devices, body(): lax.all_to_all(packed.reshape(chips, 8, 256), 'bucket', 0, 0, tiled=True)  16.3 us
    all_to_all x1, blocking collectives, gather_among(): lax.all_to_all(spread, 'bucket', 0, 0, axis_index_groups=groups, tiled=True)  13.2 us
    all_to_all x1, waiting for transfers between devices, body(): lax.all_to_all(packed.reshape(chips, 8, 256), 'bucket', 0, 0, tiled=True)  9.18 us
    ppermute x1, starting transfers between devices, body(): peer = lax.ppermute(own, 'rep', swap)  5.03 us
    ppermute x4, starting transfers between devices, body(): peer_pieces.append(lax.ppermute(pieces[n], 'rep', swap))  3.75 us
    pallas_call x1, Pallas kernels, body(): pl.pallas_call(send_kernel, out_shape=(jax.ShapeDtypeStruct((chips * 8, 2...  3.73 us
    pallas_call x2, Pallas kernels, lay_out(): pl.pallas_call(functools.partial(lay_out_kernel, count, ready), out_shape...  3.37 us
  transfers between devices with their start and end apart: 11, of which 7 were waited for; matrix products, arithmetic and copies ran while one was open for 2% of the time, Pallas kernels for 6%

profile of v7, /device:TPU:1, one launch (start us, length us, event | category | flops | bytes accessed | tf_op | source)
XLA Modules:
  0.0 103.6 jit_solution(7752149074867617695)
XLA Ops:
  0.7 3.7 %send_rows.1 = (bf16[1024,256]{1,0:T(8,128)(2,1)}, f32[8,256]{1,0:T(8,128)}) custom-call(s32[2,256]{1,0:T(2,128)} %bitcast.32, s32[2,128]{1,0:T(2,128)} %bitcast.33, bf16[1024,512]{1,0:T(8,128)(2,1)} %table_ref.1), custom_call_target="tpu_custom_call" | custom-call | tf_op jit(solution)/shard_map/send_rows/pallas_call | solution.py:324
  4.4 16.3 %all-to-all-start = ((bf16[128,8,256]{2,1,0:T(8,128)(2,1)}), bf16[128,8,256]{2,1,0:T(8,128)(2,1)S(1)}, u32[]{:S(2)}, u32[]{:S(2)}) async-start(bf16[128,8,256]{2,1,0:T(8,128)(2,1)} %bitcast.31), calls=%async_computation | async-start | bytes 1048576 | tf_op jit(solution)/shard_map/all_to_all | solution.py:343
  20.8 1.0 %collective-permute-start = (f32[8,256]{1,0:T(8,128)}, f32[8,256]{1,0:T(8,128)S(1)}, u32[]{:S(2)}, u32[]{:S(2)}) collective-permute-start(f32[8,256]{1,0:T(8,128)} %get-tuple-element.33.own_ids), channel_id=1, source_target_pairs={{0,1},{1,0},{2,3},{3,2},{4,5},{5,4},{6,7},{7,6},{8,9},{9,8},{10,11... | collective-permute-start | bytes 24584 | tf_op jit(solution)/shard_map/ppermute | solution.py:341
  21.8 0.6 fusion
  26.1 1.0 constant_dynamic-slice_fusion.1
  27.2 1.2 %count_edges.1 = (f32[8,128]{1,0:T(8,128)S(1)}, bf16[2,2,256,256]{3,2,1,0:T(8,128)(2,1)S(1)}, f32[2,256,256]{2,1,0:T(8,128)S(1)}, f32[2,8,256]{2,1,0:T(8,128)S(1)}) custom-call(s32[2]{0:T(128)S(1)} %bitcast.29, bf16[2,8,64,64]{3,2,1,0:T(8,128)(2,1)S(1)} %pad_maximum_fusion.relation_ref, s32[2,512]{1,0:T(2,128)S(1)} %get-tuple-element.67.heads_ref, ...), custom_call_target="tpu_custom_call" | custom-call | flops 268435456 | bytes 4194304 | tf_op jit(solution)/shard_map/count_edges/pallas_call | solution.py:348
  28.4 9.2 %all-to-all-done = bf16[128,8,256]{2,1,0:T(8,128)(2,1)S(1)} async-done(((bf16[128,8,256]{2,1,0:T(8,128)(2,1)}), bf16[128,8,256]{2,1,0:T(8,128)(2,1)S(1)}, u32[]{:S(2)}, u32[]{:S(2)}) %all-to-all-start) | async-done | bytes 524320 | tf_op jit(solution)/shard_map/all_to_all | solution.py:343
  37.6 2.1 %train_step.1 = bf16[1024,384]{1,0:T(8,128)(2,1)S(1)} custom-call(bf16[1024,256]{1,0:T(8,128)(2,1)S(1)} %bitcast.25, f32[8,128]{1,0:T(8,128)S(1)} %get-tuple-element.39.names, bf16[2,2,256,256]{3,2,1,0:T(8,128)(2,1)S(1)} %get-tuple-element.40.diag, f32[2,256,256]{2,1,0:T(8,128)S(1)} %get-tuple-element.41.edges, f32[2,8,256]{2,1,0:T(8,128)S(1)} %get-tuple-element.42.times), custom_call_target="tpu_custom_call" | custom-call | tf_op jit(solution)/shard_map/train_step/pallas_call | solution.py:366
  39.7 28.4 %all_to_all.15 = bf16[128,8,384]{2,1,0:T(8,128)(2,1)S(1)} all-to-all(bf16[128,8,384]{2,1,0:T(8,128)(2,1)S(1)} %bitcast.24), channel_id=1, replica_groups=mesh['bucket'=128,'rep'=2] {'bucket'}, dimensions={0} | all-to-all | bytes 1572864 | tf_op jit(solution)/shard_map/all_to_all | solution.py:380
  68.1 5.0 %collective-permute-start.5 = (bf16[1024,384]{1,0:T(8,128)(2,1)S(1)}, bf16[1024,384]{1,0:T(8,128)(2,1)S(1)}, u32[]{:S(2)}, u32[]{:S(2)}) collective-permute-start(bf16[1024,384]{1,0:T(8,128)(2,1)S(1)} %bitcast.21), channel_id=1, source_target_pairs={{0,1},{1,0},{2,3},{3,2},{4,5},{5,4},{6,7},{7,6},{8,9},{9,8},{10,11... | collective-permute-start | bytes 2359304 | tf_op jit(solution)/shard_map/ppermute | solution.py:408
  73.2 0.5 sum_relations.1
  73.8 1.3 %collective-permute-done.1 = f32[16,128]{1,0:T(8,128)S(1)} collective-permute-done((f32[16,128]{1,0:T(8,128)S(1)}, f32[16,128]{1,0:T(8,128)S(1)}, u32[]{:S(2)}, u32[]{:S(2)}) %collective-permute-start.1) | collective-permute-done | bytes 8224 | tf_op jit(solution)/shard_map/ppermute | solution.py:396
  75.1 13.2 %all_to_all.16 = bf16[32,16,128]{2,1,0:T(8,128)(2,1)S(1)} all-to-all(bf16[32,16,128]{2,1,0:T(8,128)(2,1)S(1)} %broadcast_in_dim.27), channel_id=1, replica_groups={{0,8,16,24,32,40,48,56,64,72,80,88,96,104,112,120,128,136,144,152,160,1..., dimensions={0} | all-to-all | bytes 262144 | tf_op jit(solution)/shard_map/all_to_all | solution.py:287
  88.5 0.4 collective-permute-start.4
  89.0 1.6 %collective-permute-start.3 = (bf16[512,128]{1,0:T(8,128)(2,1)S(1)}, bf16[512,128]{1,0:T(8,128)(2,1)S(1)}, u32[]{:S(2)}, u32[]{:S(2)}) collective-permute-start(bf16[512,128]{1,0:T(8,128)(2,1)S(1)} %order_column.1.refs_0_), channel_id=1, source_target_pairs={{0,4},{2,6},{4,0},{6,2},{8,12},{10,14},{12,8},{14,10},{16,20},{18,... | collective-permute-start | bytes 393224 | tf_op jit(solution)/shard_map/ppermute | solution.py:406
  90.6 1.2 %collective-permute-start.2 = (bf16[512,128]{1,0:T(8,128)(2,1)S(1)}, bf16[512,128]{1,0:T(8,128)(2,1)S(1)}, u32[]{:S(2)}, u32[]{:S(2)}) collective-permute-start(bf16[512,128]{1,0:T(8,128)(2,1)S(1)} %order_column.1.refs_0_), channel_id=1, source_target_pairs={{0,6},{2,0},{4,2},{6,4},{8,14},{10,8},{12,10},{14,12},{16,22},{18,... | collective-permute-start | bytes 393224 | tf_op jit(solution)/shard_map/ppermute | solution.py:406
  91.8 0.9 lay_out_relations.2.refs_5_
  92.8 2.9 %scatter_rows.1 = f32[1024,512]{1,0:T(8,128)} custom-call(bf16[1024,384]{1,0:T(8,128)(2,1)S(1)} %bitcast.23, bf16[1024,384]{1,0:T(8,128)(2,1)S(1)} %collective-permute-done.5.peer_ref, f32[8,256]{1,0:T(8,128)S(1)} %copy-done.1, f32[8,256]{1,0:T(8,128)S(1)} %collective-permute-done.peer_ids), custom_call_target="tpu_custom_call" | custom-call | flops 1073741824 | bytes 16777216 | tf_op jit(solution)/shard_map/scatter_rows/pallas_call | solution.py:412
  95.9 3.2 %collective-permute-start.9 = (bf16[512,128]{1,0:T(8,128)(2,1)S(1)}, bf16[512,128]{1,0:T(8,128)(2,1)S(1)}, u32[]{:S(2)}, u32[]{:S(2)}) collective-permute-start(bf16[512,128]{1,0:T(8,128)(2,1)S(1)} %collective-permute-done.2.refs_2_), channel_id=1, source_target_pairs={{0,1},{1,0},{2,3},{3,2},{4,5},{5,4},{6,7},{7,6},{8,9},{9,8},{10,11... | collective-permute-start | bytes 393224 | tf_op jit(solution)/shard_map/ppermute | solution.py:428
  99.2 0.5 collective-permute-start.7
  99.9 0.3 collective-permute-done.9.refs_3_
  100.1 0.4 collective-permute-done.8.refs_2_
  100.7 0.3 collective-permute-done.6.refs_0_
  101.0 2.4 %lay_out_relations.3 = f32[16,4,2,2,32,64]{5,4,3,2,1,0:T(8,128)} custom-call(s32[7]{0:T(128)S(1)} %get-tuple-element.55.xs_ref, s32[7]{0:T(128)S(1)} %get-tuple-element.56.qs_ref, bf16[512,128]{1,0:T(8,128)(2,1)S(1)} %collective-permute-done.6.refs_0_, bf16[512,128]{1,0:T(8,128)(2,1)S(1)} %collective-permute-done.7.refs_1_, ...), custom_call_target="tpu_custom_call", output_to_operand_aliasing={{}: (7, {})} | custom-call | flops 1048576 | bytes 4194304 | tf_op jit(solution)/shard_map/lay_out_relations/pallas_call | solution.py:301
  (29 shorter events, 1.0 us)
Async XLA Ops:
  0.6 26.5 %copy-start.5 = (s32[7]{0:T(128)S(1)}, s32[7]{0:T(128)}, u32[]{:S(2)}) copy-start(s32[7]{0:T(128)} %constant.28) | copy-start | bytes 88
  0.6 21.2 %copy-start = (s32[1,1,2,1]{2,3,1,0:T(1,128)S(1)}, s32[1,1,2,1]{2,3,1,0:T(1,128)}, u32[]{:S(2)}) copy-start(s32[1,1,2,1]{2,3,1,0:T(1,128)} %param.16) | copy-start | bytes 28
  0.7 24.2 %copy-start.2 = (s32[1,1,2,1,1000]{4,3,2,1,0:T(1,128)S(1)}, s32[1,1,2,1,1000]{4,3,2,1,0:T(1,128)}, u32[]{:S(2)}) copy-start(s32[1,1,2,1,1000]{4,3,2,1,0:T(1,128)} %param.15) | copy-start | bytes 24004
  0.7 26.5 %copy-start.3 = (s32[1,1,2,1,512]{4,3,2,1,0:T(1,128)S(1)}, s32[1,1,2,1,512]{4,3,2,1,0:T(1,128)}, u32[]{:S(2)}) copy-start(s32[1,1,2,1,512]{4,3,2,1,0:T(1,128)} %param.14) | copy-start | bytes 12292
  0.7 26.5 %copy-start.4 = (s32[1,1,2,1,512]{4,3,2,1,0:T(1,128)S(1)}, s32[1,1,2,1,512]{4,3,2,1,0:T(1,128)}, u32[]{:S(2)}) copy-start(s32[1,1,2,1,512]{4,3,2,1,0:T(1,128)} %param.13) | copy-start | bytes 12292
  4.4 33.2 %all-to-all-start = ((bf16[128,8,256]{2,1,0:T(8,128)(2,1)}), bf16[128,8,256]{2,1,0:T(8,128)(2,1)S(1)}, u32[]{:S(2)}, u32[]{:S(2)}) async-start(bf16[128,8,256]{2,1,0:T(8,128)(2,1)} %bitcast.31), calls=%async_computation | async-start | bytes 1048576 | tf_op jit(solution)/shard_map/all_to_all | solution.py:343
  20.8 7.7 %collective-permute-start = (f32[8,256]{1,0:T(8,128)}, f32[8,256]{1,0:T(8,128)S(1)}, u32[]{:S(2)}, u32[]{:S(2)}) collective-permute-start(f32[8,256]{1,0:T(8,128)} %get-tuple-element.33.own_ids), channel_id=1, source_target_pairs={{0,1},{1,0},{2,3},{3,2},{4,5},{5,4},{6,7},{7,6},{8,9},{9,8},{10,11... | collective-permute-start | bytes 24584 | tf_op jit(solution)/shard_map/ppermute | solution.py:341
  68.1 24.6 %collective-permute-start.5 = (bf16[1024,384]{1,0:T(8,128)(2,1)S(1)}, bf16[1024,384]{1,0:T(8,128)(2,1)S(1)}, u32[]{:S(2)}, u32[]{:S(2)}) collective-permute-start(bf16[1024,384]{1,0:T(8,128)(2,1)S(1)} %bitcast.21), channel_id=1, source_target_pairs={{0,1},{1,0},{2,3},{3,2},{4,5},{5,4},{6,7},{7,6},{8,9},{9,8},{10,11... | collective-permute-start | bytes 2359304 | tf_op jit(solution)/shard_map/ppermute | solution.py:408
  73.7 1.4 %collective-permute-start.1 = (f32[16,128]{1,0:T(8,128)S(1)}, f32[16,128]{1,0:T(8,128)S(1)}, u32[]{:S(2)}, u32[]{:S(2)}) collective-permute-start(f32[16,128]{1,0:T(8,128)S(1)} %get-tuple-element.44), channel_id=1, source_target_pairs={{0,1},{1,0},{2,3},{3,2},{4,5},{5,4},{6,7},{7,6},{8,9},{9,8},{10,11... | collective-permute-start | bytes 24584 | tf_op jit(solution)/shard_map/ppermute | solution.py:396
  88.5 4.2 %copy-start.1 = (f32[8,256]{1,0:T(8,128)S(1)}, f32[8,256]{1,0:T(8,128)}, u32[]{:S(2)}) copy-start(f32[8,256]{1,0:T(8,128)} %get-tuple-element.33.own_ids) | copy-start | bytes 24580
  88.5 7.2 %collective-permute-start.4 = (bf16[512,128]{1,0:T(8,128)(2,1)S(1)}, bf16[512,128]{1,0:T(8,128)(2,1)S(1)}, u32[]{:S(2)}, u32[]{:S(2)}) collective-permute-start(bf16[512,128]{1,0:T(8,128)(2,1)S(1)} %order_column.1.refs_0_), channel_id=1, source_target_pairs={{0,2},{2,4},{4,6},{6,0},{8,10},{10,12},{12,14},{14,8},{16,18},{18,... | collective-permute-start | bytes 393224 | tf_op jit(solution)/shard_map/ppermute | solution.py:406
  89.0 6.8 %collective-permute-start.3 = (bf16[512,128]{1,0:T(8,128)(2,1)S(1)}, bf16[512,128]{1,0:T(8,128)(2,1)S(1)}, u32[]{:S(2)}, u32[]{:S(2)}) collective-permute-start(bf16[512,128]{1,0:T(8,128)(2,1)S(1)} %order_column.1.refs_0_), channel_id=1, source_target_pairs={{0,4},{2,6},{4,0},{6,2},{8,12},{10,14},{12,8},{14,10},{16,20},{18,... | collective-permute-start | bytes 393224 | tf_op jit(solution)/shard_map/ppermute | solution.py:406
  90.6 5.3 %collective-permute-start.2 = (bf16[512,128]{1,0:T(8,128)(2,1)S(1)}, bf16[512,128]{1,0:T(8,128)(2,1)S(1)}, u32[]{:S(2)}, u32[]{:S(2)}) collective-permute-start(bf16[512,128]{1,0:T(8,128)(2,1)S(1)} %order_column.1.refs_0_), channel_id=1, source_target_pairs={{0,6},{2,0},{4,2},{6,4},{8,14},{10,8},{12,10},{14,12},{16,22},{18,... | collective-permute-start | bytes 393224 | tf_op jit(solution)/shard_map/ppermute | solution.py:406
  95.9 4.2 %collective-permute-start.9 = (bf16[512,128]{1,0:T(8,128)(2,1)S(1)}, bf16[512,128]{1,0:T(8,128)(2,1)S(1)}, u32[]{:S(2)}, u32[]{:S(2)}) collective-permute-start(bf16[512,128]{1,0:T(8,128)(2,1)S(1)} %collective-permute-done.2.refs_2_), channel_id=1, source_target_pairs={{0,1},{1,0},{2,3},{3,2},{4,5},{5,4},{6,7},{7,6},{8,9},{9,8},{10,11... | collective-permute-start | bytes 393224 | tf_op jit(solution)/shard_map/ppermute | solution.py:428
  99.2 1.3 %collective-permute-start.8 = (bf16[512,128]{1,0:T(8,128)(2,1)S(1)}, bf16[512,128]{1,0:T(8,128)(2,1)S(1)}, u32[]{:S(2)}, u32[]{:S(2)}) collective-permute-start(bf16[512,128]{1,0:T(8,128)(2,1)S(1)} %collective-permute-done.3.refs_1_), channel_id=1, source_target_pairs={{0,1},{1,0},{2,3},{3,2},{4,5},{5,4},{6,7},{7,6},{8,9},{9,8},{10,11... | collective-permute-start | bytes 393224 | tf_op jit(solution)/shard_map/ppermute | solution.py:428
  99.2 1.5 %collective-permute-start.7 = (bf16[512,128]{1,0:T(8,128)(2,1)S(1)}, bf16[512,128]{1,0:T(8,128)(2,1)S(1)}, u32[]{:S(2)}, u32[]{:S(2)}) collective-permute-start(bf16[512,128]{1,0:T(8,128)(2,1)S(1)} %collective-permute-done.4.refs_0_), channel_id=1, source_target_pairs={{0,1},{1,0},{2,3},{3,2},{4,5},{5,4},{6,7},{7,6},{8,9},{9,8},{10,11... | collective-permute-start | bytes 393224 | tf_op jit(solution)/shard_map/ppermute | solution.py:428
  99.7 1.3 %collective-permute-start.6 = (bf16[512,128]{1,0:T(8,128)(2,1)S(1)}, bf16[512,128]{1,0:T(8,128)(2,1)S(1)}, u32[]{:S(2)}, u32[]{:S(2)}) collective-permute-start(bf16[512,128]{1,0:T(8,128)(2,1)S(1)} %order_column.1.refs_0_), channel_id=1, source_target_pairs={{0,1},{1,0},{2,3},{3,2},{4,5},{5,4},{6,7},{7,6},{8,9},{9,8},{10,11... | collective-permute-start | bytes 393224 | tf_op jit(solution)/shard_map/ppermute | solution.py:428
